TPU v7x, 128 devices: a whole 4x4x4 slice. The times are simulated.
128 devices in a mesh: node: 32 (over z, y, core), local: 4 (over x).
Axes of the slice: x: 4, y: 4, z: 4, core: 2. Of those that a mesh axis runs over, the one named last changes fastest.
Arguments:
- tokens: bfloat16 [4096, 4096], P(('node', 'local')), may hold values from -6 to 6
- out_grad: bfloat16 [4096, 4096], P(('node', 'local')), may hold values from -6 to 6
- node_lists: int32 [4096, 4], P(('node', 'local')), may hold values from 0 to 31, as said below
- expert_local: int32 [4096, 8], P(('node', 'local')), may hold values from 0 to 15, as said below
- gate_fixed: int32 [4096, 8], P(('node', 'local')), may hold values from 4096 to 65535
- gate_weight: bfloat16 [128, 4096, 768], P(('node', 'local')), may hold values from -0.09375 to 0.09375
- up_weight: bfloat16 [128, 4096, 768], P(('node', 'local')), may hold values from -0.09375 to 0.09375
- down_weight: bfloat16 [128, 768, 4096], P(('node', 'local')), may hold values from -0.21875 to 0.21875
Outputs:
- token_grad: bfloat16 [4096, 4096], P(('node', 'local'))
- down_grad: bfloat16 [128, 768, 4096], P(('node', 'local'))
Inputs may be any that keep to these rules, and one draw needn't show every extreme that they name: `node_lists`: each row holds 4 different group numbers. `expert_local`: each row holds 8 different numbers.
All inputs are finite; a program needn't handle non-finite values.
Results may differ from a plain program's by a relative error of at most 0.0064.
Values may be sent and summed in bfloat16 or wider, within the bound.
A program may use at most 128 MiB of HBM per device.

v0:
```python
import jax
import jax.numpy as jnp
from jax import lax
from jax.sharding import PartitionSpec as P


def expert_math(x_rows, dy_rows, w_gate_e, w_up_e, w_down_e):
    gate_act = jnp.dot(x_rows, w_gate_e, preferred_element_type=jnp.float32)
    up_act = jnp.dot(x_rows, w_up_e, preferred_element_type=jnp.float32)
    sig = jax.nn.sigmoid(gate_act)
    hidden = (gate_act * sig * up_act).astype(jnp.bfloat16)
    contract_rows = (((0,), (0,)), ((), ()))
    contract_last = (((1,), (1,)), ((), ()))
    down_local = lax.dot_general(
        hidden, dy_rows, contract_rows, preferred_element_type=jnp.float32
    ).astype(jnp.bfloat16)
    hidden_grad = lax.dot_general(
        dy_rows, w_down_e, contract_last, preferred_element_type=jnp.float32
    )
    gate_grad = (hidden_grad * up_act * sig * (1.0 + gate_act * (1.0 - sig))).astype(jnp.bfloat16)
    up_grad = (hidden_grad * gate_act * sig).astype(jnp.bfloat16)
    row_grad = (
        lax.dot_general(gate_grad, w_gate_e, contract_last, preferred_element_type=jnp.float32)
        + lax.dot_general(up_grad, w_up_e, contract_last, preferred_element_type=jnp.float32)
    ).astype(jnp.bfloat16)
    return (down_local, row_grad)


def body(
    tokens, out_grad, node_lists, expert_local, gate_fixed, gate_weight, up_weight, down_weight
):
    nodes = lax.axis_size("node")
    per_node = lax.axis_size("local")
    experts = nodes * per_node
    tok_dev, top_count = expert_local.shape
    width = tokens.shape[1]
    capacity = tok_dev * top_count // experts
    node_pick = jnp.take_along_axis(node_lists, expert_local // per_node, axis=1)
    expert_ids = (node_pick * per_node + expert_local % per_node).reshape(-1)
    onehot = (expert_ids[:, None] == jnp.arange(experts, dtype=jnp.int32)[None, :]).astype(
        jnp.int32
    )
    running = jnp.cumsum(onehot, axis=0)
    slot = jnp.sum(onehot * running, axis=1) - 1
    kept = slot < capacity
    position = jnp.where(kept, expert_ids * capacity + slot, experts * capacity)
    w_gate_e = gate_weight[0]
    w_up_e = up_weight[0]
    w_down_e = down_weight[0]
    gate_flat = gate_fixed.reshape(-1)
    table = jnp.full((experts * capacity,), -1, jnp.int32)
    table = table.at[position].set(jnp.arange(tok_dev * top_count, dtype=jnp.int32), mode="drop")
    valid = table >= 0
    safe = jnp.maximum(table, 0)
    rows = safe // top_count
    send_x = jnp.where(valid[:, None], tokens[rows], jnp.zeros((), jnp.bfloat16)).reshape(
        experts, capacity, width
    )
    gate_val = gate_flat[safe].astype(jnp.float32) * (1.0 / 65536.0)
    send_dy = jnp.where(valid[:, None], gate_val[:, None] * out_grad[rows].astype(jnp.float32), 0.0)
    send_dy = send_dy.astype(jnp.bfloat16).reshape(experts, capacity, width)
    recv_x, recv_dy = (
        lax.all_to_all(send_x, ("node", "local"), split_axis=0, concat_axis=0, tiled=True),
        lax.all_to_all(send_dy, ("node", "local"), split_axis=0, concat_axis=0, tiled=True),
    )
    x_rows = recv_x.reshape(experts * capacity, width)
    dy_rows = recv_dy.reshape(experts * capacity, width)
    down_local, row_grad = expert_math(x_rows, dy_rows, w_gate_e, w_up_e, w_down_e)
    returned = lax.all_to_all(
        row_grad.reshape(experts, capacity, width),
        ("node", "local"),
        split_axis=0,
        concat_axis=0,
        tiled=True,
    )
    returned = returned.reshape(experts * capacity, width)
    lookup = jnp.where(kept, position, 0)
    picked = jnp.where(kept[:, None], returned[lookup].astype(jnp.float32), 0.0)
    token_grad = jnp.sum(picked.reshape(tok_dev, top_count, width), axis=1).astype(jnp.bfloat16)
    return (token_grad, down_local[None])


def solution(mesh):
    return jax.shard_map(
        body,
        mesh=mesh,
        in_specs=(
            P(("node", "local"), None),
            P(("node", "local"), None),
            P(("node", "local"), None),
            P(("node", "local"), None),
            P(("node", "local"), None),
            P(("node", "local"), None, None),
            P(("node", "local"), None, None),
            P(("node", "local"), None, None),
        ),
        out_specs=(P(("node", "local"), None), P(("node", "local"), None, None)),
        check_vma=False,
    )
```

profile of v0, /device:TPU:1, one launch (start us, length us, event | category | flops | bytes accessed | tf_op | source)
XLA Modules:
  0.0 159.3 jit_solution(8351006543683448232)
XLA Ops:
  0.6 0.0 copy-start
  0.6 0.0 copy-start.1
  0.7 0.8 copy.10
  1.5 0.1 reshape.191
  1.6 0.0 copy-done.1
  1.6 2.4 %gather_fusion.4 = s32[256]{0:T(256)S(1)} fusion(s32[32,4]{0,1:T(4,128)S(1)} %copy-done.1, s32[256]{0:T(256)S(1)} %reshape.191), kind=kCustom, calls=%fused_computation.4 | custom fusion | bytes 4096 | tf_op jit(solution)/shard_map/jit(take_along_axis)/gather | solution.py:38
  4.0 0.1 reshape.194
  4.1 0.1 eq.31
  4.2 0.1 eq.27
  4.3 0.1 copy.14
  4.4 0.2 fusion.21
  4.7 0.2 fusion.22
  4.9 0.1 mul.73
  5.0 1.4 scatter_custom_fusion
  6.5 0.0 copy-done
  6.5 1.8 %gather_fusion.2 = bf16[256,4096]{1,0:T(8,128)(2,1)S(1)} fusion(bf16[32,4096]{1,0:T(8,128)(2,1)S(1)} %copy-done, s32[1024]{0:T(1024)S(1)} %get-tuple-element.8), kind=kCustom, calls=%fused_computation.2 | custom fusion | bytes 4195328 | tf_op jit(solution)/shard_map/gather | solution.py:56
  8.3 2.6 %gather.22 = bf16[128,2,4096]{2,1,0:T(2,128)(2,1)} reshape(bf16[256,4096]{1,0:T(8,128)(2,1)S(1)} %gather_fusion.2) | data formatting | bytes 4194304 | tf_op jit(solution)/shard_map/gather | solution.py:56
  11.0 0.2 broadcast_in_dim.62
  11.1 4.8 %broadcast_select_fusion = bf16[128,2,4096]{2,1,0:T(2,128)(2,1)} fusion(bf16[128,2,4096]{2,1,0:T(2,128)(2,1)} %gather.22, pred[128,2]{1,0:T(8,128)(4,1)S(1)} %broadcast_in_dim.62), kind=kLoop, calls=%fused_computation.23 | loop fusion | flops 1048576 | bytes 4194560 | tf_op jit(solution)/shard_map/jit(_where)/select_n | solution.py:56
  15.9 0.0 copy-start.2
  15.9 12.0 %all-to-all-start.1 = ((bf16[128,2,4096]{2,1,0:T(2,128)(2,1)}), bf16[128,2,4096]{2,1,0:T(2,128)(2,1)}, u32[]{:S(2)}, u32[]{:S(2)}) async-start(bf16[128,2,4096]{2,1,0:T(2,128)(2,1)} %broadcast_select_fusion), calls=%async_computation.1 | async-start | bytes 4194304 | tf_op jit(solution)/shard_map/all_to_all | solution.py:63
  27.9 0.0 copy-done.2
  27.9 1.8 %gather_fusion.1 = bf16[256,4096]{1,0:T(8,128)(2,1)S(1)} fusion(bf16[32,4096]{1,0:T(8,128)(2,1)S(1)} %copy-done.2, s32[1024]{0:T(1024)S(1)} %get-tuple-element.8), kind=kCustom, calls=%fused_computation.1 | custom fusion | bytes 4195328 | tf_op jit(solution)/shard_map/gather | solution.py:60
  29.8 0.0 copy-start.5
  29.8 3.9 %reshape.157 = f32[128,2,4096]{2,1,0:T(2,128)} reshape(bf16[256,4096]{1,0:T(8,128)(2,1)S(1)} %gather_fusion.1) | data formatting | bytes 6291456 | tf_op jit(solution)/shard_map/convert_element_type | solution.py:60
  33.7 0.0 copy-done.5
  33.7 0.1 copy.16
  33.8 0.1 reshape.152
  33.9 1.9 %gather_fusion = s32[256]{0:T(256)S(1)} fusion(s32[256]{0:T(256)S(1)} %reshape.152, s32[1024]{0:T(1024)S(1)} %get-tuple-element.9), kind=kCustom, calls=%fused_computation | custom fusion | bytes 3072 | tf_op jit(solution)/shard_map/gather | solution.py:59
  35.8 0.1 mul.76
  36.0 6.9 %select_convert_fusion = bf16[128,2,4096]{2,1,0:T(2,128)(2,1)} fusion(f32[128,2,4096]{2,1,0:T(2,128)} %reshape.157, pred[128,2]{1,0:T(8,128)(4,1)S(1)} %broadcast_in_dim.62, f32[128,2]{1,0:T(8,128)S(1)} %mul.76), kind=kLoop, calls=%fused_computation.22 | loop fusion | flops 3145728 | bytes 6292736 | tf_op jit(solution)/shard_map/convert_element_type | solution.py:61
  42.9 15.5 %all-to-all-done.1 = bf16[128,2,4096]{2,1,0:T(2,128)(2,1)} async-done(((bf16[128,2,4096]{2,1,0:T(2,128)(2,1)}), bf16[128,2,4096]{2,1,0:T(2,128)(2,1)}, u32[]{:S(2)}, u32[]{:S(2)}) %all-to-all-start.1) | async-done | bytes 2097184 | tf_op jit(solution)/shard_map/all_to_all | solution.py:63
  58.4 4.9 %all-to-all-start = ((bf16[128,2,4096]{2,1,0:T(2,128)(2,1)}), bf16[128,2,4096]{2,1,0:T(2,128)(2,1)}, u32[]{:S(2)}, u32[]{:S(2)}) async-start(bf16[128,2,4096]{2,1,0:T(2,128)(2,1)} %select_convert_fusion), calls=%async_computation | async-start | bytes 4194304 | tf_op jit(solution)/shard_map/all_to_all | solution.py:64
  63.3 0.0 slice-start
  63.3 4.2 %reshape.154 = bf16[256,4096]{1,0:T(8,128)(2,1)} reshape(bf16[128,2,4096]{2,1,0:T(2,128)(2,1)} %all-to-all-done.1) | data formatting | bytes 4194304 | tf_op jit(solution)/shard_map/reshape | solution.py:66
  67.6 0.0 slice-start.1
  67.6 0.0 copy-start.4
  67.6 5.3 %fusion.2 = f32[256,768]{1,0:T(8,128)S(1)} fusion(bf16[256,4096]{1,0:T(8,128)(2,1)} %reshape.154, bf16[1,4096,768]{2,1,0:T(8,128)(2,1)} %param.13), kind=kOutput, calls=%fused_computation.9 | convolution fusion | flops 1610612736 | bytes 9175040 | tf_op jit(solution)/shard_map/dot_general | solution.py:8
  72.9 0.0 slice-done
  73.0 0.0 slice-done.1
  73.0 0.0 copy-done.4
  73.0 2.7 %fusion.6 = f32[256,768]{1,0:T(8,128)} fusion(bf16[256,4096]{1,0:T(8,128)(2,1)S(1)} %copy-done.4, bf16[1,4096,768]{2,1,0:T(8,128)(2,1)S(1)} %bitcast.45), kind=kOutput, calls=%fused_computation.13 | convolution fusion | flops 1610612736 | bytes 9175040 | tf_op jit(solution)/shard_map/dot_general | solution.py:9
  75.7 18.2 %all-to-all-done = bf16[128,2,4096]{2,1,0:T(2,128)(2,1)} async-done(((bf16[128,2,4096]{2,1,0:T(2,128)(2,1)}), bf16[128,2,4096]{2,1,0:T(2,128)(2,1)}, u32[]{:S(2)}, u32[]{:S(2)}) %all-to-all-start) | async-done | bytes 2097184 | tf_op jit(solution)/shard_map/all_to_all | solution.py:64
  93.9 2.7 %reshape.153 = bf16[256,4096]{1,0:T(8,128)(2,1)S(1)} reshape(bf16[128,2,4096]{2,1,0:T(2,128)(2,1)} %all-to-all-done) | data formatting | bytes 4194304 | tf_op jit(solution)/shard_map/reshape | solution.py:67
  96.7 0.0 copy-start.3
  96.7 0.0 slice-start.2
  96.7 4.8 %fusion.8 = f32[256,768]{1,0:T(8,128)S(1)} fusion(bf16[256,4096]{1,0:T(8,128)(2,1)S(1)} %reshape.153, bf16[1,768,4096]{2,1,0:T(8,128)(2,1)} %param.15), kind=kOutput, calls=%fused_computation.15 | convolution fusion | flops 1610612736 | bytes 9175040 | tf_op jit(solution)/shard_map/dot_general | solution.py:17
  101.5 0.0 copy-done.3
  101.5 0.0 slice-start.3
  101.5 4.9 %fusion = f32[256,4096]{1,0:T(8,128)S(1)} fusion(bf16[1,4096,768]{2,1,0:T(8,128)(2,1)} %param.13, f32[256,768]{1,0:T(8,128)S(1)} %fusion.2, f32[256,768]{1,0:T(8,128)S(1)} %fusion.8, f32[256,768]{1,0:T(8,128)S(1)} %copy-done.3), kind=kOutput, calls=%fused_computation.7 | convolution fusion | flops 1612578816 | bytes 12845056 | tf_op jit(solution)/shard_map/dot_general | solution.py:23
  106.3 0.0 slice-done.2
  106.4 0.0 slice-done.3
  106.4 3.2 %fusion.14 = bf16[256,4096]{1,0:T(8,128)(2,1)} fusion(f32[256,4096]{1,0:T(8,128)S(1)} %fusion, bf16[1,4096,768]{2,1,0:T(8,128)(2,1)S(1)} %bitcast.47, f32[256,768]{1,0:T(8,128)S(1)} %fusion.8, f32[256,768]{1,0:T(8,128)S(1)} %fusion.2), kind=kOutput, calls=%fused_computation.19 | convolution fusion | flops 1613889536 | bytes 14155776 | tf_op jit(solution)/shard_map/dot_general | solution.py:24
  109.5 4.4 %reshape.155 = bf16[128,2,4096]{2,1,0:T(2,128)(2,1)} reshape(bf16[256,4096]{1,0:T(8,128)(2,1)} %fusion.14) | data formatting | bytes 4194304 | tf_op jit(solution)/shard_map/reshape | solution.py:70
  113.9 5.0 %all-to-all-start.2 = ((bf16[128,2,4096]{2,1,0:T(2,128)(2,1)}), bf16[128,2,4096]{2,1,0:T(2,128)(2,1)}, u32[]{:S(2)}, u32[]{:S(2)}) async-start(bf16[128,2,4096]{2,1,0:T(2,128)(2,1)} %reshape.155), calls=%async_computation.2 | async-start | bytes 4194304 | tf_op jit(solution)/shard_map/all_to_all | solution.py:69
  118.9 0.1 lt.62
  119.0 5.7 %fusion.10 = bf16[1,768,4096]{2,1,0:T(8,128)(2,1)} fusion(bf16[256,4096]{1,0:T(8,128)(2,1)S(1)} %reshape.153, f32[256,768]{1,0:T(8,128)} %fusion.6, f32[256,768]{1,0:T(8,128)S(1)} %fusion.2), kind=kOutput, calls=%fused_computation.17 | convolution fusion | flops 1614938112 | bytes 9961472 | tf_op jit(solution)/shard_map/dot_general | solution.py:14
  124.7 24.7 %all-to-all-done.2 = bf16[128,2,4096]{2,1,0:T(2,128)(2,1)} async-done(((bf16[128,2,4096]{2,1,0:T(2,128)(2,1)}), bf16[128,2,4096]{2,1,0:T(2,128)(2,1)}, u32[]{:S(2)}, u32[]{:S(2)}) %all-to-all-start.2) | async-done | bytes 2097184 | tf_op jit(solution)/shard_map/all_to_all | solution.py:69
  149.4 2.7 %reshape.156 = bf16[256,4096]{1,0:T(8,128)(2,1)S(1)} reshape(bf16[128,2,4096]{2,1,0:T(2,128)(2,1)} %all-to-all-done.2) | data formatting | bytes 4194304 | tf_op jit(solution)/shard_map/reshape | solution.py:76
  152.2 3.2 %gather_fusion.3 = bf16[256,4096]{1,0:T(8,128)(2,1)} fusion(bf16[256,4096]{1,0:T(8,128)(2,1)S(1)} %reshape.156, s32[1024]{0:T(1024)S(1)} %pad_clamp_fusion), kind=kCustom, calls=%fused_computation.3 | custom fusion | bytes 4195328 | tf_op jit(solution)/shard_map/gather | solution.py:78
  155.4 3.9 %fusion.17 = bf16[32,4096]{1,0:T(8,128)(2,1)} fusion(bf16[256,4096]{1,0:T(8,128)(2,1)} %gather_fusion.3, pred[32,8]{1,0:T(8,128)(4,1)S(1)} %lt.62), kind=kLoop, calls=%fused_computation.21 | loop fusion | flops 3014656 | bytes 2359552 | tf_op jit(solution)/shard_map/reduce_sum | solution.py:79
  (19 shorter events, 0.2 us)
Async XLA Ops:
  0.6 5.9 %copy-start = (bf16[32,4096]{1,0:T(8,128)(2,1)S(1)}, bf16[32,4096]{1,0:T(8,128)(2,1)}, u32[]{:S(2)}) copy-start(bf16[32,4096]{1,0:T(8,128)(2,1)} %param.8) | copy-start | bytes 786436
  0.6 0.9 copy-start.1
  15.9 12.0 %copy-start.2 = (bf16[32,4096]{1,0:T(8,128)(2,1)S(1)}, bf16[32,4096]{1,0:T(8,128)(2,1)}, u32[]{:S(2)}) copy-start(bf16[32,4096]{1,0:T(8,128)(2,1)} %param.9) | copy-start | bytes 786436
  15.9 42.4 %all-to-all-start.1 = ((bf16[128,2,4096]{2,1,0:T(2,128)(2,1)}), bf16[128,2,4096]{2,1,0:T(2,128)(2,1)}, u32[]{:S(2)}, u32[]{:S(2)}) async-start(bf16[128,2,4096]{2,1,0:T(2,128)(2,1)} %broadcast_select_fusion), calls=%async_computation.1 | async-start | bytes 4194304 | tf_op jit(solution)/shard_map/all_to_all | solution.py:63
  29.8 3.9 %copy-start.5 = (s32[32,8]{0,1:T(8,128)S(1)}, s32[32,8]{0,1:T(8,128)}, u32[]{:S(2)}) copy-start(s32[32,8]{0,1:T(8,128)} %param.12) | copy-start | bytes 3076
  58.4 35.5 %all-to-all-start = ((bf16[128,2,4096]{2,1,0:T(2,128)(2,1)}), bf16[128,2,4096]{2,1,0:T(2,128)(2,1)}, u32[]{:S(2)}, u32[]{:S(2)}) async-start(bf16[128,2,4096]{2,1,0:T(2,128)(2,1)} %select_convert_fusion), calls=%async_computation | async-start | bytes 4194304 | tf_op jit(solution)/shard_map/all_to_all | solution.py:64
  63.3 9.6 %slice-start = ((s8[6291456]{0:T(1024)(128)(4,1)}), s8[2097152]{0:T(1024)(128)(4,1)S(1)}, s32[]{:S(2)}) async-start(s8[6291456]{0:T(1024)(128)(4,1)} %bitcast.44), calls=%async_computation.3 | async-start | bytes 4194304
  67.6 5.4 %slice-start.1 = ((s8[6291456]{0:T(1024)(128)(4,1)}), s8[4194304]{0:T(1024)(128)(4,1)S(1)}, s32[]{:S(2)}) async-start(s8[6291456]{0:T(1024)(128)(4,1)} %bitcast.44), calls=%async_computation.4 | async-start | bytes 8388608
  67.6 5.4 %copy-start.4 = (bf16[256,4096]{1,0:T(8,128)(2,1)S(1)}, bf16[256,4096]{1,0:T(8,128)(2,1)}, u32[]{:S(2)}) copy-start(bf16[256,4096]{1,0:T(8,128)(2,1)} %reshape.154) | copy-start | bytes 6291460
  96.7 4.8 %copy-start.3 = (f32[256,768]{1,0:T(8,128)S(1)}, f32[256,768]{1,0:T(8,128)}, u32[]{:S(2)}) copy-start(f32[256,768]{1,0:T(8,128)} %fusion.6) | copy-start | bytes 2359300
  96.7 9.7 %slice-start.2 = ((s8[6291456]{0:T(1024)(128)(4,1)}), s8[4194304]{0:T(1024)(128)(4,1)S(1)}, s32[]{:S(2)}) async-start(s8[6291456]{0:T(1024)(128)(4,1)} %bitcast.46), calls=%async_computation.5 | async-start | bytes 8388608
  101.5 4.9 %slice-start.3 = ((s8[6291456]{0:T(1024)(128)(4,1)}), s8[2097152]{0:T(1024)(128)(4,1)S(1)}, s32[]{:S(2)}) async-start(s8[6291456]{0:T(1024)(128)(4,1)} %bitcast.46), calls=%async_computation.6 | async-start | bytes 4194304
  113.9 35.5 %all-to-all-start.2 = ((bf16[128,2,4096]{2,1,0:T(2,128)(2,1)}), bf16[128,2,4096]{2,1,0:T(2,128)(2,1)}, u32[]{:S(2)}, u32[]{:S(2)}) async-start(bf16[128,2,4096]{2,1,0:T(2,128)(2,1)} %reshape.155), calls=%async_computation.2 | async-start | bytes 4194304 | tf_op jit(solution)/shard_map/all_to_all | solution.py:69
where the time goes:
time: 160 us; the launch traced here: 159 us
  waiting for transfers between devices  58.4 us (36%)
  local copies, waits for them, and re-layouts  35.3 us (22%)
  matrix products  26.6 us (17%)
  starting transfers between devices  21.9 us (14%)
  other arithmetic  16.2 us (10%)
    all_to_all x1, waiting for transfers between devices, body(): lax.all_to_all(row_grad.reshape(experts, capacity, width), ('node', 'loca...  24.7 us
    all_to_all x1, waiting for transfers between devices, body(): lax.all_to_all(send_dy, ('node', 'local'), split_axis=0, concat_axis=0, t...  18.2 us
    all_to_all x1, waiting for transfers between devices, body(): lax.all_to_all(send_x, ('node', 'local'), split_axis=0, concat_axis=0, ti...  15.5 us
    all_to_all x1, starting transfers between devices, body(): lax.all_to_all(send_x, ('node', 'local'), split_axis=0, concat_axis=0, ti...  12 us
    convert_element_type x1, other arithmetic, body(): send_dy = send_dy.astype(jnp.bfloat16).reshape(experts, capacity, width)  6.94 us
    dot_general x1, matrix products, expert_math(): lax.dot_general(hidden, dy_rows, contract_rows, preferred_element_type=jn...  5.71 us
    dot_general x1, matrix products, expert_math(): gate_act = jnp.dot(x_rows, w_gate_e, preferred_element_type=jnp.float32)  5.34 us
    all_to_all x1, starting transfers between devices, body(): lax.all_to_all(row_grad.reshape(experts, capacity, width), ('node', 'loca...  4.97 us
  transfers between devices with their start and end apart: 3, of which 3 were waited for; matrix products, arithmetic and copies ran while one was open for 21% of the time, Pallas kernels for 0%

commit v1 on v0

--- a/solution.py
+++ b/solution.py
@@ -1,7 +1,78 @@
+import functools
 import jax
 import jax.numpy as jnp
 from jax import lax
 from jax.sharding import PartitionSpec as P
+from jax.experimental import pallas as pl
+from jax.experimental.pallas import tpu as pltpu
+
+
+def _exchange_kernel(n_local, *refs):
+    count = (len(refs) - 2) // 2
+    srcs = refs[:count]
+    dsts = refs[count:2 * count]
+    send_sems = refs[2 * count]
+    recv_sems = refs[2 * count + 1]
+    node = lax.axis_index("node")
+    local = lax.axis_index("local")
+    me = node * n_local + local
+    devices = lax.axis_size("node") * n_local
+    rows = srcs[0].shape[0] // devices
+
+    def copy_to(p, i):
+        return pltpu.make_async_remote_copy(
+            src_ref=srcs[i].at[pl.ds(p * rows, rows)],
+            dst_ref=dsts[i].at[pl.ds(me * rows, rows)],
+            send_sem=send_sems.at[i],
+            recv_sem=recv_sems.at[i],
+            device_id=(p // n_local, p % n_local),
+            device_id_type=pl.DeviceIdType.MESH,
+        )
+
+    def local_copy(i):
+        return pltpu.make_async_copy(
+            srcs[i].at[pl.ds(me * rows, rows)],
+            dsts[i].at[pl.ds(me * rows, rows)],
+            recv_sems.at[i],
+        )
+
+    for i in range(count):
+        local_copy(i).start()
+
+    def start_body(step, carry):
+        p = lax.rem(me + step, devices)
+        for i in range(count):
+            copy_to(p, i).start()
+        return carry
+
+    lax.fori_loop(1, devices, start_body, 0)
+    nxt = lax.rem(me + 1, devices)
+    for i in range(count):
+        pltpu.make_async_copy(dsts[i], dsts[i], recv_sems.at[i]).wait()
+        pltpu.make_async_remote_copy(
+            src_ref=srcs[i].at[pl.ds(0, (devices - 1) * rows)],
+            dst_ref=dsts[i].at[pl.ds(0, (devices - 1) * rows)],
+            send_sem=send_sems.at[i],
+            recv_sem=recv_sems.at[i],
+            device_id=(nxt // n_local, nxt % n_local),
+            device_id_type=pl.DeviceIdType.MESH,
+        ).wait_send()
+
+
+def exchange(*arrays):
+    n_local = lax.axis_size("local")
+    count = len(arrays)
+    return pl.pallas_call(
+        functools.partial(_exchange_kernel, n_local),
+        out_shape=[jax.ShapeDtypeStruct(a.shape, a.dtype) for a in arrays],
+        in_specs=[pl.BlockSpec(memory_space=pl.ANY)] * count,
+        out_specs=[pl.BlockSpec(memory_space=pl.ANY)] * count,
+        scratch_shapes=[
+            pltpu.SemaphoreType.DMA((count,)),
+            pltpu.SemaphoreType.DMA((count,)),
+        ],
+        compiler_params=pltpu.CompilerParams(has_side_effects=True),
+    )(*arrays)
 
 
 def expert_math(x_rows, dy_rows, w_gate_e, w_up_e, w_down_e):
@@ -53,26 +124,17 @@
     valid = table >= 0
     safe = jnp.maximum(table, 0)
     rows = safe // top_count
-    send_x = jnp.where(valid[:, None], tokens[rows], jnp.zeros((), jnp.bfloat16)).reshape(
-        experts, capacity, width
-    )
+    send_x = jnp.where(valid[:, None], tokens[rows], jnp.zeros((), jnp.bfloat16))
     gate_val = gate_flat[safe].astype(jnp.float32) * (1.0 / 65536.0)
     send_dy = jnp.where(valid[:, None], gate_val[:, None] * out_grad[rows].astype(jnp.float32), 0.0)
-    send_dy = send_dy.astype(jnp.bfloat16).reshape(experts, capacity, width)
-    recv_x, recv_dy = (
-        lax.all_to_all(send_x, ("node", "local"), split_axis=0, concat_axis=0, tiled=True),
-        lax.all_to_all(send_dy, ("node", "local"), split_axis=0, concat_axis=0, tiled=True),
-    )
-    x_rows = recv_x.reshape(experts * capacity, width)
-    dy_rows = recv_dy.reshape(experts * capacity, width)
+    send_dy = send_dy.astype(jnp.bfloat16)
+    tile_rows = 8
+    flat = (experts * tile_rows, capacity * width // tile_rows)
+    x_rows, dy_rows = exchange(send_x.reshape(flat), send_dy.reshape(flat))
+    x_rows = x_rows.reshape(experts * capacity, width)
+    dy_rows = dy_rows.reshape(experts * capacity, width)
     down_local, row_grad = expert_math(x_rows, dy_rows, w_gate_e, w_up_e, w_down_e)
-    returned = lax.all_to_all(
-        row_grad.reshape(experts, capacity, width),
-        ("node", "local"),
-        split_axis=0,
-        concat_axis=0,
-        tiled=True,
-    )
+    (returned,) = exchange(row_grad.reshape(flat))
     returned = returned.reshape(experts * capacity, width)
     lookup = jnp.where(kept, position, 0)
     picked = jnp.where(kept[:, None], returned[lookup].astype(jnp.float32), 0.0)

time: 160 us -> 190 us (1.19)
  Pallas kernels: 0 us -> 119 us
  waiting for transfers between devices: 58.4 us -> 0 us
  starting transfers between devices: 21.9 us -> 0 us
  other arithmetic: 16.2 us -> 11.7 us
  local copies, waits for them, and re-layouts: 35.3 us -> 32.9 us
    pallas_call x0 -> x2, Pallas kernels: none -> 119 us  [exchange(): pl.pallas_call(functools.partial(_exchange_kernel, n_local), out_shape=[j...]
    all_to_all x3 -> x0, waiting for transfers between devices: 58.4 us -> none  [the longest x1 24.7 us: body(): lax.all_to_all(row_grad.reshape(experts, capacity, width), ('node', 'loca...]
    all_to_all x3 -> x0, starting transfers between devices: 21.9 us -> none  [the longest x1 12 us: body(): lax.all_to_all(send_x, ('node', 'local'), split_axis=0, concat_axis=0, ti...]
    convert_element_type x1, other arithmetic: 6.94 us -> 3.92 us  [body(): send_dy = send_dy.astype(jnp.bfloat16)]
    dot_general x1, matrix products: 4.86 us -> 1.92 us  [expert_math(): lax.dot_general(gate_grad, w_gate_e, contract_last, preferred_element_typ...]
    reshape x3, local copies, waits for them, and re-layouts: 11.4 us -> 8.77 us  [the longest x1 3.1 us: body(): x_rows = x_rows.reshape(experts * capacity, width)]
    dot_general x1, matrix products: 2.72 us -> 4.77 us  [expert_math(): up_act = jnp.dot(x_rows, w_up_e, preferred_element_type=jnp.float32)]
  transfers between devices with their start and end apart: 3 -> 0, of which waited for: 3 -> 0; matrix products, arithmetic and copies ran while one was open for 21% -> 0% of each run, Pallas kernels for 0% -> 0%
where the time goes in v1:
time: 190 us
  Pallas kernels  119 us (63%)
  local copies, waits for them, and re-layouts  32.9 us (17%)
  matrix products  25 us (13%)
  other arithmetic  11.7 us (6%)
    pallas_call x2, Pallas kernels, exchange(): pl.pallas_call(functools.partial(_exchange_kernel, n_local), out_shape=[j...  119 us
    dot_general x1, matrix products, expert_math(): lax.dot_general(hidden, dy_rows, contract_rows, preferred_element_type=jn...  5.71 us
    dot_general x1, matrix products, expert_math(): lax.dot_general(dy_rows, w_down_e, contract_last, preferred_element_type=...  5.39 us
    dot_general x1, matrix products, expert_math(): gate_act = jnp.dot(x_rows, w_gate_e, preferred_element_type=jnp.float32)  5.33 us
    dot_general x1, matrix products, expert_math(): up_act = jnp.dot(x_rows, w_up_e, preferred_element_type=jnp.float32)  4.77 us
    gather x2, local copies, waits for them, and re-layouts, body(): tokens[rows]  4.41 us
    reduce_sum x1, other arithmetic, body(): jnp.sum(picked.reshape(tok_dev, top_count, width), axis=1)  4.05 us
    convert_element_type x1, other arithmetic, body(): send_dy = send_dy.astype(jnp.bfloat16)  3.92 us

profile of v1, /device:TPU:1, one launch (start us, length us, event | category | flops | bytes accessed | tf_op | source)
XLA Modules:
  0.0 190.0 jit_solution(6234631099973368043)
XLA Ops:
  0.6 0.0 copy-start
  0.6 0.0 copy-start.1
  0.7 0.8 copy.10
  1.5 0.1 reshape.176
  1.6 0.0 copy-done.1
  1.6 2.4 %gather_fusion.4 = s32[256]{0:T(256)S(1)} fusion(s32[32,4]{0,1:T(4,128)S(1)} %copy-done.1, s32[256]{0:T(256)S(1)} %reshape.176), kind=kCustom, calls=%fused_computation.4 | custom fusion | bytes 4096 | tf_op jit(solution)/shard_map/jit(take_along_axis)/gather | solution.py:109
  4.0 0.1 reshape.179
  4.1 0.1 eq.31
  4.2 0.1 copy.14
  4.3 0.2 fusion.21
  4.6 0.1 eq.27
  4.7 0.2 fusion.22
  4.9 0.1 mul.74
  5.0 1.4 scatter_custom_fusion
  6.5 0.0 copy-done
  6.5 1.8 gather_fusion
  8.3 2.6 %gather.20 = bf16[1024,1024]{1,0:T(8,128)(2,1)} reshape(bf16[256,4096]{1,0:T(8,128)(2,1)S(1)} %gather_fusion) | data formatting | bytes 4194304 | tf_op jit(solution)/shard_map/gather | solution.py:127
  10.9 0.1 broadcast_in_dim.64
  11.0 0.1 broadcast_in_dim.65
  11.1 0.0 copy-start.2
  11.2 3.2 %broadcast_select_fusion.refs_0_ = bf16[1024,1024]{1,0:T(8,128)(2,1)} fusion(bf16[1024,1024]{1,0:T(8,128)(2,1)} %gather.20, pred[1024]{0:T(1024)(128)(4,1)S(1)} %broadcast_in_dim.65), kind=kLoop, calls=%fused_computation.23 | loop fusion | flops 1048576 | bytes 4195328 | tf_op jit(solution)/shard_map/jit(_where)/select_n | solution.py:127
  14.4 0.0 copy-done.2
  14.4 1.8 gather_fusion.2
  16.2 0.0 copy-start.8
  16.2 2.9 %reshape.142 = f32[1024,1024]{1,0:T(8,128)} reshape(bf16[256,4096]{1,0:T(8,128)(2,1)S(1)} %gather_fusion.2) | data formatting | bytes 6291456 | tf_op jit(solution)/shard_map/convert_element_type | solution.py:129
  19.1 0.0 copy-done.8
  19.1 0.1 copy.16
  19.2 0.1 reshape.137
  19.3 1.9 %gather_fusion.1 = s32[256]{0:T(256)S(1)} fusion(s32[256]{0:T(256)S(1)} %reshape.137, s32[1024]{0:T(1024)S(1)} %get-tuple-element.12), kind=kCustom, calls=%fused_computation.1 | custom fusion | bytes 3072 | tf_op jit(solution)/shard_map/gather | solution.py:128
  21.2 0.1 mul.77
  21.3 0.1 mul.78
  21.4 3.9 %select_convert_fusion.refs_1_ = bf16[1024,1024]{1,0:T(8,128)(2,1)} fusion(f32[1024,1024]{1,0:T(8,128)} %reshape.142, f32[1024]{0:T(1024)S(1)} %mul.78, pred[1024]{0:T(1024)(128)(4,1)S(1)} %broadcast_in_dim.65), kind=kLoop, calls=%fused_computation.22 | loop fusion | flops 3145728 | bytes 6296576 | tf_op jit(solution)/shard_map/convert_element_type | solution.py:130
  25.4 78.4 %shard_map.95 = (bf16[1024,1024]{1,0:T(8,128)(2,1)}, bf16[1024,1024]{1,0:T(8,128)(2,1)}) custom-call(bf16[1024,1024]{1,0:T(8,128)(2,1)} %broadcast_select_fusion.refs_0_, bf16[1024,1024]{1,0:T(8,128)(2,1)} %select_convert_fusion.refs_1_), custom_call_target="tpu_custom_call" | custom-call | tf_op jit(solution)/shard_map/pallas_call | solution.py:65
  103.8 3.1 %reshape.139 = bf16[256,4096]{1,0:T(8,128)(2,1)S(1)} reshape(bf16[1024,1024]{1,0:T(8,128)(2,1)} %get-tuple-element.5) | data formatting | bytes 4194304 | tf_op jit(solution)/shard_map/reshape | solution.py:134
  106.9 0.0 copy-start.6
  106.9 5.3 %fusion.2 = f32[256,768]{1,0:T(8,128)S(1)} fusion(bf16[256,4096]{1,0:T(8,128)(2,1)S(1)} %reshape.139, bf16[1,4096,768]{2,1,0:T(8,128)(2,1)} %param.13), kind=kOutput, calls=%fused_computation.9 | convolution fusion | flops 1610612736 | bytes 9175040 | tf_op jit(solution)/shard_map/dot_general | solution.py:79
  112.2 0.0 copy-done.6
  112.2 3.1 %reshape.138 = bf16[256,4096]{1,0:T(8,128)(2,1)S(1)} reshape(bf16[1024,1024]{1,0:T(8,128)(2,1)} %get-tuple-element.4) | data formatting | bytes 4194304 | tf_op jit(solution)/shard_map/reshape | solution.py:135
  115.3 0.0 copy-start.3
  115.4 0.0 copy-start.7
  115.4 0.0 slice-start.2
  115.4 0.0 slice-start
  115.4 5.4 %fusion.8 = f32[256,768]{1,0:T(8,128)S(1)} fusion(bf16[256,4096]{1,0:T(8,128)(2,1)S(1)} %reshape.138, bf16[1,768,4096]{2,1,0:T(8,128)(2,1)} %param.15), kind=kOutput, calls=%fused_computation.15 | convolution fusion | flops 1610612736 | bytes 9175040 | tf_op jit(solution)/shard_map/dot_general | solution.py:88
  120.8 0.0 copy-done.3
  120.8 0.0 copy-done.7
  120.8 0.0 slice-start.3
  120.8 0.0 slice-start.1
  120.8 4.8 %fusion.6 = f32[256,768]{1,0:T(8,128)S(1)} fusion(bf16[256,4096]{1,0:T(8,128)(2,1)S(1)} %copy-done.7, bf16[1,4096,768]{2,1,0:T(8,128)(2,1)} %param.14), kind=kOutput, calls=%fused_computation.13 | convolution fusion | flops 1610612736 | bytes 9175040 | tf_op jit(solution)/shard_map/dot_general | solution.py:80
  125.6 0.0 copy-start.5
  125.6 0.9 copy-done.5
  126.5 0.0 slice-done.2
  126.5 0.0 slice-done.3
  126.5 1.9 %fusion = f32[256,4096]{1,0:T(8,128)S(1)} fusion(bf16[1,4096,768]{2,1,0:T(8,128)(2,1)S(1)} %bitcast.47, f32[256,768]{1,0:T(8,128)S(1)} %fusion.2, f32[256,768]{1,0:T(8,128)S(1)} %fusion.8, f32[256,768]{1,0:T(8,128)S(1)} %fusion.6), kind=kOutput, calls=%fused_computation.7 | convolution fusion | flops 1612578816 | bytes 12845056 | tf_op jit(solution)/shard_map/dot_general | solution.py:94
  128.4 0.0 slice-done
  128.5 0.0 slice-done.1
  128.5 1.8 fusion.14
  130.3 2.6 %reshape.140.refs_0_ = bf16[1024,1024]{1,0:T(8,128)(2,1)} reshape(bf16[256,4096]{1,0:T(8,128)(2,1)S(1)} %fusion.14) | data formatting | bytes 4194304 | tf_op jit(solution)/shard_map/reshape | solution.py:137
  132.9 41.0 %shard_map.96 = bf16[1024,1024]{1,0:T(8,128)(2,1)} custom-call(bf16[1024,1024]{1,0:T(8,128)(2,1)} %reshape.140.refs_0_), custom_call_target="tpu_custom_call" | custom-call | tf_op jit(solution)/shard_map/pallas_call | solution.py:65
  173.8 3.1 %reshape.141 = bf16[256,4096]{1,0:T(8,128)(2,1)S(1)} reshape(bf16[1024,1024]{1,0:T(8,128)(2,1)} %shard_map.96) | data formatting | bytes 4194304 | tf_op jit(solution)/shard_map/reshape | solution.py:138
  177.0 3.2 %gather_fusion.3 = bf16[256,4096]{1,0:T(8,128)(2,1)} fusion(bf16[256,4096]{1,0:T(8,128)(2,1)S(1)} %reshape.141, s32[1024]{0:T(1024)S(1)} %pad_clamp_fusion), kind=kCustom, calls=%fused_computation.3 | custom fusion | bytes 4195328 | tf_op jit(solution)/shard_map/gather | solution.py:140
  180.2 0.1 lt.62
  180.2 4.1 %fusion.17 = bf16[32,4096]{1,0:T(8,128)(2,1)} fusion(bf16[256,4096]{1,0:T(8,128)(2,1)} %gather_fusion.3, pred[32,8]{1,0:T(8,128)(4,1)S(1)} %lt.62), kind=kLoop, calls=%fused_computation.21 | loop fusion | flops 3014656 | bytes 2359552 | tf_op jit(solution)/shard_map/reduce_sum | solution.py:141
  184.3 0.0 copy-done.4
  184.3 5.7 %fusion.10 = bf16[1,768,4096]{2,1,0:T(8,128)(2,1)} fusion(bf16[256,4096]{1,0:T(8,128)(2,1)S(1)} %copy-done.4, f32[256,768]{1,0:T(8,128)} %copy-done.5, f32[256,768]{1,0:T(8,128)S(1)} %fusion.2), kind=kOutput, calls=%fused_computation.17 | convolution fusion | flops 1614938112 | bytes 9961472 | tf_op jit(solution)/shard_map/dot_general | solution.py:85
  (20 shorter events, 0.2 us)
Async XLA Ops:
  0.6 5.8 %copy-start = (bf16[32,4096]{1,0:T(8,128)(2,1)S(1)}, bf16[32,4096]{1,0:T(8,128)(2,1)}, u32[]{:S(2)}) copy-start(bf16[32,4096]{1,0:T(8,128)(2,1)} %param.8) | copy-start | bytes 786436
  0.6 0.9 copy-start.1
  11.1 3.2 %copy-start.2 = (bf16[32,4096]{1,0:T(8,128)(2,1)S(1)}, bf16[32,4096]{1,0:T(8,128)(2,1)}, u32[]{:S(2)}) copy-start(bf16[32,4096]{1,0:T(8,128)(2,1)} %param.9) | copy-start | bytes 786436
  16.2 2.9 %copy-start.8 = (s32[32,8]{0,1:T(8,128)S(1)}, s32[32,8]{0,1:T(8,128)}, u32[]{:S(2)}) copy-start(s32[32,8]{0,1:T(8,128)} %param.12) | copy-start | bytes 3076
  106.9 5.3 %copy-start.6 = (bf16[256,4096]{1,0:T(8,128)(2,1)}, bf16[256,4096]{1,0:T(8,128)(2,1)S(1)}, u32[]{:S(2)}) copy-start(bf16[256,4096]{1,0:T(8,128)(2,1)S(1)} %reshape.139) | copy-start | bytes 6291460
  115.3 5.5 %copy-start.3 = (bf16[256,4096]{1,0:T(8,128)(2,1)}, bf16[256,4096]{1,0:T(8,128)(2,1)S(1)}, u32[]{:S(2)}) copy-start(bf16[256,4096]{1,0:T(8,128)(2,1)S(1)} %reshape.138) | copy-start | bytes 6291460
  115.4 5.5 %copy-start.7 = (bf16[256,4096]{1,0:T(8,128)(2,1)S(1)}, bf16[256,4096]{1,0:T(8,128)(2,1)}, u32[]{:S(2)}) copy-start(bf16[256,4096]{1,0:T(8,128)(2,1)} %copy-done.6) | copy-start | bytes 6291460
  115.4 11.1 %slice-start.2 = ((s8[6291456]{0:T(1024)(128)(4,1)}), s8[4194304]{0:T(1024)(128)(4,1)S(1)}, s32[]{:S(2)}) async-start(s8[6291456]{0:T(1024)(128)(4,1)} %bitcast.46), calls=%async_computation.2 | async-start | bytes 8388608
  115.4 13.1 %slice-start = ((s8[6291456]{0:T(1024)(128)(4,1)}), s8[4194304]{0:T(1024)(128)(4,1)S(1)}, s32[]{:S(2)}) async-start(s8[6291456]{0:T(1024)(128)(4,1)} %bitcast.44), calls=%async_computation | async-start | bytes 8388608
  120.8 5.7 %slice-start.3 = ((s8[6291456]{0:T(1024)(128)(4,1)}), s8[2097152]{0:T(1024)(128)(4,1)S(1)}, s32[]{:S(2)}) async-start(s8[6291456]{0:T(1024)(128)(4,1)} %bitcast.46), calls=%async_computation.3 | async-start | bytes 4194304
  120.8 7.6 %slice-start.1 = ((s8[6291456]{0:T(1024)(128)(4,1)}), s8[2097152]{0:T(1024)(128)(4,1)S(1)}, s32[]{:S(2)}) async-start(s8[6291456]{0:T(1024)(128)(4,1)} %bitcast.44), calls=%async_computation.1 | async-start | bytes 4194304
  125.6 0.9 copy-start.5
  180.1 4.2 %copy-start.4 = (bf16[256,4096]{1,0:T(8,128)(2,1)S(1)}, bf16[256,4096]{1,0:T(8,128)(2,1)}, u32[]{:S(2)}) copy-start(bf16[256,4096]{1,0:T(8,128)(2,1)} %copy-done.3) | copy-start | bytes 6291460

commit v2 on v1

--- a/solution.py
+++ b/solution.py
@@ -39,8 +39,18 @@
     for i in range(count):
         local_copy(i).start()
 
+    core = node % 2
+    y_pos = (node // 2) % 4
+    z_pos = node // 8
+
     def start_body(step, carry):
-        p = lax.rem(me + step, devices)
+        t = step % 64
+        d_core = step // 64
+        dx = t % 4
+        dy = (t // 4 + dx) % 4
+        dz = (t // 16 + t // 4 + dx) % 4
+        node_to = (((z_pos + dz) % 4) * 4 + (y_pos + dy) % 4) * 2 + (core + d_core) % 2
+        p = node_to * n_local + (local + dx) % 4
         for i in range(count):
             copy_to(p, i).start()
         return carry

time: 190 us -> 170 us (0.89)
  Pallas kernels: 119 us -> 98.5 us
    pallas_call x2, Pallas kernels: 119 us -> 98.5 us  [exchange(): pl.pallas_call(functools.partial(_exchange_kernel, n_local), out_shape=[j...]
where the time goes in v2:
time: 170 us; the launch traced here: 169 us
  Pallas kernels  98.5 us (58%)
  local copies, waits for them, and re-layouts  32.9 us (19%)
  matrix products  25 us (15%)
  other arithmetic  11.7 us (7%)
    pallas_call x2, Pallas kernels, exchange(): pl.pallas_call(functools.partial(_exchange_kernel, n_local), out_shape=[j...  98.5 us
    dot_general x1, matrix products, expert_math(): lax.dot_general(hidden, dy_rows, contract_rows, preferred_element_type=jn...  5.71 us
    dot_general x1, matrix products, expert_math(): lax.dot_general(dy_rows, w_down_e, contract_last, preferred_element_type=...  5.39 us
    dot_general x1, matrix products, expert_math(): gate_act = jnp.dot(x_rows, w_gate_e, preferred_element_type=jnp.float32)  5.32 us
    dot_general x1, matrix products, expert_math(): up_act = jnp.dot(x_rows, w_up_e, preferred_element_type=jnp.float32)  4.77 us
    gather x2, local copies, waits for them, and re-layouts, body(): tokens[rows]  4.41 us
    reduce_sum x1, other arithmetic, body(): jnp.sum(picked.reshape(tok_dev, top_count, width), axis=1)  4.05 us
    convert_element_type x1, other arithmetic, body(): send_dy = send_dy.astype(jnp.bfloat16)  3.92 us

profile of v2, /device:TPU:1, one launch (start us, length us, event | category | flops | bytes accessed | tf_op | source)
XLA Modules:
  0.0 169.1 jit_solution(5313841552539117059)
XLA Ops:
  0.6 0.0 copy-start
  0.6 0.0 copy-start.1
  0.7 0.8 copy.10
  1.5 0.1 reshape.176
  1.6 0.0 copy-done.1
  1.6 2.4 %gather_fusion.4 = s32[256]{0:T(256)S(1)} fusion(s32[32,4]{0,1:T(4,128)S(1)} %copy-done.1, s32[256]{0:T(256)S(1)} %reshape.176), kind=kCustom, calls=%fused_computation.4 | custom fusion | bytes 4096 | tf_op jit(solution)/shard_map/jit(take_along_axis)/gather | solution.py:119
  4.0 0.1 reshape.179
  4.1 0.1 eq.31
  4.2 0.1 copy.14
  4.3 0.2 fusion.21
  4.6 0.1 eq.27
  4.7 0.2 fusion.22
  4.9 0.1 mul.74
  5.0 1.4 scatter_custom_fusion
  6.5 0.0 copy-done
  6.5 1.8 %gather_fusion = bf16[256,4096]{1,0:T(8,128)(2,1)S(1)} fusion(bf16[32,4096]{1,0:T(8,128)(2,1)S(1)} %copy-done, s32[1024]{0:T(1024)S(1)} %get-tuple-element.13), kind=kCustom, calls=%fused_computation | custom fusion | bytes 4195328 | tf_op jit(solution)/shard_map/gather | solution.py:137
  8.3 2.6 %gather.20 = bf16[1024,1024]{1,0:T(8,128)(2,1)} reshape(bf16[256,4096]{1,0:T(8,128)(2,1)S(1)} %gather_fusion) | data formatting | bytes 4194304 | tf_op jit(solution)/shard_map/gather | solution.py:137
  10.9 0.1 broadcast_in_dim.64
  11.0 0.1 broadcast_in_dim.65
  11.1 0.0 copy-start.2
  11.2 3.2 %broadcast_select_fusion.refs_0_ = bf16[1024,1024]{1,0:T(8,128)(2,1)} fusion(bf16[1024,1024]{1,0:T(8,128)(2,1)} %gather.20, pred[1024]{0:T(1024)(128)(4,1)S(1)} %broadcast_in_dim.65), kind=kLoop, calls=%fused_computation.23 | loop fusion | flops 1048576 | bytes 4195328 | tf_op jit(solution)/shard_map/jit(_where)/select_n | solution.py:137
  14.4 0.0 copy-done.2
  14.4 1.8 %gather_fusion.2 = bf16[256,4096]{1,0:T(8,128)(2,1)S(1)} fusion(bf16[32,4096]{1,0:T(8,128)(2,1)S(1)} %copy-done.2, s32[1024]{0:T(1024)S(1)} %get-tuple-element.13), kind=kCustom, calls=%fused_computation.2 | custom fusion | bytes 4195328 | tf_op jit(solution)/shard_map/gather | solution.py:139
  16.2 0.0 copy-start.8
  16.2 2.9 %reshape.142 = f32[1024,1024]{1,0:T(8,128)} reshape(bf16[256,4096]{1,0:T(8,128)(2,1)S(1)} %gather_fusion.2) | data formatting | bytes 6291456 | tf_op jit(solution)/shard_map/convert_element_type | solution.py:139
  19.1 0.0 copy-done.8
  19.1 0.1 copy.16
  19.2 0.1 reshape.137
  19.3 1.9 %gather_fusion.1 = s32[256]{0:T(256)S(1)} fusion(s32[256]{0:T(256)S(1)} %reshape.137, s32[1024]{0:T(1024)S(1)} %get-tuple-element.12), kind=kCustom, calls=%fused_computation.1 | custom fusion | bytes 3072 | tf_op jit(solution)/shard_map/gather | solution.py:138
  21.2 0.1 mul.77
  21.3 0.1 mul.78
  21.4 3.9 %select_convert_fusion.refs_1_ = bf16[1024,1024]{1,0:T(8,128)(2,1)} fusion(f32[1024,1024]{1,0:T(8,128)} %reshape.142, f32[1024]{0:T(1024)S(1)} %mul.78, pred[1024]{0:T(1024)(128)(4,1)S(1)} %broadcast_in_dim.65), kind=kLoop, calls=%fused_computation.22 | loop fusion | flops 3145728 | bytes 6296576 | tf_op jit(solution)/shard_map/convert_element_type | solution.py:140
  25.4 63.6 %shard_map.95 = (bf16[1024,1024]{1,0:T(8,128)(2,1)}, bf16[1024,1024]{1,0:T(8,128)(2,1)}) custom-call(bf16[1024,1024]{1,0:T(8,128)(2,1)} %broadcast_select_fusion.refs_0_, bf16[1024,1024]{1,0:T(8,128)(2,1)} %select_convert_fusion.refs_1_), custom_call_target="tpu_custom_call" | custom-call | tf_op jit(solution)/shard_map/pallas_call | solution.py:75
  89.0 3.1 %reshape.139 = bf16[256,4096]{1,0:T(8,128)(2,1)S(1)} reshape(bf16[1024,1024]{1,0:T(8,128)(2,1)} %get-tuple-element.5) | data formatting | bytes 4194304 | tf_op jit(solution)/shard_map/reshape | solution.py:144
  92.1 0.0 copy-start.6
  92.1 5.3 %fusion.2 = f32[256,768]{1,0:T(8,128)S(1)} fusion(bf16[256,4096]{1,0:T(8,128)(2,1)S(1)} %reshape.139, bf16[1,4096,768]{2,1,0:T(8,128)(2,1)} %param.13), kind=kOutput, calls=%fused_computation.9 | convolution fusion | flops 1610612736 | bytes 9175040 | tf_op jit(solution)/shard_map/dot_general | solution.py:89
  97.4 0.0 copy-done.6
  97.4 3.1 %reshape.138 = bf16[256,4096]{1,0:T(8,128)(2,1)S(1)} reshape(bf16[1024,1024]{1,0:T(8,128)(2,1)} %get-tuple-element.4) | data formatting | bytes 4194304 | tf_op jit(solution)/shard_map/reshape | solution.py:145
  100.5 0.0 copy-start.3
  100.5 0.0 copy-start.7
  100.6 0.0 slice-start.2
  100.6 0.0 slice-start
  100.6 5.4 %fusion.8 = f32[256,768]{1,0:T(8,128)S(1)} fusion(bf16[256,4096]{1,0:T(8,128)(2,1)S(1)} %reshape.138, bf16[1,768,4096]{2,1,0:T(8,128)(2,1)} %param.15), kind=kOutput, calls=%fused_computation.15 | convolution fusion | flops 1610612736 | bytes 9175040 | tf_op jit(solution)/shard_map/dot_general | solution.py:98
  106.0 0.0 copy-done.3
  106.0 0.0 copy-done.7
  106.0 0.0 slice-start.3
  106.0 0.0 slice-start.1
  106.0 4.8 %fusion.6 = f32[256,768]{1,0:T(8,128)S(1)} fusion(bf16[256,4096]{1,0:T(8,128)(2,1)S(1)} %copy-done.7, bf16[1,4096,768]{2,1,0:T(8,128)(2,1)} %param.14), kind=kOutput, calls=%fused_computation.13 | convolution fusion | flops 1610612736 | bytes 9175040 | tf_op jit(solution)/shard_map/dot_general | solution.py:90
  110.8 0.0 copy-start.5
  110.8 0.9 copy-done.5
  111.7 0.0 slice-done.2
  111.7 0.0 slice-done.3
  111.7 1.9 %fusion = f32[256,4096]{1,0:T(8,128)S(1)} fusion(bf16[1,4096,768]{2,1,0:T(8,128)(2,1)S(1)} %bitcast.47, f32[256,768]{1,0:T(8,128)S(1)} %fusion.2, f32[256,768]{1,0:T(8,128)S(1)} %fusion.8, f32[256,768]{1,0:T(8,128)S(1)} %fusion.6), kind=kOutput, calls=%fused_computation.7 | convolution fusion | flops 1612578816 | bytes 12845056 | tf_op jit(solution)/shard_map/dot_general | solution.py:104
  113.6 0.0 slice-done
  113.6 0.0 slice-done.1
  113.7 1.8 %fusion.14 = bf16[256,4096]{1,0:T(8,128)(2,1)S(1)} fusion(f32[256,4096]{1,0:T(8,128)S(1)} %fusion, bf16[1,4096,768]{2,1,0:T(8,128)(2,1)S(1)} %bitcast.45, f32[256,768]{1,0:T(8,128)S(1)} %fusion.8, f32[256,768]{1,0:T(8,128)S(1)} %fusion.2), kind=kOutput, calls=%fused_computation.19 | convolution fusion | flops 1613889536 | bytes 14155776 | tf_op jit(solution)/shard_map/dot_general | solution.py:105
  115.5 2.6 %reshape.140.refs_0_ = bf16[1024,1024]{1,0:T(8,128)(2,1)} reshape(bf16[256,4096]{1,0:T(8,128)(2,1)S(1)} %fusion.14) | data formatting | bytes 4194304 | tf_op jit(solution)/shard_map/reshape | solution.py:147
  118.1 34.9 %shard_map.96 = bf16[1024,1024]{1,0:T(8,128)(2,1)} custom-call(bf16[1024,1024]{1,0:T(8,128)(2,1)} %reshape.140.refs_0_), custom_call_target="tpu_custom_call" | custom-call | tf_op jit(solution)/shard_map/pallas_call | solution.py:75
  153.0 3.1 %reshape.141 = bf16[256,4096]{1,0:T(8,128)(2,1)S(1)} reshape(bf16[1024,1024]{1,0:T(8,128)(2,1)} %shard_map.96) | data formatting | bytes 4194304 | tf_op jit(solution)/shard_map/reshape | solution.py:148
  156.1 3.2 %gather_fusion.3 = bf16[256,4096]{1,0:T(8,128)(2,1)} fusion(bf16[256,4096]{1,0:T(8,128)(2,1)S(1)} %reshape.141, s32[1024]{0:T(1024)S(1)} %pad_clamp_fusion), kind=kCustom, calls=%fused_computation.3 | custom fusion | bytes 4195328 | tf_op jit(solution)/shard_map/gather | solution.py:150
  159.3 0.1 lt.62
  159.4 4.1 %fusion.17 = bf16[32,4096]{1,0:T(8,128)(2,1)} fusion(bf16[256,4096]{1,0:T(8,128)(2,1)} %gather_fusion.3, pred[32,8]{1,0:T(8,128)(4,1)S(1)} %lt.62), kind=kLoop, calls=%fused_computation.21 | loop fusion | flops 3014656 | bytes 2359552 | tf_op jit(solution)/shard_map/reduce_sum | solution.py:151
  163.4 0.0 copy-done.4
  163.4 5.7 %fusion.10 = bf16[1,768,4096]{2,1,0:T(8,128)(2,1)} fusion(bf16[256,4096]{1,0:T(8,128)(2,1)S(1)} %copy-done.4, f32[256,768]{1,0:T(8,128)} %copy-done.5, f32[256,768]{1,0:T(8,128)S(1)} %fusion.2), kind=kOutput, calls=%fused_computation.17 | convolution fusion | flops 1614938112 | bytes 9961472 | tf_op jit(solution)/shard_map/dot_general | solution.py:95
  (20 shorter events, 0.2 us)
Async XLA Ops:
  0.6 5.8 %copy-start = (bf16[32,4096]{1,0:T(8,128)(2,1)S(1)}, bf16[32,4096]{1,0:T(8,128)(2,1)}, u32[]{:S(2)}) copy-start(bf16[32,4096]{1,0:T(8,128)(2,1)} %param.8) | copy-start | bytes 786436
  0.6 0.9 copy-start.1
  11.1 3.2 %copy-start.2 = (bf16[32,4096]{1,0:T(8,128)(2,1)S(1)}, bf16[32,4096]{1,0:T(8,128)(2,1)}, u32[]{:S(2)}) copy-start(bf16[32,4096]{1,0:T(8,128)(2,1)} %param.9) | copy-start | bytes 786436
  16.2 2.9 %copy-start.8 = (s32[32,8]{0,1:T(8,128)S(1)}, s32[32,8]{0,1:T(8,128)}, u32[]{:S(2)}) copy-start(s32[32,8]{0,1:T(8,128)} %param.12) | copy-start | bytes 3076
  92.1 5.3 %copy-start.6 = (bf16[256,4096]{1,0:T(8,128)(2,1)}, bf16[256,4096]{1,0:T(8,128)(2,1)S(1)}, u32[]{:S(2)}) copy-start(bf16[256,4096]{1,0:T(8,128)(2,1)S(1)} %reshape.139) | copy-start | bytes 6291460
  100.5 5.4 %copy-start.3 = (bf16[256,4096]{1,0:T(8,128)(2,1)}, bf16[256,4096]{1,0:T(8,128)(2,1)S(1)}, u32[]{:S(2)}) copy-start(bf16[256,4096]{1,0:T(8,128)(2,1)S(1)} %reshape.138) | copy-start | bytes 6291460
  100.5 5.4 %copy-start.7 = (bf16[256,4096]{1,0:T(8,128)(2,1)S(1)}, bf16[256,4096]{1,0:T(8,128)(2,1)}, u32[]{:S(2)}) copy-start(bf16[256,4096]{1,0:T(8,128)(2,1)} %copy-done.6) | copy-start | bytes 6291460
  100.6 11.1 %slice-start.2 = ((s8[6291456]{0:T(1024)(128)(4,1)}), s8[4194304]{0:T(1024)(128)(4,1)S(1)}, s32[]{:S(2)}) async-start(s8[6291456]{0:T(1024)(128)(4,1)} %bitcast.46), calls=%async_computation.2 | async-start | bytes 8388608
  100.6 13.1 %slice-start = ((s8[6291456]{0:T(1024)(128)(4,1)}), s8[4194304]{0:T(1024)(128)(4,1)S(1)}, s32[]{:S(2)}) async-start(s8[6291456]{0:T(1024)(128)(4,1)} %bitcast.44), calls=%async_computation | async-start | bytes 8388608
  106.0 5.7 %slice-start.3 = ((s8[6291456]{0:T(1024)(128)(4,1)}), s8[2097152]{0:T(1024)(128)(4,1)S(1)}, s32[]{:S(2)}) async-start(s8[6291456]{0:T(1024)(128)(4,1)} %bitcast.46), calls=%async_computation.3 | async-start | bytes 4194304
  106.0 7.6 %slice-start.1 = ((s8[6291456]{0:T(1024)(128)(4,1)}), s8[2097152]{0:T(1024)(128)(4,1)S(1)}, s32[]{:S(2)}) async-start(s8[6291456]{0:T(1024)(128)(4,1)} %bitcast.44), calls=%async_computation.1 | async-start | bytes 4194304
  110.8 0.9 copy-start.5
  159.3 4.2 %copy-start.4 = (bf16[256,4096]{1,0:T(8,128)(2,1)S(1)}, bf16[256,4096]{1,0:T(8,128)(2,1)}, u32[]{:S(2)}) copy-start(bf16[256,4096]{1,0:T(8,128)(2,1)} %copy-done.3) | copy-start | bytes 6291460

commit v3 on v0

--- a/solution.py
+++ b/solution.py
@@ -5,23 +5,19 @@
 
 
 def expert_math(x_rows, dy_rows, w_gate_e, w_up_e, w_down_e):
-    gate_act = jnp.dot(x_rows, w_gate_e, preferred_element_type=jnp.float32)
-    up_act = jnp.dot(x_rows, w_up_e, preferred_element_type=jnp.float32)
+    gate_act = jnp.einsum("psd,dh->psh", x_rows, w_gate_e, preferred_element_type=jnp.float32)
+    up_act = jnp.einsum("psd,dh->psh", x_rows, w_up_e, preferred_element_type=jnp.float32)
     sig = jax.nn.sigmoid(gate_act)
     hidden = (gate_act * sig * up_act).astype(jnp.bfloat16)
-    contract_rows = (((0,), (0,)), ((), ()))
-    contract_last = (((1,), (1,)), ((), ()))
-    down_local = lax.dot_general(
-        hidden, dy_rows, contract_rows, preferred_element_type=jnp.float32
+    down_local = jnp.einsum(
+        "psh,psd->hd", hidden, dy_rows, preferred_element_type=jnp.float32
     ).astype(jnp.bfloat16)
-    hidden_grad = lax.dot_general(
-        dy_rows, w_down_e, contract_last, preferred_element_type=jnp.float32
-    )
+    hidden_grad = jnp.einsum("psd,hd->psh", dy_rows, w_down_e, preferred_element_type=jnp.float32)
     gate_grad = (hidden_grad * up_act * sig * (1.0 + gate_act * (1.0 - sig))).astype(jnp.bfloat16)
     up_grad = (hidden_grad * gate_act * sig).astype(jnp.bfloat16)
     row_grad = (
-        lax.dot_general(gate_grad, w_gate_e, contract_last, preferred_element_type=jnp.float32)
-        + lax.dot_general(up_grad, w_up_e, contract_last, preferred_element_type=jnp.float32)
+        jnp.einsum("psh,dh->psd", gate_grad, w_gate_e, preferred_element_type=jnp.float32)
+        + jnp.einsum("psh,dh->psd", up_grad, w_up_e, preferred_element_type=jnp.float32)
     ).astype(jnp.bfloat16)
     return (down_local, row_grad)
 
@@ -53,26 +49,16 @@
     valid = table >= 0
     safe = jnp.maximum(table, 0)
     rows = safe // top_count
-    send_x = jnp.where(valid[:, None], tokens[rows], jnp.zeros((), jnp.bfloat16)).reshape(
-        experts, capacity, width
-    )
+    x_sel = jnp.where(valid[:, None], tokens[rows], jnp.zeros((), jnp.bfloat16))
     gate_val = gate_flat[safe].astype(jnp.float32) * (1.0 / 65536.0)
-    send_dy = jnp.where(valid[:, None], gate_val[:, None] * out_grad[rows].astype(jnp.float32), 0.0)
-    send_dy = send_dy.astype(jnp.bfloat16).reshape(experts, capacity, width)
-    recv_x, recv_dy = (
-        lax.all_to_all(send_x, ("node", "local"), split_axis=0, concat_axis=0, tiled=True),
-        lax.all_to_all(send_dy, ("node", "local"), split_axis=0, concat_axis=0, tiled=True),
-    )
-    x_rows = recv_x.reshape(experts * capacity, width)
-    dy_rows = recv_dy.reshape(experts * capacity, width)
-    down_local, row_grad = expert_math(x_rows, dy_rows, w_gate_e, w_up_e, w_down_e)
-    returned = lax.all_to_all(
-        row_grad.reshape(experts, capacity, width),
-        ("node", "local"),
-        split_axis=0,
-        concat_axis=0,
-        tiled=True,
-    )
+    dy_sel = (gate_val[:, None] * out_grad[rows].astype(jnp.float32)).astype(jnp.bfloat16)
+    dy_sel = jnp.where(valid[:, None], dy_sel, jnp.zeros((), jnp.bfloat16))
+    send_x = x_sel.reshape(experts, capacity, width)
+    send_dy = dy_sel.reshape(experts, capacity, width)
+    recv_x = lax.all_to_all(send_x, ("node", "local"), split_axis=0, concat_axis=0, tiled=True)
+    recv_dy = lax.all_to_all(send_dy, ("node", "local"), split_axis=0, concat_axis=0, tiled=True)
+    down_local, row_grad = expert_math(recv_x, recv_dy, w_gate_e, w_up_e, w_down_e)
+    returned = lax.all_to_all(row_grad, ("node", "local"), split_axis=0, concat_axis=0, tiled=True)
     returned = returned.reshape(experts * capacity, width)
     lookup = jnp.where(kept, position, 0)
     picked = jnp.where(kept[:, None], returned[lookup].astype(jnp.float32), 0.0)

time: 160 us -> 172 us (1.075)
  blocking collectives: 0 us -> 42.2 us
  waiting for transfers between devices: 58.4 us -> 41.5 us
  starting transfers between devices: 21.9 us -> 10.1 us
  matrix products: 26.6 us -> 36.1 us
  local copies, waits for them, and re-layouts: 35.3 us -> 29.3 us
  other arithmetic: 16.2 us -> 11.1 us
    all_to_all x0 -> x1, blocking collectives: none -> 42.2 us  [body(): lax.all_to_all(send_x, ('node', 'local'), split_axis=0, concat_axis=0, ti...]
    all_to_all x2 -> x1, waiting for transfers between devices: 40.2 us -> 22.9 us  [body(): lax.all_to_all(row_grad, ('node', 'local'), split_axis=0, concat_axis=0,...]
    all_to_all x2 -> x1, starting transfers between devices: 16.9 us -> 4.89 us  [body(): lax.all_to_all(row_grad, ('node', 'local'), split_axis=0, concat_axis=0,...]
    reshape x3 -> x0, local copies, waits for them, and re-layouts: 11.4 us -> none  [the longest x1 4.39 us: body(): row_grad.reshape(experts, capacity, width)]
    dot_general x6, matrix products: 26.6 us -> 36.1 us  [the longest x1 7.64 us: expert_math(): jnp.einsum('psh,psd->hd', hidden, dy_rows, preferred_element_type=jnp.flo...]
    convert_element_type x1 -> x0, other arithmetic: 6.94 us -> none  [body(): send_dy = send_dy.astype(jnp.bfloat16).reshape(experts, capacity, width)]
    convert_element_type x0 -> x1, local copies, waits for them, and re-layouts: none -> 3.52 us  [expert_math(): row_grad = (jnp.einsum('psh,dh->psd', gate_grad, w_gate_e, preferred_elem...]
    gather x2, local copies, waits for them, and re-layouts: 4.47 us -> 6.35 us  [body(): x_sel = jnp.where(valid[:, None], tokens[rows], jnp.zeros((), jnp.bfloat16))]
  transfers between devices with their start and end apart: 3 -> 2, of which waited for: 3 -> 2; matrix products, arithmetic and copies ran while one was open for 21% -> 11% of each run, Pallas kernels for 0% -> 0%
where the time goes in v3:
time: 172 us; the launch traced here: 171 us
  blocking collectives  42.2 us (25%)
  waiting for transfers between devices  41.5 us (24%)
  matrix products  36.1 us (21%)
  local copies, waits for them, and re-layouts  29.3 us (17%)
  other arithmetic  11.1 us (6%)
  starting transfers between devices  10.1 us (6%)
    all_to_all x1, blocking collectives, body(): lax.all_to_all(send_x, ('node', 'local'), split_axis=0, concat_axis=0, ti...  42.2 us
    all_to_all x1, waiting for transfers between devices, body(): lax.all_to_all(row_grad, ('node', 'local'), split_axis=0, concat_axis=0,...  22.9 us
    all_to_all x1, waiting for transfers between devices, body(): lax.all_to_all(send_dy, ('node', 'local'), split_axis=0, concat_axis=0, t...  18.6 us
    dot_general x1, matrix products, expert_math(): jnp.einsum('psh,psd->hd', hidden, dy_rows, preferred_element_type=jnp.flo...  7.64 us
    dot_general x1, matrix products, expert_math(): jnp.einsum('psd,hd->psh', dy_rows, w_down_e, preferred_element_type=jnp.f...  7.18 us
    dot_general x1, matrix products, expert_math(): jnp.einsum('psd,dh->psh', x_rows, w_gate_e, preferred_element_type=jnp.fl...  7.16 us
    select_n x1, other arithmetic, body(): dy_sel = jnp.where(valid[:, None], dy_sel, jnp.zeros((), jnp.bfloat16))  6.67 us
    gather x2, local copies, waits for them, and re-layouts, body(): x_sel = jnp.where(valid[:, None], tokens[rows], jnp.zeros((), jnp.bfloat16))  6.35 us
  transfers between devices with their start and end apart: 2, of which 2 were waited for; matrix products, arithmetic and copies ran while one was open for 11% of the time, Pallas kernels for 0%

profile of v3, /device:TPU:1, one launch (start us, length us, event | category | flops | bytes accessed | tf_op | source)
XLA Modules:
  0.0 171.3 jit_solution(7436586627833071267)
XLA Ops:
  0.6 0.0 copy-start
  0.6 0.0 copy-start.1
  0.7 0.8 copy.24
  1.5 0.1 reshape.179
  1.6 0.0 copy-done.1
  1.6 2.4 %gather_fusion.4 = s32[256]{0:T(256)S(1)} fusion(s32[32,4]{0,1:T(4,128)S(1)} %copy-done.1, s32[256]{0:T(256)S(1)} %reshape.179), kind=kCustom, calls=%fused_computation.4 | custom fusion | bytes 4096 | tf_op jit(solution)/shard_map/jit(take_along_axis)/gather | solution.py:34
  4.0 0.1 reshape.182
  4.1 0.1 eq.31
  4.2 0.1 eq.27
  4.3 0.1 copy.28
  4.4 0.2 fusion.25
  4.7 0.2 fusion.26
  4.9 0.1 mul.73
  5.0 1.4 scatter_custom_fusion
  6.5 0.2 broadcast_in_dim.60
  6.6 0.0 copy-done
  6.7 1.8 %gather_fusion.1 = bf16[256,4096]{1,0:T(8,128)(2,1)S(1)} fusion(bf16[32,4096]{1,0:T(8,128)(2,1)S(1)} %copy-done, s32[1024]{0:T(1024)S(1)} %get-tuple-element.10), kind=kCustom, calls=%fused_computation.1 | custom fusion | bytes 4195328 | tf_op jit(solution)/shard_map/gather | solution.py:54
  8.5 0.0 copy-start.5
  8.5 3.9 %reshape.145 = f32[128,2,4096]{2,1,0:T(2,128)} reshape(bf16[256,4096]{1,0:T(8,128)(2,1)S(1)} %gather_fusion.1) | data formatting | bytes 6291456 | tf_op jit(solution)/shard_map/convert_element_type | solution.py:54
  12.4 0.0 copy-done.5
  12.4 0.0 copy-start.2
  12.4 0.1 copy.30
  12.5 0.1 reshape.143
  12.6 1.9 %gather_fusion = s32[256]{0:T(256)S(1)} fusion(s32[256]{0:T(256)S(1)} %reshape.143, s32[1024]{0:T(1024)S(1)} %get-tuple-element.11), kind=kCustom, calls=%fused_computation | custom fusion | bytes 3072 | tf_op jit(solution)/shard_map/gather | solution.py:53
  14.6 0.1 mul.76
  14.7 0.0 copy-done.2
  14.7 3.2 %gather_fusion.2 = bf16[256,4096]{1,0:T(8,128)(2,1)} fusion(bf16[32,4096]{1,0:T(8,128)(2,1)S(1)} %copy-done.2, s32[1024]{0:T(1024)S(1)} %get-tuple-element.10), kind=kCustom, calls=%fused_computation.2 | custom fusion | bytes 4195328 | tf_op jit(solution)/shard_map/gather | solution.py:52
  17.9 3.2 %gather.22 = bf16[128,2,4096]{2,1,0:T(2,128)(2,1)S(1)} reshape(bf16[256,4096]{1,0:T(8,128)(2,1)} %gather_fusion.2) | data formatting | bytes 4194304 | tf_op jit(solution)/shard_map/gather | solution.py:52
  21.1 6.7 %broadcast_select_fusion.1 = (bf16[128,2,4096]{2,1,0:T(2,128)(2,1)}, bf16[128,2,4096]{2,1,0:T(2,128)(2,1)S(1)}) fusion(pred[128,2]{1,0:T(8,128)(4,1)S(1)} %broadcast_in_dim.60, f32[128,2,4096]{2,1,0:T(2,128)} %reshape.145, f32[128,2]{1,0:T(8,128)S(1)} %mul.76, bf16[128,2,4096]{2,1,0:T(2,128)(2,1)S(1)} %gather.22), kind=kLoop, calls=%fused_computation.24 | loop fusion | flops 4194304 | bytes 10487040 | tf_op jit(solution)/shard_map/jit(_where)/select_n | solution.py:55
  27.8 42.2 %all_to_all.15 = bf16[128,2,4096]{2,1,0:T(2,128)(2,1)} all-to-all(bf16[128,2,4096]{2,1,0:T(2,128)(2,1)S(1)} %get-tuple-element.5), channel_id=1, replica_groups=mesh['node'=32,'local'=4] {'node','local'}, dimensions={0} | all-to-all | bytes 4194304 | tf_op jit(solution)/shard_map/all_to_all | solution.py:58
  70.0 0.0 slice-start
  70.0 5.2 %all-to-all-start = ((bf16[128,2,4096]{2,1,0:T(2,128)(2,1)}), bf16[128,2,4096]{2,1,0:T(2,128)(2,1)}, u32[]{:S(2)}, u32[]{:S(2)}) async-start(bf16[128,2,4096]{2,1,0:T(2,128)(2,1)} %get-tuple-element.4), calls=%async_computation | async-start | bytes 4194304 | tf_op jit(solution)/shard_map/all_to_all | solution.py:59
  75.2 0.0 slice-start.1
  75.2 0.0 copy-start.3
  75.2 7.2 %fusion.2 = f32[128,2,768]{2,0,1:T(8,128)S(1)} fusion(bf16[1,4096,768]{2,1,0:T(8,128)(2,1)} %param.13, bf16[128,2,4096]{2,1,0:T(2,128)(2,1)} %all_to_all.15), kind=kOutput, calls=%fused_computation.9 | convolution fusion | flops 1610612736 | bytes 9175040 | tf_op jit(solution)/shard_map/psd,dh->psh/dot_general | solution.py:8
  82.4 0.0 slice-done
  82.4 0.0 slice-done.1
  82.4 0.0 copy-done.3
  82.4 4.6 %fusion.6 = f32[128,2,768]{2,0,1:T(8,128)} fusion(bf16[1,4096,768]{2,1,0:T(8,128)(2,1)S(1)} %bitcast.48, bf16[128,2,4096]{2,1,0:T(2,128)(2,1)S(1)} %copy-done.3), kind=kOutput, calls=%fused_computation.13 | convolution fusion | flops 1610612736 | bytes 9175040 | tf_op jit(solution)/shard_map/psd,dh->psh/dot_general | solution.py:9
  87.0 0.0 copy-start.4
  87.0 18.6 %all-to-all-done = bf16[128,2,4096]{2,1,0:T(2,128)(2,1)} async-done(((bf16[128,2,4096]{2,1,0:T(2,128)(2,1)}), bf16[128,2,4096]{2,1,0:T(2,128)(2,1)}, u32[]{:S(2)}, u32[]{:S(2)}) %all-to-all-start) | async-done | bytes 2097184 | tf_op jit(solution)/shard_map/all_to_all | solution.py:59
  105.6 7.2 %fusion.8 = f32[128,2,768]{2,0,1:T(8,128)S(1)} fusion(bf16[1,768,4096]{2,1,0:T(8,128)(2,1)} %param.15, bf16[128,2,4096]{2,1,0:T(2,128)(2,1)} %all-to-all-done), kind=kOutput, calls=%fused_computation.15 | convolution fusion | flops 1610612736 | bytes 9175040 | tf_op jit(solution)/shard_map/psd,hd->psh/dot_general | solution.py:15
  112.8 0.0 copy-done.4
  112.8 4.7 %fusion = f32[128,2,4096]{2,0,1:T(8,128)S(1)} fusion(bf16[1,4096,768]{2,1,0:T(8,128)(2,1)} %param.13, f32[128,2,768]{2,0,1:T(8,128)S(1)} %fusion.2, f32[128,2,768]{2,0,1:T(8,128)S(1)} %fusion.8, f32[128,2,768]{2,0,1:T(8,128)S(1)} %copy-done.4), kind=kOutput, calls=%fused_computation.7 | convolution fusion | flops 1612578816 | bytes 12845056 | tf_op jit(solution)/shard_map/psh,dh->psd/dot_general | solution.py:19
  117.5 4.8 %fusion.14 = bf16[128,2,4096]{2,0,1:T(8,128)(2,1)S(1)} fusion(f32[128,2,4096]{2,0,1:T(8,128)S(1)} %fusion, bf16[1,4096,768]{2,1,0:T(8,128)(2,1)} %param.14, f32[128,2,768]{2,0,1:T(8,128)S(1)} %fusion.8, f32[128,2,768]{2,0,1:T(8,128)S(1)} %fusion.2), kind=kOutput, calls=%fused_computation.19 | convolution fusion | flops 1613889536 | bytes 14155776 | tf_op jit(solution)/shard_map/psh,dh->psd/dot_general | solution.py:20
  122.4 3.5 %copy.34 = bf16[128,2,4096]{2,1,0:T(2,128)(2,1)} copy(bf16[128,2,4096]{2,0,1:T(8,128)(2,1)S(1)} %fusion.14) | data formatting | bytes 4194304 | tf_op jit(solution)/shard_map/convert_element_type | solution.py:21
  125.9 4.9 %all-to-all-start.2 = ((bf16[128,2,4096]{2,1,0:T(2,128)(2,1)}), bf16[128,2,4096]{2,1,0:T(2,128)(2,1)}, u32[]{:S(2)}, u32[]{:S(2)}) async-start(bf16[128,2,4096]{2,1,0:T(2,128)(2,1)} %copy.34), calls=%async_computation.2 | async-start | bytes 4194304 | tf_op jit(solution)/shard_map/all_to_all | solution.py:61
  130.8 0.1 lt.62
  130.9 7.6 %fusion.10 = bf16[1,768,4096]{2,1,0:T(8,128)(2,1)} fusion(bf16[128,2,4096]{2,1,0:T(2,128)(2,1)} %all-to-all-done, f32[128,2,768]{2,0,1:T(8,128)S(1)} %copy-done.4, f32[128,2,768]{2,0,1:T(8,128)S(1)} %fusion.2), kind=kOutput, calls=%fused_computation.17 | convolution fusion | flops 1614938112 | bytes 9961472 | tf_op jit(solution)/shard_map/psh,psd->hd/dot_general | solution.py:12
  138.5 22.9 %all-to-all-done.2 = bf16[128,2,4096]{2,1,0:T(2,128)(2,1)} async-done(((bf16[128,2,4096]{2,1,0:T(2,128)(2,1)}), bf16[128,2,4096]{2,1,0:T(2,128)(2,1)}, u32[]{:S(2)}, u32[]{:S(2)}) %all-to-all-start.2) | async-done | bytes 2097184 | tf_op jit(solution)/shard_map/all_to_all | solution.py:61
  161.4 2.7 %reshape.144 = bf16[256,4096]{1,0:T(8,128)(2,1)S(1)} reshape(bf16[128,2,4096]{2,1,0:T(2,128)(2,1)} %all-to-all-done.2) | data formatting | bytes 4194304 | tf_op jit(solution)/shard_map/reshape | solution.py:62
  164.2 3.2 %gather_fusion.3 = bf16[256,4096]{1,0:T(8,128)(2,1)} fusion(bf16[256,4096]{1,0:T(8,128)(2,1)S(1)} %reshape.144, s32[1024]{0:T(1024)S(1)} %pad_clamp_fusion), kind=kCustom, calls=%fused_computation.3 | custom fusion | bytes 4195328 | tf_op jit(solution)/shard_map/gather | solution.py:64
  167.3 3.9 %fusion.17 = bf16[32,4096]{1,0:T(8,128)(2,1)} fusion(bf16[256,4096]{1,0:T(8,128)(2,1)} %gather_fusion.3, pred[32,8]{1,0:T(8,128)(4,1)S(1)} %lt.62), kind=kLoop, calls=%fused_computation.21 | loop fusion | flops 3014656 | bytes 2359552 | tf_op jit(solution)/shard_map/reduce_sum | solution.py:65
  (18 shorter events, 0.2 us)
Async XLA Ops:
  0.6 6.0 %copy-start = (bf16[32,4096]{1,0:T(8,128)(2,1)S(1)}, bf16[32,4096]{1,0:T(8,128)(2,1)}, u32[]{:S(2)}) copy-start(bf16[32,4096]{1,0:T(8,128)(2,1)} %param.9) | copy-start | bytes 786436
  0.6 0.9 copy-start.1
  8.5 3.9 %copy-start.5 = (s32[32,8]{0,1:T(8,128)S(1)}, s32[32,8]{0,1:T(8,128)}, u32[]{:S(2)}) copy-start(s32[32,8]{0,1:T(8,128)} %param.12) | copy-start | bytes 3076
  12.4 2.3 %copy-start.2 = (bf16[32,4096]{1,0:T(8,128)(2,1)S(1)}, bf16[32,4096]{1,0:T(8,128)(2,1)}, u32[]{:S(2)}) copy-start(bf16[32,4096]{1,0:T(8,128)(2,1)} %param.8) | copy-start | bytes 786436
  70.0 12.4 %slice-start = ((s8[6291456]{0:T(1024)(128)(4,1)}), s8[2097152]{0:T(1024)(128)(4,1)S(1)}, s32[]{:S(2)}) async-start(s8[6291456]{0:T(1024)(128)(4,1)} %bitcast.47), calls=%async_computation.3 | async-start | bytes 4194304
  70.0 35.6 %all-to-all-start = ((bf16[128,2,4096]{2,1,0:T(2,128)(2,1)}), bf16[128,2,4096]{2,1,0:T(2,128)(2,1)}, u32[]{:S(2)}, u32[]{:S(2)}) async-start(bf16[128,2,4096]{2,1,0:T(2,128)(2,1)} %get-tuple-element.4), calls=%async_computation | async-start | bytes 4194304 | tf_op jit(solution)/shard_map/all_to_all | solution.py:59
  75.2 7.2 %slice-start.1 = ((s8[6291456]{0:T(1024)(128)(4,1)}), s8[4194304]{0:T(1024)(128)(4,1)S(1)}, s32[]{:S(2)}) async-start(s8[6291456]{0:T(1024)(128)(4,1)} %bitcast.47), calls=%async_computation.4 | async-start | bytes 8388608
  75.2 7.2 %copy-start.3 = (bf16[128,2,4096]{2,1,0:T(2,128)(2,1)S(1)}, bf16[128,2,4096]{2,1,0:T(2,128)(2,1)}, u32[]{:S(2)}) copy-start(bf16[128,2,4096]{2,1,0:T(2,128)(2,1)} %all_to_all.15) | copy-start | bytes 6291460
  87.0 25.8 %copy-start.4 = (f32[128,2,768]{2,0,1:T(8,128)S(1)}, f32[128,2,768]{2,0,1:T(8,128)}, u32[]{:S(2)}) copy-start(f32[128,2,768]{2,0,1:T(8,128)} %fusion.6) | copy-start | bytes 2359300
  125.9 35.5 %all-to-all-start.2 = ((bf16[128,2,4096]{2,1,0:T(2,128)(2,1)}), bf16[128,2,4096]{2,1,0:T(2,128)(2,1)}, u32[]{:S(2)}, u32[]{:S(2)}) async-start(bf16[128,2,4096]{2,1,0:T(2,128)(2,1)} %copy.34), calls=%async_computation.2 | async-start | bytes 4194304 | tf_op jit(solution)/shard_map/all_to_all | solution.py:61

commit v4 on v2

--- a/solution.py
+++ b/solution.py
@@ -134,21 +134,28 @@
     valid = table >= 0
     safe = jnp.maximum(table, 0)
     rows = safe // top_count
-    send_x = jnp.where(valid[:, None], tokens[rows], jnp.zeros((), jnp.bfloat16))
-    gate_val = gate_flat[safe].astype(jnp.float32) * (1.0 / 65536.0)
-    send_dy = jnp.where(valid[:, None], gate_val[:, None] * out_grad[rows].astype(jnp.float32), 0.0)
-    send_dy = send_dy.astype(jnp.bfloat16)
     tile_rows = 8
-    flat = (experts * tile_rows, capacity * width // tile_rows)
-    x_rows, dy_rows = exchange(send_x.reshape(flat), send_dy.reshape(flat))
-    x_rows = x_rows.reshape(experts * capacity, width)
-    dy_rows = dy_rows.reshape(experts * capacity, width)
+    blocks = tile_rows // capacity
+    piece = width // blocks
+    holds = valid[:, None] & (rows[:, None] == jnp.arange(tok_dev, dtype=jnp.int32)[None, :])
+    same_block = jnp.eye(blocks, dtype=jnp.bool_)
+    select = (holds[:, None, :, None] & same_block[None, :, None, :]).reshape(
+        experts * tile_rows, tok_dev * blocks
+    ).astype(jnp.bfloat16)
+    tok_pieces = tokens.reshape(tok_dev * blocks, piece)
+    og_pieces = out_grad.reshape(tok_dev * blocks, piece)
+    send_x = jnp.dot(select, tok_pieces, preferred_element_type=jnp.float32).astype(jnp.bfloat16)
+    gate_val = jnp.where(valid, gate_flat[safe].astype(jnp.float32) * (1.0 / 65536.0), 0.0)
+    gate_rows = jnp.repeat(gate_val, blocks)
+    og_sel = jnp.dot(select, og_pieces, preferred_element_type=jnp.float32)
+    send_dy = (gate_rows[:, None] * og_sel).astype(jnp.bfloat16)
+    x_flat, dy_flat = exchange(send_x, send_dy)
+    x_rows = x_flat.reshape(experts * capacity, width)
+    dy_rows = dy_flat.reshape(experts * capacity, width)
     down_local, row_grad = expert_math(x_rows, dy_rows, w_gate_e, w_up_e, w_down_e)
-    (returned,) = exchange(row_grad.reshape(flat))
-    returned = returned.reshape(experts * capacity, width)
-    lookup = jnp.where(kept, position, 0)
-    picked = jnp.where(kept[:, None], returned[lookup].astype(jnp.float32), 0.0)
-    token_grad = jnp.sum(picked.reshape(tok_dev, top_count, width), axis=1).astype(jnp.bfloat16)
+    (returned,) = exchange(row_grad.reshape(experts * tile_rows, piece))
+    total = jnp.dot(select.T, returned, preferred_element_type=jnp.float32)
+    token_grad = total.reshape(tok_dev, width).astype(jnp.bfloat16)
     return (token_grad, down_local[None])
 
 

time: 170 us -> 173 us (1.018)
  matrix products: 25 us -> 31.9 us
  other arithmetic: 11.7 us -> 5.02 us
  local copies, waits for them, and re-layouts: 32.9 us -> 36 us
    and x0 -> x1, local copies, waits for them, and re-layouts: none -> 15.9 us  [body(): holds[:, None, :, None] & same_block[None, :, None, :]]
    gather x5 -> x1, local copies, waits for them, and re-layouts: 11.4 us -> 1.95 us  [body(): gate_flat[safe].astype(jnp.float32) * (1.0 / 65536.0)]
    dot_general x0 -> x3, matrix products: none -> 6.16 us  [the longest x1 2.09 us: body(): total = jnp.dot(select.T, returned, preferred_element_type=jnp.float32)]
    and x0 -> x2, other arithmetic: none -> 4.48 us  [the longest x1 4.34 us: body(): holds[:, None, :, None] & same_block[None, :, None, :]]
    reduce_sum x1 -> x0, other arithmetic: 4.05 us -> none  [body(): jnp.sum(picked.reshape(tok_dev, top_count, width), axis=1)]
    convert_element_type x1 -> x0, other arithmetic: 3.92 us -> none  [body(): send_dy = send_dy.astype(jnp.bfloat16)]
    select_n x2, other arithmetic: 3.21 us -> 0.01 us  [the longest x1 0.01 us: body(): table.at[position]]
    convert_element_type x1, local copies, waits for them, and re-layouts: 2.87 us -> 0.87 us  [body(): token_grad = total.reshape(tok_dev, width).astype(jnp.bfloat16)]
where the time goes in v4:
time: 173 us; the launch traced here: 172 us
  Pallas kernels  98.5 us (57%)
  local copies, waits for them, and re-layouts  36 us (21%)
  matrix products  31.9 us (18%)
  other arithmetic  5.02 us (3%)
    pallas_call x2, Pallas kernels, exchange(): pl.pallas_call(functools.partial(_exchange_kernel, n_local), out_shape=[j...  98.5 us
    and x1, local copies, waits for them, and re-layouts, body(): holds[:, None, :, None] & same_block[None, :, None, :]  15.9 us
    dot_general x1, matrix products, expert_math(): lax.dot_general(hidden, dy_rows, contract_rows, preferred_element_type=jn...  5.72 us
    dot_general x1, matrix products, expert_math(): gate_act = jnp.dot(x_rows, w_gate_e, preferred_element_type=jnp.float32)  5.35 us
    dot_general x1, matrix products, expert_math(): lax.dot_general(dy_rows, w_down_e, contract_last, preferred_element_type=...  4.77 us
    dot_general x1, matrix products, expert_math(): up_act = jnp.dot(x_rows, w_up_e, preferred_element_type=jnp.float32)  4.74 us
    reshape x1, local copies, waits for them, and re-layouts, body(): returned, = exchange(row_grad.reshape(experts * tile_rows, piece))  4.35 us
    and x1, other arithmetic, body(): holds[:, None, :, None] & same_block[None, :, None, :]  4.34 us

profile of v4, /device:TPU:1, one launch (start us, length us, event | category | flops | bytes accessed | tf_op | source)
XLA Modules:
  0.0 172.4 jit_solution(9555432008565599384)
XLA Ops:
  0.6 0.0 copy-start
  0.7 0.8 copy.10
  1.4 0.1 reshape.167
  1.5 0.0 copy-done
  1.5 0.0 copy-start.6
  1.6 2.4 %gather_fusion.1 = s32[256]{0:T(256)S(1)} fusion(s32[32,4]{0,1:T(4,128)S(1)} %copy-done, s32[256]{0:T(256)S(1)} %reshape.167), kind=kCustom, calls=%fused_computation.1 | custom fusion | bytes 4096 | tf_op jit(solution)/shard_map/jit(take_along_axis)/gather | solution.py:119
  4.0 0.1 reshape.170
  4.1 0.1 eq.55
  4.2 0.1 copy.14
  4.3 0.2 fusion.20
  4.6 0.1 eq.51
  4.7 0.2 fusion.21
  4.9 0.1 mul.63
  5.0 1.4 scatter_custom_fusion
  6.4 0.0 copy-done.6
  6.4 0.1 copy.16
  6.5 0.1 reshape.154
  6.6 1.9 %gather_fusion = s32[256]{0:T(256)S(1)} fusion(s32[256]{0:T(256)S(1)} %reshape.154, s32[1024]{0:T(1024)S(1)} %pad_clamp_fusion), kind=kCustom, calls=%fused_computation | custom fusion | bytes 3072 | tf_op jit(solution)/shard_map/gather | solution.py:148
  8.6 0.1 fusion.23
  8.7 0.0 copy-start.4
  8.7 4.3 %broadcast_and_fusion = pred[256,4,32,4]{3,2,1,0:T(32,128)(4,1)} fusion(pred[4,4]{1,0:T(4,128)(4,1)S(1)} %iota_compare_fusion.2, pred[256,32]{1,0:T(8,128)(4,1)S(1)} %fusion.23), kind=kLoop, calls=%fused_computation.3 | loop fusion | flops 131072 | bytes 139280 | tf_op jit(solution)/shard_map/and | solution.py:142
  13.1 0.0 copy-start.5
  13.1 15.9 %and.69 = pred[1024,128]{1,0:T(32,128)(4,1)S(1)} reshape(pred[256,4,32,4]{3,2,1,0:T(32,128)(4,1)} %broadcast_and_fusion) | data formatting | bytes 262144 | tf_op jit(solution)/shard_map/and | solution.py:142
  29.0 0.0 copy-done.4
  29.0 0.2 reshape.153
  29.1 2.0 %convolution_convert_fusion.1.refs_0_ = bf16[1024,1024]{1,0:T(8,128)(2,1)} fusion(pred[1024,128]{1,0:T(32,128)(4,1)S(1)} %and.69, bf16[128,1024]{1,0:T(8,128)(2,1)S(1)} %reshape.153), kind=kOutput, calls=%fused_computation.19 | convolution fusion | flops 269484032 | bytes 2490368 | tf_op jit(solution)/shard_map/dot_general | solution.py:147
  31.2 0.0 copy-done.5
  31.2 0.2 reshape.155
  31.3 0.1 broadcast_in_dim.36
  31.4 0.1 mul.66
  31.6 2.0 %multiply_convert_fusion.refs_1_ = bf16[1024,1024]{1,0:T(8,128)(2,1)} fusion(pred[1024,128]{1,0:T(32,128)(4,1)S(1)} %and.69, bf16[128,1024]{1,0:T(8,128)(2,1)S(1)} %reshape.155, f32[1024]{0:T(1024)S(1)} %mul.66), kind=kOutput, calls=%fused_computation.18 | convolution fusion | flops 270532608 | bytes 2494464 | tf_op jit(solution)/shard_map/dot_general | solution.py:150
  33.6 63.6 %shard_map.95 = (bf16[1024,1024]{1,0:T(8,128)(2,1)}, bf16[1024,1024]{1,0:T(8,128)(2,1)}) custom-call(bf16[1024,1024]{1,0:T(8,128)(2,1)} %convolution_convert_fusion.1.refs_0_, bf16[1024,1024]{1,0:T(8,128)(2,1)} %multiply_convert_fusion.refs_1_), custom_call_target="tpu_custom_call" | custom-call | tf_op jit(solution)/shard_map/pallas_call | solution.py:75
  97.2 3.1 %reshape.157 = bf16[256,4096]{1,0:T(8,128)(2,1)S(1)} reshape(bf16[1024,1024]{1,0:T(8,128)(2,1)} %get-tuple-element.5) | data formatting | bytes 4194304 | tf_op jit(solution)/shard_map/reshape | solution.py:153
  100.3 0.0 copy-start.2
  100.3 5.3 %fusion.2 = f32[256,768]{1,0:T(8,128)S(1)} fusion(bf16[256,4096]{1,0:T(8,128)(2,1)S(1)} %reshape.157, bf16[1,4096,768]{2,1,0:T(8,128)(2,1)} %param.13), kind=kOutput, calls=%fused_computation.7 | convolution fusion | flops 1610612736 | bytes 9175040 | tf_op jit(solution)/shard_map/dot_general | solution.py:89
  105.7 0.0 copy-done.2
  105.7 3.1 %reshape.156 = bf16[256,4096]{1,0:T(8,128)(2,1)S(1)} reshape(bf16[1024,1024]{1,0:T(8,128)(2,1)} %get-tuple-element.4) | data formatting | bytes 4194304 | tf_op jit(solution)/shard_map/reshape | solution.py:154
  108.8 0.0 copy-start.3
  108.8 0.0 slice-start.2
  108.8 0.0 slice-start
  108.8 4.8 %fusion.8 = f32[256,768]{1,0:T(8,128)S(1)} fusion(bf16[256,4096]{1,0:T(8,128)(2,1)S(1)} %reshape.156, bf16[1,768,4096]{2,1,0:T(8,128)(2,1)} %param.15), kind=kOutput, calls=%fused_computation.13 | convolution fusion | flops 1610612736 | bytes 9175040 | tf_op jit(solution)/shard_map/dot_general | solution.py:98
  113.6 0.0 copy-done.3
  113.6 0.0 slice-start.3
  113.6 0.0 slice-start.1
  113.7 4.7 %fusion.6 = f32[256,768]{1,0:T(8,128)S(1)} fusion(bf16[256,4096]{1,0:T(8,128)(2,1)S(1)} %copy-done.3, bf16[1,4096,768]{2,1,0:T(8,128)(2,1)} %param.14), kind=kOutput, calls=%fused_computation.11 | convolution fusion | flops 1610612736 | bytes 9175040 | tf_op jit(solution)/shard_map/dot_general | solution.py:90
  118.4 0.0 copy-start.1
  118.4 0.9 copy-done.1
  119.3 0.0 slice-done.2
  119.3 0.0 slice-done.3
  119.3 1.9 %fusion = f32[256,4096]{1,0:T(8,128)S(1)} fusion(bf16[1,4096,768]{2,1,0:T(8,128)(2,1)S(1)} %bitcast.51, f32[256,768]{1,0:T(8,128)S(1)} %fusion.2, f32[256,768]{1,0:T(8,128)S(1)} %fusion.8, f32[256,768]{1,0:T(8,128)S(1)} %fusion.6), kind=kOutput, calls=%fused_computation.5 | convolution fusion | flops 1612578816 | bytes 12845056 | tf_op jit(solution)/shard_map/dot_general | solution.py:104
  121.3 0.0 slice-done
  121.3 0.0 slice-done.1
  121.3 3.2 %fusion.14 = bf16[256,4096]{1,0:T(8,128)(2,1)} fusion(f32[256,4096]{1,0:T(8,128)S(1)} %fusion, bf16[1,4096,768]{2,1,0:T(8,128)(2,1)S(1)} %bitcast.49, f32[256,768]{1,0:T(8,128)S(1)} %fusion.8, f32[256,768]{1,0:T(8,128)S(1)} %fusion.2), kind=kOutput, calls=%fused_computation.17 | convolution fusion | flops 1613889536 | bytes 14155776 | tf_op jit(solution)/shard_map/dot_general | solution.py:105
  124.5 4.3 %reshape.158.refs_0_ = bf16[1024,1024]{1,0:T(8,128)(2,1)} reshape(bf16[256,4096]{1,0:T(8,128)(2,1)} %fusion.14) | data formatting | bytes 4194304 | tf_op jit(solution)/shard_map/reshape | solution.py:156
  128.8 34.9 %shard_map.96 = bf16[1024,1024]{1,0:T(8,128)(2,1)} custom-call(bf16[1024,1024]{1,0:T(8,128)(2,1)} %reshape.158.refs_0_), custom_call_target="tpu_custom_call" | custom-call | tf_op jit(solution)/shard_map/pallas_call | solution.py:75
  163.7 2.1 %convolution_convert_fusion.2 = bf16[128,1024]{1,0:T(8,128)(2,1)S(1)} fusion(pred[1024,128]{1,0:T(32,128)(4,1)S(1)} %and.69, bf16[1024,1024]{1,0:T(8,128)(2,1)} %shard_map.96), kind=kOutput, calls=%fused_computation.20 | convolution fusion | flops 268566528 | bytes 2490368 | tf_op jit(solution)/shard_map/dot_general | solution.py:157
  165.8 0.9 convert_element_type.44
  166.7 5.7 %fusion.10 = bf16[1,768,4096]{2,1,0:T(8,128)(2,1)} fusion(bf16[256,4096]{1,0:T(8,128)(2,1)S(1)} %reshape.156, f32[256,768]{1,0:T(8,128)} %copy-done.1, f32[256,768]{1,0:T(8,128)S(1)} %fusion.2), kind=kOutput, calls=%fused_computation.15 | convolution fusion | flops 1614938112 | bytes 9961472 | tf_op jit(solution)/shard_map/dot_general | solution.py:95
  (17 shorter events, 0.2 us)
Async XLA Ops:
  0.6 0.9 copy-start
  1.5 4.9 %copy-start.6 = (s32[32,8]{0,1:T(8,128)S(1)}, s32[32,8]{0,1:T(8,128)}, u32[]{:S(2)}) copy-start(s32[32,8]{0,1:T(8,128)} %param.12) | copy-start | bytes 3076
  8.7 20.2 %copy-start.4 = (bf16[32,4096]{1,0:T(8,128)(2,1)S(1)}, bf16[32,4096]{1,0:T(8,128)(2,1)}, u32[]{:S(2)}) copy-start(bf16[32,4096]{1,0:T(8,128)(2,1)} %param.8) | copy-start | bytes 786436
  13.1 18.1 %copy-start.5 = (bf16[32,4096]{1,0:T(8,128)(2,1)S(1)}, bf16[32,4096]{1,0:T(8,128)(2,1)}, u32[]{:S(2)}) copy-start(bf16[32,4096]{1,0:T(8,128)(2,1)} %param.9) | copy-start | bytes 786436
  100.3 5.4 %copy-start.2 = (bf16[256,4096]{1,0:T(8,128)(2,1)}, bf16[256,4096]{1,0:T(8,128)(2,1)S(1)}, u32[]{:S(2)}) copy-start(bf16[256,4096]{1,0:T(8,128)(2,1)S(1)} %reshape.157) | copy-start | bytes 6291460
  108.8 4.8 %copy-start.3 = (bf16[256,4096]{1,0:T(8,128)(2,1)S(1)}, bf16[256,4096]{1,0:T(8,128)(2,1)}, u32[]{:S(2)}) copy-start(bf16[256,4096]{1,0:T(8,128)(2,1)} %copy-done.2) | copy-start | bytes 6291460
  108.8 10.5 %slice-start.2 = ((s8[6291456]{0:T(1024)(128)(4,1)}), s8[4194304]{0:T(1024)(128)(4,1)S(1)}, s32[]{:S(2)}) async-start(s8[6291456]{0:T(1024)(128)(4,1)} %bitcast.50), calls=%async_computation.2 | async-start | bytes 8388608
  108.8 12.4 %slice-start = ((s8[6291456]{0:T(1024)(128)(4,1)}), s8[4194304]{0:T(1024)(128)(4,1)S(1)}, s32[]{:S(2)}) async-start(s8[6291456]{0:T(1024)(128)(4,1)} %bitcast.48), calls=%async_computation | async-start | bytes 8388608
  113.6 5.7 %slice-start.3 = ((s8[6291456]{0:T(1024)(128)(4,1)}), s8[2097152]{0:T(1024)(128)(4,1)S(1)}, s32[]{:S(2)}) async-start(s8[6291456]{0:T(1024)(128)(4,1)} %bitcast.50), calls=%async_computation.3 | async-start | bytes 4194304
  113.6 7.6 %slice-start.1 = ((s8[6291456]{0:T(1024)(128)(4,1)}), s8[2097152]{0:T(1024)(128)(4,1)S(1)}, s32[]{:S(2)}) async-start(s8[6291456]{0:T(1024)(128)(4,1)} %bitcast.48), calls=%async_computation.1 | async-start | bytes 4194304
  118.4 0.9 copy-start.1

commit v5 on v4

--- a/solution.py
+++ b/solution.py
@@ -137,10 +137,14 @@
     tile_rows = 8
     blocks = tile_rows // capacity
     piece = width // blocks
-    holds = valid[:, None] & (rows[:, None] == jnp.arange(tok_dev, dtype=jnp.int32)[None, :])
-    same_block = jnp.eye(blocks, dtype=jnp.bool_)
-    select = (holds[:, None, :, None] & same_block[None, :, None, :]).reshape(
-        experts * tile_rows, tok_dev * blocks
+    slot_token = jnp.where(valid, rows, -1)
+    row_key = jnp.where(
+        jnp.repeat(valid, blocks),
+        jnp.repeat(slot_token, blocks) * blocks + jnp.arange(experts * tile_rows, dtype=jnp.int32) % blocks,
+        -1,
+    )
+    select = (
+        row_key[:, None] == jnp.arange(tok_dev * blocks, dtype=jnp.int32)[None, :]
     ).astype(jnp.bfloat16)
     tok_pieces = tokens.reshape(tok_dev * blocks, piece)
     og_pieces = out_grad.reshape(tok_dev * blocks, piece)

time: 173 us -> 155 us (0.90)
  local copies, waits for them, and re-layouts: 36 us -> 22.2 us
  other arithmetic: 5.02 us -> 0.55 us
    and x1 -> x0, local copies, waits for them, and re-layouts: 15.9 us -> none  [body(): holds[:, None, :, None] & same_block[None, :, None, :]]
    and x2 -> x0, other arithmetic: 4.48 us -> none  [the longest x1 4.34 us: body(): holds[:, None, :, None] & same_block[None, :, None, :]]
where the time goes in v5:
time: 155 us; the launch traced here: 154 us
  Pallas kernels  98.5 us (64%)
  matrix products  32.2 us (21%)
  local copies, waits for them, and re-layouts  22.2 us (14%)
    pallas_call x2, Pallas kernels, exchange(): pl.pallas_call(functools.partial(_exchange_kernel, n_local), out_shape=[j...  98.5 us
    dot_general x1, matrix products, expert_math(): lax.dot_general(hidden, dy_rows, contract_rows, preferred_element_type=jn...  5.72 us
    dot_general x1, matrix products, expert_math(): gate_act = jnp.dot(x_rows, w_gate_e, preferred_element_type=jnp.float32)  5.35 us
    dot_general x1, matrix products, expert_math(): lax.dot_general(dy_rows, w_down_e, contract_last, preferred_element_type=...  4.77 us
    dot_general x1, matrix products, expert_math(): up_act = jnp.dot(x_rows, w_up_e, preferred_element_type=jnp.float32)  4.74 us
    reshape x1, local copies, waits for them, and re-layouts, body(): returned, = exchange(row_grad.reshape(experts * tile_rows, piece))  4.33 us
    dot_general x1, matrix products, expert_math(): lax.dot_general(up_grad, w_up_e, contract_last, preferred_element_type=jn...  3.19 us
    reshape x1, local copies, waits for them, and re-layouts, body(): x_rows = x_flat.reshape(experts * capacity, width)  3.1 us

profile of v5, /device:TPU:1, one launch (start us, length us, event | category | flops | bytes accessed | tf_op | source)
XLA Modules:
  0.0 154.4 jit_solution(7188367190233329131)
XLA Ops:
  0.6 0.0 copy-start
  0.6 1.1 reshape.120
  1.8 0.8 copy.16
  2.5 0.1 reshape.121
  2.6 0.8 copy.10
  3.4 0.1 reshape.134
  3.5 0.0 copy-done
  3.5 2.4 %gather_fusion.1 = s32[256]{0:T(256)S(1)} fusion(s32[32,4]{0,1:T(4,128)S(1)} %copy-done, s32[256]{0:T(256)S(1)} %reshape.134), kind=kCustom, calls=%fused_computation.1 | custom fusion | bytes 4096 | tf_op jit(solution)/shard_map/jit(take_along_axis)/gather | solution.py:119
  5.9 0.0 copy-start.4
  5.9 0.1 reshape.137
  6.1 0.1 eq.46
  6.2 0.1 copy.14
  6.3 0.2 fusion.23
  6.6 0.1 eq.42
  6.7 0.2 fusion.24
  6.9 0.1 mul.79
  7.0 1.4 scatter_custom_fusion
  8.4 1.9 %gather_fusion = s32[256]{0:T(256)S(1)} fusion(s32[256]{0:T(256)S(1)} %reshape.121, s32[1024]{0:T(1024)S(1)} %pad_clamp_fusion), kind=kCustom, calls=%fused_computation | custom fusion | bytes 3072 | tf_op jit(solution)/shard_map/gather | solution.py:152
  10.4 0.1 broadcast_in_dim.42
  10.5 0.1 reshape.119
  10.6 0.1 broadcast_in_dim.43
  10.7 0.1 mul.82
  10.9 2.1 %convolution_convert_fusion.1.refs_0_ = bf16[1024,1024]{1,0:T(8,128)(2,1)} fusion(bf16[128,1024]{1,0:T(8,128)(2,1)S(1)} %reshape.120, s32[1024]{0:T(1024)S(1)} %fusion.31), kind=kOutput, calls=%fused_computation.18 | convolution fusion | flops 269615104 | bytes 2363392 | tf_op jit(solution)/shard_map/dot_general | solution.py:151
  12.9 0.0 copy-done.4
  12.9 0.2 reshape.122
  13.1 0.1 broadcast_in_dim.47
  13.2 0.1 mul.86
  13.3 2.1 %multiply_convert_fusion.refs_1_ = bf16[1024,1024]{1,0:T(8,128)(2,1)} fusion(bf16[128,1024]{1,0:T(8,128)(2,1)S(1)} %reshape.122, f32[1024]{0:T(1024)S(1)} %mul.86, s32[1024]{0:T(1024)S(1)} %fusion.31), kind=kOutput, calls=%fused_computation.17 | convolution fusion | flops 270663680 | bytes 2367488 | tf_op jit(solution)/shard_map/dot_general | solution.py:154
  15.4 63.6 %shard_map.95 = (bf16[1024,1024]{1,0:T(8,128)(2,1)}, bf16[1024,1024]{1,0:T(8,128)(2,1)}) custom-call(bf16[1024,1024]{1,0:T(8,128)(2,1)} %convolution_convert_fusion.1.refs_0_, bf16[1024,1024]{1,0:T(8,128)(2,1)} %multiply_convert_fusion.refs_1_), custom_call_target="tpu_custom_call" | custom-call | tf_op jit(solution)/shard_map/pallas_call | solution.py:75
  79.0 3.1 %reshape.124 = bf16[256,4096]{1,0:T(8,128)(2,1)S(1)} reshape(bf16[1024,1024]{1,0:T(8,128)(2,1)} %get-tuple-element.5) | data formatting | bytes 4194304 | tf_op jit(solution)/shard_map/reshape | solution.py:157
  82.1 0.0 copy-start.2
  82.1 5.3 %fusion.2 = f32[256,768]{1,0:T(8,128)S(1)} fusion(bf16[256,4096]{1,0:T(8,128)(2,1)S(1)} %reshape.124, bf16[1,4096,768]{2,1,0:T(8,128)(2,1)} %param.13), kind=kOutput, calls=%fused_computation.6 | convolution fusion | flops 1610612736 | bytes 9175040 | tf_op jit(solution)/shard_map/dot_general | solution.py:89
  87.5 0.0 copy-done.2
  87.5 3.1 %reshape.123 = bf16[256,4096]{1,0:T(8,128)(2,1)S(1)} reshape(bf16[1024,1024]{1,0:T(8,128)(2,1)} %get-tuple-element.4) | data formatting | bytes 4194304 | tf_op jit(solution)/shard_map/reshape | solution.py:158
  90.6 0.0 copy-start.3
  90.6 0.0 slice-start.2
  90.6 0.0 slice-start
  90.7 4.8 %fusion.8 = f32[256,768]{1,0:T(8,128)S(1)} fusion(bf16[256,4096]{1,0:T(8,128)(2,1)S(1)} %reshape.123, bf16[1,768,4096]{2,1,0:T(8,128)(2,1)} %param.15), kind=kOutput, calls=%fused_computation.12 | convolution fusion | flops 1610612736 | bytes 9175040 | tf_op jit(solution)/shard_map/dot_general | solution.py:98
  95.4 0.0 copy-done.3
  95.4 0.0 slice-start.3
  95.5 0.0 slice-start.1
  95.5 4.7 %fusion.6 = f32[256,768]{1,0:T(8,128)S(1)} fusion(bf16[256,4096]{1,0:T(8,128)(2,1)S(1)} %copy-done.3, bf16[1,4096,768]{2,1,0:T(8,128)(2,1)} %param.14), kind=kOutput, calls=%fused_computation.10 | convolution fusion | flops 1610612736 | bytes 9175040 | tf_op jit(solution)/shard_map/dot_general | solution.py:90
  100.2 0.0 copy-start.1
  100.2 0.9 copy-done.1
  101.1 0.0 slice-done.2
  101.1 0.0 slice-done.3
  101.1 1.9 %fusion = f32[256,4096]{1,0:T(8,128)S(1)} fusion(bf16[1,4096,768]{2,1,0:T(8,128)(2,1)S(1)} %bitcast.46, f32[256,768]{1,0:T(8,128)S(1)} %fusion.2, f32[256,768]{1,0:T(8,128)S(1)} %fusion.8, f32[256,768]{1,0:T(8,128)S(1)} %fusion.6), kind=kOutput, calls=%fused_computation.4 | convolution fusion | flops 1612578816 | bytes 12845056 | tf_op jit(solution)/shard_map/dot_general | solution.py:104
  103.1 0.0 slice-done
  103.1 0.0 slice-done.1
  103.1 3.2 %fusion.14 = bf16[256,4096]{1,0:T(8,128)(2,1)} fusion(f32[256,4096]{1,0:T(8,128)S(1)} %fusion, bf16[1,4096,768]{2,1,0:T(8,128)(2,1)S(1)} %bitcast.44, f32[256,768]{1,0:T(8,128)S(1)} %fusion.8, f32[256,768]{1,0:T(8,128)S(1)} %fusion.2), kind=kOutput, calls=%fused_computation.16 | convolution fusion | flops 1613889536 | bytes 14155776 | tf_op jit(solution)/shard_map/dot_general | solution.py:105
  106.3 4.3 %reshape.125.refs_0_ = bf16[1024,1024]{1,0:T(8,128)(2,1)} reshape(bf16[256,4096]{1,0:T(8,128)(2,1)} %fusion.14) | data formatting | bytes 4194304 | tf_op jit(solution)/shard_map/reshape | solution.py:160
  110.6 34.9 %shard_map.96 = bf16[1024,1024]{1,0:T(8,128)(2,1)} custom-call(bf16[1024,1024]{1,0:T(8,128)(2,1)} %reshape.125.refs_0_), custom_call_target="tpu_custom_call" | custom-call | tf_op jit(solution)/shard_map/pallas_call | solution.py:75
  145.5 2.3 %convolution_convert_fusion.2 = bf16[128,1024]{1,0:T(8,128)(2,1)S(1)} fusion(bf16[1024,1024]{1,0:T(8,128)(2,1)} %shard_map.96, s32[1024]{0:T(1024)S(1)} %fusion.31), kind=kOutput, calls=%fused_computation.19 | convolution fusion | flops 268697600 | bytes 2363392 | tf_op jit(solution)/shard_map/dot_general | solution.py:161
  147.8 0.9 convert_element_type.44
  148.6 5.7 %fusion.10 = bf16[1,768,4096]{2,1,0:T(8,128)(2,1)} fusion(bf16[256,4096]{1,0:T(8,128)(2,1)S(1)} %reshape.123, f32[256,768]{1,0:T(8,128)} %copy-done.1, f32[256,768]{1,0:T(8,128)S(1)} %fusion.2), kind=kOutput, calls=%fused_computation.14 | convolution fusion | flops 1614938112 | bytes 9961472 | tf_op jit(solution)/shard_map/dot_general | solution.py:95
  (18 shorter events, 0.2 us)
Async XLA Ops:
  0.6 2.9 %copy-start = (s32[32,4]{0,1:T(4,128)S(1)}, s32[32,4]{0,1:T(4,128)}, u32[]{:S(2)}) copy-start(s32[32,4]{0,1:T(4,128)} %param.10) | copy-start | bytes 1540
  5.9 7.0 %copy-start.4 = (bf16[32,4096]{1,0:T(8,128)(2,1)S(1)}, bf16[32,4096]{1,0:T(8,128)(2,1)}, u32[]{:S(2)}) copy-start(bf16[32,4096]{1,0:T(8,128)(2,1)} %param.9) | copy-start | bytes 786436
  82.1 5.4 %copy-start.2 = (bf16[256,4096]{1,0:T(8,128)(2,1)}, bf16[256,4096]{1,0:T(8,128)(2,1)S(1)}, u32[]{:S(2)}) copy-start(bf16[256,4096]{1,0:T(8,128)(2,1)S(1)} %reshape.124) | copy-start | bytes 6291460
  90.6 4.8 %copy-start.3 = (bf16[256,4096]{1,0:T(8,128)(2,1)S(1)}, bf16[256,4096]{1,0:T(8,128)(2,1)}, u32[]{:S(2)}) copy-start(bf16[256,4096]{1,0:T(8,128)(2,1)} %copy-done.2) | copy-start | bytes 6291460
  90.6 10.5 %slice-start.2 = ((s8[6291456]{0:T(1024)(128)(4,1)}), s8[4194304]{0:T(1024)(128)(4,1)S(1)}, s32[]{:S(2)}) async-start(s8[6291456]{0:T(1024)(128)(4,1)} %bitcast.45), calls=%async_computation.2 | async-start | bytes 8388608
  90.6 12.4 %slice-start = ((s8[6291456]{0:T(1024)(128)(4,1)}), s8[4194304]{0:T(1024)(128)(4,1)S(1)}, s32[]{:S(2)}) async-start(s8[6291456]{0:T(1024)(128)(4,1)} %bitcast.43), calls=%async_computation | async-start | bytes 8388608
  95.4 5.7 %slice-start.3 = ((s8[6291456]{0:T(1024)(128)(4,1)}), s8[2097152]{0:T(1024)(128)(4,1)S(1)}, s32[]{:S(2)}) async-start(s8[6291456]{0:T(1024)(128)(4,1)} %bitcast.45), calls=%async_computation.3 | async-start | bytes 4194304
  95.5 7.6 %slice-start.1 = ((s8[6291456]{0:T(1024)(128)(4,1)}), s8[2097152]{0:T(1024)(128)(4,1)S(1)}, s32[]{:S(2)}) async-start(s8[6291456]{0:T(1024)(128)(4,1)} %bitcast.43), calls=%async_computation.1 | async-start | bytes 4194304
  100.2 0.9 copy-start.1

commit v6 on v5

--- a/solution.py
+++ b/solution.py
@@ -146,16 +146,28 @@
     select = (
         row_key[:, None] == jnp.arange(tok_dev * blocks, dtype=jnp.int32)[None, :]
     ).astype(jnp.bfloat16)
-    tok_pieces = tokens.reshape(tok_dev * blocks, piece)
-    og_pieces = out_grad.reshape(tok_dev * blocks, piece)
-    send_x = jnp.dot(select, tok_pieces, preferred_element_type=jnp.float32).astype(jnp.bfloat16)
+    n_sel = tok_dev * blocks
+    sources = jnp.concatenate(
+        [tokens.reshape(n_sel, piece), out_grad.reshape(n_sel, piece)], axis=0
+    )
+    select2 = jnp.concatenate(
+        [
+            jnp.concatenate([select.reshape(experts, tile_rows, n_sel), jnp.zeros((experts, tile_rows, n_sel), jnp.bfloat16)], axis=2),
+            jnp.concatenate([jnp.zeros((experts, tile_rows, n_sel), jnp.bfloat16), select.reshape(experts, tile_rows, n_sel)], axis=2),
+        ],
+        axis=1,
+    ).reshape(experts * 2 * tile_rows, 2 * n_sel)
     gate_val = jnp.where(valid, gate_flat[safe].astype(jnp.float32) * (1.0 / 65536.0), 0.0)
-    gate_rows = jnp.repeat(gate_val, blocks)
-    og_sel = jnp.dot(select, og_pieces, preferred_element_type=jnp.float32)
-    send_dy = (gate_rows[:, None] * og_sel).astype(jnp.bfloat16)
-    x_flat, dy_flat = exchange(send_x, send_dy)
-    x_rows = x_flat.reshape(experts * capacity, width)
-    dy_rows = dy_flat.reshape(experts * capacity, width)
+    scale = jnp.concatenate(
+        [jnp.ones((experts, tile_rows), jnp.float32), jnp.repeat(gate_val, blocks).reshape(experts, tile_rows)],
+        axis=1,
+    ).reshape(-1)
+    picked = jnp.dot(select2, sources, preferred_element_type=jnp.float32)
+    send_both = (scale[:, None] * picked).astype(jnp.bfloat16)
+    (recv_both,) = exchange(send_both)
+    recv_both = recv_both.reshape(experts, 2 * tile_rows, piece)
+    x_rows = recv_both[:, :tile_rows].reshape(experts * capacity, width)
+    dy_rows = recv_both[:, tile_rows:].reshape(experts * capacity, width)
     down_local, row_grad = expert_math(x_rows, dy_rows, w_gate_e, w_up_e, w_down_e)
     (returned,) = exchange(row_grad.reshape(experts * tile_rows, piece))
     total = jnp.dot(select.T, returned, preferred_element_type=jnp.float32)

time: 155 us -> 157 us (1.013)
  local copies, waits for them, and re-layouts: 22.2 us -> 25.5 us
    slice x0 -> x1, local copies, waits for them, and re-layouts: none -> 3.98 us  [body(): dy_rows = recv_both[:, tile_rows:].reshape(experts * capacity, width)]
    dot_general x2 -> x1, matrix products: 4.18 us -> 3.28 us  [body(): picked = jnp.dot(select2, sources, preferred_element_type=jnp.float32)]
where the time goes in v6:
time: 157 us
  Pallas kernels  98.4 us (63%)
  matrix products  31.1 us (20%)
  local copies, waits for them, and re-layouts  25.5 us (16%)
    pallas_call x2, Pallas kernels, exchange(): pl.pallas_call(functools.partial(_exchange_kernel, n_local), out_shape=[j...  98.4 us
    dot_general x1, matrix products, expert_math(): lax.dot_general(hidden, dy_rows, contract_rows, preferred_element_type=jn...  5.72 us
    dot_general x1, matrix products, expert_math(): gate_act = jnp.dot(x_rows, w_gate_e, preferred_element_type=jnp.float32)  5.2 us
    dot_general x1, matrix products, expert_math(): lax.dot_general(dy_rows, w_down_e, contract_last, preferred_element_type=...  4.76 us
    dot_general x1, matrix products, expert_math(): up_act = jnp.dot(x_rows, w_up_e, preferred_element_type=jnp.float32)  4.74 us
    reshape x1, local copies, waits for them, and re-layouts, body(): returned, = exchange(row_grad.reshape(experts * tile_rows, piece))  4.33 us
    slice x1, local copies, waits for them, and re-layouts, body(): dy_rows = recv_both[:, tile_rows:].reshape(experts * capacity, width)  3.98 us
    dot_general x1, matrix products, body(): picked = jnp.dot(select2, sources, preferred_element_type=jnp.float32)  3.28 us

profile of v6, /device:TPU:1, one launch (start us, length us, event | category | flops | bytes accessed | tf_op | source)
XLA Modules:
  0.0 157.0 jit_solution(1232858808913881112)
XLA Ops:
  0.6 0.0 copy-start
  0.6 0.8 copy.16
  1.4 0.1 reshape.149
  1.5 0.8 copy.10
  2.3 0.1 reshape.165
  2.4 0.0 copy-done
  2.4 2.4 %gather_fusion.1 = s32[256]{0:T(256)S(1)} fusion(s32[32,4]{0,1:T(4,128)S(1)} %copy-done, s32[256]{0:T(256)S(1)} %reshape.165), kind=kCustom, calls=%fused_computation.1 | custom fusion | bytes 4096 | tf_op jit(solution)/shard_map/jit(take_along_axis)/gather | solution.py:119
  4.8 0.0 copy-start.3
  4.8 0.0 copy-start.4
  4.8 0.1 reshape.168
  5.0 0.1 eq.53
  5.0 0.1 copy.14
  5.2 0.2 fusion.28
  5.5 0.1 eq.49
  5.6 0.2 fusion.29
  5.8 0.1 mul.89
  5.9 1.4 scatter_custom_fusion
  7.3 1.9 %gather_fusion = s32[256]{0:T(256)S(1)} fusion(s32[256]{0:T(256)S(1)} %reshape.149, s32[1024]{0:T(1024)S(1)} %pad_clamp_fusion), kind=kCustom, calls=%fused_computation | custom fusion | bytes 3072 | tf_op jit(solution)/shard_map/gather | solution.py:160
  9.3 0.2 broadcast_in_dim.65
  9.4 0.1 copy.19
  9.5 0.1 mul.98
  9.7 0.1 copy.20
  9.8 0.1 copy.21
  9.9 0.2 fusion.23
  10.1 0.1 fusion.19
  10.2 0.1 broadcast_in_dim.62
  10.4 0.1 copy.17
  10.4 0.1 copy.22
  10.6 0.1 concatenate.15.clone
  10.6 0.1 mul.96
  10.7 0.0 copy-done.3
  10.7 0.2 reshape.152
  10.9 0.0 copy-done.4
  10.9 0.2 reshape.151
  11.1 3.3 %multiply_convert_fusion.refs_0_ = bf16[2048,1024]{1,0:T(8,128)(2,1)} fusion(bf16[2048,256]{1,0:T(8,128)(2,1)S(1)} %bitcast.52, f32[2048]{0:T(1024)S(1)} %mul.96, bf16[128,1024]{1,0:T(8,128)(2,1)S(1)} %reshape.152, bf16[128,1024]{1,0:T(8,128)(2,1)S(1)} %reshape.151), kind=kOutput, calls=%fused_computation.3 | convolution fusion | flops 1078984704 | bytes 5775360 | tf_op jit(solution)/shard_map/dot_general | solution.py:165
  14.4 63.6 %shard_map.95 = bf16[2048,1024]{1,0:T(8,128)(2,1)} custom-call(bf16[2048,1024]{1,0:T(8,128)(2,1)} %multiply_convert_fusion.refs_0_), custom_call_target="tpu_custom_call" | custom-call | tf_op jit(solution)/shard_map/pallas_call | solution.py:75
  78.0 4.0 %fusion.54 = (bf16[128,8,1024]{2,1,0:T(8,128)(2,1)}, bf16[128,8,1024]{2,1,0:T(8,128)(2,1)S(1)}) fusion(bf16[128,16,1024]{2,1,0:T(8,128)(2,1)} %bitcast.47), kind=kLoop, calls=%fused_computation.89 | loop fusion | bytes 8388608 | tf_op jit(solution)/shard_map/slice | solution.py:170
  81.9 2.5 %reshape.155 = bf16[256,4096]{1,0:T(8,128)(2,1)} reshape(bf16[128,8,1024]{2,1,0:T(8,128)(2,1)S(1)} %get-tuple-element.7) | data formatting | bytes 4194304 | tf_op jit(solution)/shard_map/reshape | solution.py:169
  84.5 5.2 %fusion.2 = f32[256,768]{1,0:T(8,128)S(1)} fusion(bf16[256,4096]{1,0:T(8,128)(2,1)} %reshape.155, bf16[1,4096,768]{2,1,0:T(8,128)(2,1)} %param.13), kind=kOutput, calls=%fused_computation.7 | convolution fusion | flops 1610612736 | bytes 9175040 | tf_op jit(solution)/shard_map/dot_general | solution.py:89
  89.7 3.1 %reshape.154 = bf16[256,4096]{1,0:T(8,128)(2,1)S(1)} reshape(bf16[128,8,1024]{2,1,0:T(8,128)(2,1)} %get-tuple-element.6) | data formatting | bytes 4194304 | tf_op jit(solution)/shard_map/reshape | solution.py:170
  92.8 0.0 copy-start.2
  92.8 0.0 slice-start.2
  92.8 0.0 slice-start
  92.8 4.8 %fusion.8 = f32[256,768]{1,0:T(8,128)S(1)} fusion(bf16[256,4096]{1,0:T(8,128)(2,1)S(1)} %reshape.154, bf16[1,768,4096]{2,1,0:T(8,128)(2,1)} %param.15), kind=kOutput, calls=%fused_computation.13 | convolution fusion | flops 1610612736 | bytes 9175040 | tf_op jit(solution)/shard_map/dot_general | solution.py:98
  97.6 0.0 copy-done.2
  97.6 0.0 slice-start.3
  97.6 0.0 slice-start.1
  97.6 4.7 %fusion.6 = f32[256,768]{1,0:T(8,128)S(1)} fusion(bf16[256,4096]{1,0:T(8,128)(2,1)S(1)} %copy-done.2, bf16[1,4096,768]{2,1,0:T(8,128)(2,1)} %param.14), kind=kOutput, calls=%fused_computation.11 | convolution fusion | flops 1610612736 | bytes 9175040 | tf_op jit(solution)/shard_map/dot_general | solution.py:90
  102.4 0.0 copy-start.1
  102.4 0.9 copy-done.1
  103.3 0.0 slice-done.2
  103.3 0.0 slice-done.3
  103.3 1.9 %fusion = f32[256,4096]{1,0:T(8,128)S(1)} fusion(bf16[1,4096,768]{2,1,0:T(8,128)(2,1)S(1)} %bitcast.51, f32[256,768]{1,0:T(8,128)S(1)} %fusion.2, f32[256,768]{1,0:T(8,128)S(1)} %fusion.8, f32[256,768]{1,0:T(8,128)S(1)} %fusion.6), kind=kOutput, calls=%fused_computation.5 | convolution fusion | flops 1612578816 | bytes 12845056 | tf_op jit(solution)/shard_map/dot_general | solution.py:104
  105.2 0.0 slice-done
  105.3 3.2 %fusion.14 = bf16[256,4096]{1,0:T(8,128)(2,1)} fusion(f32[256,4096]{1,0:T(8,128)S(1)} %fusion, bf16[1,4096,768]{2,1,0:T(8,128)(2,1)S(1)} %bitcast.49, f32[256,768]{1,0:T(8,128)S(1)} %fusion.8, f32[256,768]{1,0:T(8,128)S(1)} %fusion.2), kind=kOutput, calls=%fused_computation.17 | convolution fusion | flops 1613889536 | bytes 14155776 | tf_op jit(solution)/shard_map/dot_general | solution.py:105
  108.5 4.3 %reshape.156.refs_0_ = bf16[1024,1024]{1,0:T(8,128)(2,1)} reshape(bf16[256,4096]{1,0:T(8,128)(2,1)} %fusion.14) | data formatting | bytes 4194304 | tf_op jit(solution)/shard_map/reshape | solution.py:172
  112.8 34.9 %shard_map.96 = bf16[1024,1024]{1,0:T(8,128)(2,1)} custom-call(bf16[1024,1024]{1,0:T(8,128)(2,1)} %reshape.156.refs_0_), custom_call_target="tpu_custom_call" | custom-call | tf_op jit(solution)/shard_map/pallas_call | solution.py:75
  147.7 0.1 broadcast_in_dim.57
  147.8 0.1 reshape.148
  147.9 0.1 broadcast_in_dim.58
  148.0 0.1 mul.92
  148.1 2.3 %convolution_convert_fusion.1 = bf16[128,1024]{1,0:T(8,128)(2,1)S(1)} fusion(bf16[1024,1024]{1,0:T(8,128)(2,1)} %shard_map.96, s32[1024]{0:T(1024)S(1)} %fusion.36), kind=kOutput, calls=%fused_computation.22 | convolution fusion | flops 268697600 | bytes 2363392 | tf_op jit(solution)/shard_map/dot_general | solution.py:173
  150.4 0.9 convert_element_type.44
  151.3 5.7 %fusion.10 = bf16[1,768,4096]{2,1,0:T(8,128)(2,1)} fusion(bf16[256,4096]{1,0:T(8,128)(2,1)S(1)} %reshape.154, f32[256,768]{1,0:T(8,128)} %copy-done.1, f32[256,768]{1,0:T(8,128)S(1)} %fusion.2), kind=kOutput, calls=%fused_computation.15 | convolution fusion | flops 1614938112 | bytes 9961472 | tf_op jit(solution)/shard_map/dot_general | solution.py:95
  (23 shorter events, 0.2 us)
Async XLA Ops:
  0.6 1.8 %copy-start = (s32[32,4]{0,1:T(4,128)S(1)}, s32[32,4]{0,1:T(4,128)}, u32[]{:S(2)}) copy-start(s32[32,4]{0,1:T(4,128)} %param.10) | copy-start | bytes 1540
  4.8 5.9 %copy-start.3 = (bf16[32,4096]{1,0:T(8,128)(2,1)S(1)}, bf16[32,4096]{1,0:T(8,128)(2,1)}, u32[]{:S(2)}) copy-start(bf16[32,4096]{1,0:T(8,128)(2,1)} %param.9) | copy-start | bytes 786436
  4.8 6.1 %copy-start.4 = (bf16[32,4096]{1,0:T(8,128)(2,1)S(1)}, bf16[32,4096]{1,0:T(8,128)(2,1)}, u32[]{:S(2)}) copy-start(bf16[32,4096]{1,0:T(8,128)(2,1)} %param.8) | copy-start | bytes 786436
  92.8 4.8 %copy-start.2 = (bf16[256,4096]{1,0:T(8,128)(2,1)S(1)}, bf16[256,4096]{1,0:T(8,128)(2,1)}, u32[]{:S(2)}) copy-start(bf16[256,4096]{1,0:T(8,128)(2,1)} %reshape.155) | copy-start | bytes 6291460
  92.8 10.5 %slice-start.2 = ((s8[6291456]{0:T(1024)(128)(4,1)}), s8[4194304]{0:T(1024)(128)(4,1)S(1)}, s32[]{:S(2)}) async-start(s8[6291456]{0:T(1024)(128)(4,1)} %bitcast.50), calls=%async_computation.2 | async-start | bytes 8388608
  92.8 12.4 %slice-start = ((s8[6291456]{0:T(1024)(128)(4,1)}), s8[4194304]{0:T(1024)(128)(4,1)S(1)}, s32[]{:S(2)}) async-start(s8[6291456]{0:T(1024)(128)(4,1)} %bitcast.48), calls=%async_computation | async-start | bytes 8388608
  97.6 5.7 %slice-start.3 = ((s8[6291456]{0:T(1024)(128)(4,1)}), s8[2097152]{0:T(1024)(128)(4,1)S(1)}, s32[]{:S(2)}) async-start(s8[6291456]{0:T(1024)(128)(4,1)} %bitcast.50), calls=%async_computation.3 | async-start | bytes 4194304
  97.6 7.6 %slice-start.1 = ((s8[6291456]{0:T(1024)(128)(4,1)}), s8[2097152]{0:T(1024)(128)(4,1)S(1)}, s32[]{:S(2)}) async-start(s8[6291456]{0:T(1024)(128)(4,1)} %bitcast.48), calls=%async_computation.1 | async-start | bytes 4194304
  102.4 0.9 copy-start.1

commit v7 on v5

--- a/solution.py
+++ b/solution.py
@@ -7,12 +7,16 @@
 from jax.experimental.pallas import tpu as pltpu
 
 
-def _exchange_kernel(n_local, *refs):
-    count = (len(refs) - 2) // 2
+def _exchange_kernel(n_local, count, n_work_in, n_work_out, work, *refs):
     srcs = refs[:count]
-    dsts = refs[count:2 * count]
-    send_sems = refs[2 * count]
-    recv_sems = refs[2 * count + 1]
+    work_in = refs[count:count + n_work_in]
+    base = count + n_work_in
+    dsts = refs[base:base + count]
+    work_out = refs[base + count:base + count + n_work_out]
+    base = base + count + n_work_out
+    send_sems = refs[base]
+    recv_sems = refs[base + 1]
+    work_scratch = refs[base + 2:]
     node = lax.axis_index("node")
     local = lax.axis_index("local")
     me = node * n_local + local
@@ -56,6 +60,8 @@
         return carry
 
     lax.fori_loop(1, devices, start_body, 0)
+    if work is not None:
+        work(*work_in, *work_out, *work_scratch)
     nxt = lax.rem(me + 1, devices)
     for i in range(count):
         pltpu.make_async_copy(dsts[i], dsts[i], recv_sems.at[i]).wait()
@@ -69,25 +75,47 @@
         ).wait_send()
 
 
-def exchange(*arrays):
+def exchange(arrays, work=None, work_in=(), work_in_specs=(), work_out=(), work_out_specs=(),
+             work_scratch=()):
     n_local = lax.axis_size("local")
     count = len(arrays)
     return pl.pallas_call(
-        functools.partial(_exchange_kernel, n_local),
-        out_shape=[jax.ShapeDtypeStruct(a.shape, a.dtype) for a in arrays],
-        in_specs=[pl.BlockSpec(memory_space=pl.ANY)] * count,
-        out_specs=[pl.BlockSpec(memory_space=pl.ANY)] * count,
+        functools.partial(_exchange_kernel, n_local, count, len(work_in), len(work_out), work),
+        out_shape=[jax.ShapeDtypeStruct(a.shape, a.dtype) for a in arrays] + list(work_out),
+        in_specs=[pl.BlockSpec(memory_space=pl.ANY)] * count + list(work_in_specs),
+        out_specs=[pl.BlockSpec(memory_space=pl.ANY)] * count + list(work_out_specs),
         scratch_shapes=[
             pltpu.SemaphoreType.DMA((count,)),
             pltpu.SemaphoreType.DMA((count,)),
-        ],
+        ] + list(work_scratch),
         compiler_params=pltpu.CompilerParams(has_side_effects=True),
-    )(*arrays)
-
-
-def expert_math(x_rows, dy_rows, w_gate_e, w_up_e, w_down_e):
-    gate_act = jnp.dot(x_rows, w_gate_e, preferred_element_type=jnp.float32)
-    up_act = jnp.dot(x_rows, w_up_e, preferred_element_type=jnp.float32)
+    )(*arrays, *work_in)
+
+
+def _gate_up_work(x_ref, wg_hbm, wu_hbm, gate_out, up_out, wbuf, wsem):
+    k_total = x_ref.shape[1]
+    k_step = 512
+    copies = [
+        pltpu.make_async_copy(w, wbuf.at[i], wsem.at[i]) for i, w in enumerate((wg_hbm, wu_hbm))
+    ]
+    for c in copies:
+        c.start()
+    for i, out in enumerate((gate_out, up_out)):
+        copies[i].wait()
+        out[...] = jnp.zeros(out.shape, out.dtype)
+
+        def step(k, carry, i=i, out=out):
+            kk = pl.multiple_of(k * k_step, k_step)
+            out[...] += jnp.dot(
+                x_ref[:, pl.ds(kk, k_step)], wbuf[i, pl.ds(kk, k_step), :],
+                preferred_element_type=jnp.float32,
+            )
+            return carry
+
+        lax.fori_loop(0, k_total // k_step, step, 0)
+
+
+def expert_rest(gate_act, up_act, dy_rows, w_gate_e, w_up_e, w_down_e):
     sig = jax.nn.sigmoid(gate_act)
     hidden = (gate_act * sig * up_act).astype(jnp.bfloat16)
     contract_rows = (((0,), (0,)), ((), ()))
@@ -153,11 +181,32 @@
     gate_rows = jnp.repeat(gate_val, blocks)
     og_sel = jnp.dot(select, og_pieces, preferred_element_type=jnp.float32)
     send_dy = (gate_rows[:, None] * og_sel).astype(jnp.bfloat16)
-    x_flat, dy_flat = exchange(send_x, send_dy)
+    (x_flat,) = exchange([send_x])
     x_rows = x_flat.reshape(experts * capacity, width)
+    hid = w_gate_e.shape[1]
+    n_rows = experts * capacity
+    dy_flat, gate_act, up_act = exchange(
+        [send_dy],
+        work=_gate_up_work,
+        work_in=(x_rows, w_gate_e, w_up_e),
+        work_in_specs=(
+            pl.BlockSpec(memory_space=pltpu.VMEM),
+            pl.BlockSpec(memory_space=pl.ANY),
+            pl.BlockSpec(memory_space=pl.ANY),
+        ),
+        work_out=(
+            jax.ShapeDtypeStruct((n_rows, hid), jnp.float32),
+            jax.ShapeDtypeStruct((n_rows, hid), jnp.float32),
+        ),
+        work_out_specs=(pl.BlockSpec(memory_space=pltpu.VMEM),) * 2,
+        work_scratch=(
+            pltpu.VMEM((2,) + w_gate_e.shape, w_gate_e.dtype),
+            pltpu.SemaphoreType.DMA((2,)),
+        ),
+    )
     dy_rows = dy_flat.reshape(experts * capacity, width)
-    down_local, row_grad = expert_math(x_rows, dy_rows, w_gate_e, w_up_e, w_down_e)
-    (returned,) = exchange(row_grad.reshape(experts * tile_rows, piece))
+    down_local, row_grad = expert_rest(gate_act, up_act, dy_rows, w_gate_e, w_up_e, w_down_e)
+    (returned,) = exchange([row_grad.reshape(experts * tile_rows, piece)])
     total = jnp.dot(select.T, returned, preferred_element_type=jnp.float32)
     token_grad = total.reshape(tok_dev, width).astype(jnp.bfloat16)
     return (token_grad, down_local[None])

time: 155 us -> 161 us (1.039)
  Pallas kernels: 98.5 us -> 112 us
  matrix products: 32.2 us -> 25 us
    pallas_call x2 -> x3, Pallas kernels: 98.5 us -> 112 us  [exchange(): pl.pallas_call(functools.partial(_exchange_kernel, n_local, count, len(wo...]
    dot_general x6 -> x4, matrix products: 25.7 us -> 18.6 us  [the longest x1 5.72 us: expert_rest(): lax.dot_general(hidden, dy_rows, contract_rows, preferred_element_type=jn...]
where the time goes in v7:
time: 161 us
  Pallas kernels  112 us (70%)
  matrix products  25 us (16%)
  local copies, waits for them, and re-layouts  21.9 us (14%)
    pallas_call x3, Pallas kernels, exchange(): pl.pallas_call(functools.partial(_exchange_kernel, n_local, count, len(wo...  112 us
    dot_general x1, matrix products, expert_rest(): lax.dot_general(hidden, dy_rows, contract_rows, preferred_element_type=jn...  5.72 us
    dot_general x1, matrix products, expert_rest(): lax.dot_general(gate_grad, w_gate_e, contract_last, preferred_element_typ...  4.89 us
    dot_general x1, matrix products, expert_rest(): lax.dot_general(dy_rows, w_down_e, contract_last, preferred_element_type=...  4.76 us
    reshape x1, local copies, waits for them, and re-layouts, body(): x_rows = x_flat.reshape(experts * capacity, width)  4.33 us
    reshape x1, local copies, waits for them, and re-layouts, body(): returned, = exchange([row_grad.reshape(experts * tile_rows, piece)])  4.33 us

profile of v7, /device:TPU:1, one launch (start us, length us, event | category | flops | bytes accessed | tf_op | source)
XLA Modules:
  0.0 160.7 jit_solution(8167042133960778347)
XLA Ops:
  0.6 0.0 copy-start
  0.6 1.1 reshape.121
  1.8 0.8 copy.10
  2.6 0.1 reshape.134
  2.6 0.0 copy-done
  2.7 0.0 copy-start.4
  2.7 2.4 %gather_fusion.1 = s32[256]{0:T(256)S(1)} fusion(s32[32,4]{0,1:T(4,128)S(1)} %copy-done, s32[256]{0:T(256)S(1)} %reshape.134), kind=kCustom, calls=%fused_computation.1 | custom fusion | bytes 4096 | tf_op jit(solution)/shard_map/jit(take_along_axis)/gather | solution.py:147
  5.1 0.0 copy-start.3
  5.1 0.1 reshape.137
  5.2 0.1 eq.46
  5.3 0.1 copy.14
  5.4 0.2 fusion.11
  5.7 0.1 eq.42
  5.8 0.2 fusion.12
  6.0 0.1 mul.79
  6.1 1.4 scatter_custom_fusion
  7.6 0.0 copy-done.4
  7.6 0.1 copy.16
  7.6 0.1 reshape.120
  7.7 1.9 %gather_fusion = s32[256]{0:T(256)S(1)} fusion(s32[256]{0:T(256)S(1)} %reshape.120, s32[1024]{0:T(1024)S(1)} %pad_clamp_fusion), kind=kCustom, calls=%fused_computation | custom fusion | bytes 3072 | tf_op jit(solution)/shard_map/gather | solution.py:180
  9.7 0.1 broadcast_in_dim.47
  9.8 0.1 mul.86
  9.9 0.1 broadcast_in_dim.42
  10.0 0.1 reshape.119
  10.2 0.1 broadcast_in_dim.43
  10.3 0.1 mul.82
  10.4 2.1 %multiply_convert_fusion.refs_0_ = bf16[1024,1024]{1,0:T(8,128)(2,1)} fusion(bf16[128,1024]{1,0:T(8,128)(2,1)S(1)} %reshape.121, f32[1024]{0:T(1024)S(1)} %mul.86, s32[1024]{0:T(1024)S(1)} %fusion.19), kind=kOutput, calls=%fused_computation.9 | convolution fusion | flops 270663680 | bytes 2367488 | tf_op jit(solution)/shard_map/dot_general | solution.py:182
  12.5 0.0 copy-done.3
  12.5 0.2 reshape.122
  12.7 2.1 %convolution_convert_fusion.1.refs_0_ = bf16[1024,1024]{1,0:T(8,128)(2,1)} fusion(bf16[128,1024]{1,0:T(8,128)(2,1)S(1)} %reshape.122, s32[1024]{0:T(1024)S(1)} %fusion.19), kind=kOutput, calls=%fused_computation.10 | convolution fusion | flops 269615104 | bytes 2363392 | tf_op jit(solution)/shard_map/dot_general | solution.py:179
  14.8 41.3 %shard_map.95 = bf16[1024,1024]{1,0:T(8,128)(2,1)} custom-call(bf16[1024,1024]{1,0:T(8,128)(2,1)} %convolution_convert_fusion.1.refs_0_), custom_call_target="tpu_custom_call" | custom-call | tf_op jit(solution)/shard_map/pallas_call | solution.py:82
  56.1 4.3 %reshape.123.refs_1_ = bf16[256,4096]{1,0:T(8,128)(2,1)} reshape(bf16[1024,1024]{1,0:T(8,128)(2,1)} %shard_map.95) | data formatting | bytes 4194304 | tf_op jit(solution)/shard_map/reshape | solution.py:185
  60.4 36.9 %shard_map.96 = (bf16[1024,1024]{1,0:T(8,128)(2,1)}, f32[256,768]{1,0:T(8,128)}, f32[256,768]{1,0:T(8,128)}) custom-call(bf16[1024,1024]{1,0:T(8,128)(2,1)} %multiply_convert_fusion.refs_0_, bf16[256,4096]{1,0:T(8,128)(2,1)} %reshape.123.refs_1_, bf16[4096,768]{1,0:T(8,128)(2,1)} %bitcast.36, bf16[4096,768]{1,0:T(8,128)(2,1)} %bitcast.33), custom_call_target="tpu_custom_call" | custom-call | tf_op jit(solution)/shard_map/pallas_call | solution.py:82
  97.3 3.1 %reshape.124 = bf16[256,4096]{1,0:T(8,128)(2,1)S(1)} reshape(bf16[1024,1024]{1,0:T(8,128)(2,1)} %get-tuple-element.5) | data formatting | bytes 4194304 | tf_op jit(solution)/shard_map/reshape | solution.py:207
  100.4 0.0 copy-start.1
  100.4 0.0 copy-start.2
  100.4 0.0 slice-start
  100.4 4.8 %fusion = f32[256,768]{1,0:T(8,128)S(1)} fusion(bf16[256,4096]{1,0:T(8,128)(2,1)S(1)} %reshape.124, bf16[1,768,4096]{2,1,0:T(8,128)(2,1)} %param.15), kind=kOutput, calls=%fused_computation.4 | convolution fusion | flops 1610612736 | bytes 9175040 | tf_op jit(solution)/shard_map/dot_general | solution.py:126
  105.2 0.0 copy-done.1
  105.2 0.0 copy-done.2
  105.2 0.0 slice-start.1
  105.2 4.9 %fusion.4 = f32[256,4096]{1,0:T(8,128)S(1)} fusion(f32[256,768]{1,0:T(8,128)S(1)} %copy-done.1, f32[256,768]{1,0:T(8,128)S(1)} %fusion, f32[256,768]{1,0:T(8,128)S(1)} %copy-done.2, bf16[1,4096,768]{2,1,0:T(8,128)(2,1)} %param.13), kind=kOutput, calls=%fused_computation.17 | convolution fusion | flops 1612578816 | bytes 12845056 | tf_op jit(solution)/shard_map/dot_general | solution.py:132
  110.1 0.0 slice-done
  110.2 0.0 slice-done.1
  110.2 3.2 %fusion.3 = bf16[256,4096]{1,0:T(8,128)(2,1)} fusion(f32[256,4096]{1,0:T(8,128)S(1)} %fusion.4, f32[256,768]{1,0:T(8,128)S(1)} %fusion, f32[256,768]{1,0:T(8,128)S(1)} %copy-done.1, bf16[1,4096,768]{2,1,0:T(8,128)(2,1)S(1)} %bitcast.35), kind=kOutput, calls=%fused_computation.8 | convolution fusion | flops 1613889536 | bytes 14155776 | tf_op jit(solution)/shard_map/dot_general | solution.py:133
  113.4 4.3 %reshape.125.refs_0_ = bf16[1024,1024]{1,0:T(8,128)(2,1)} reshape(bf16[256,4096]{1,0:T(8,128)(2,1)} %fusion.3) | data formatting | bytes 4194304 | tf_op jit(solution)/shard_map/reshape | solution.py:209
  117.7 34.1 %shard_map.97 = bf16[1024,1024]{1,0:T(8,128)(2,1)} custom-call(bf16[1024,1024]{1,0:T(8,128)(2,1)} %reshape.125.refs_0_), custom_call_target="tpu_custom_call" | custom-call | tf_op jit(solution)/shard_map/pallas_call | solution.py:82
  151.8 2.3 %convolution_convert_fusion.2 = bf16[128,1024]{1,0:T(8,128)(2,1)S(1)} fusion(bf16[1024,1024]{1,0:T(8,128)(2,1)} %shard_map.97, s32[1024]{0:T(1024)S(1)} %fusion.19), kind=kOutput, calls=%fused_computation.11 | convolution fusion | flops 268697600 | bytes 2363392 | tf_op jit(solution)/shard_map/dot_general | solution.py:210
  154.1 0.9 convert_element_type.44
  155.0 5.7 %fusion.2 = bf16[1,768,4096]{2,1,0:T(8,128)(2,1)} fusion(bf16[256,4096]{1,0:T(8,128)(2,1)S(1)} %reshape.124, f32[256,768]{1,0:T(8,128)} %get-tuple-element.6, f32[256,768]{1,0:T(8,128)S(1)} %copy-done.1), kind=kOutput, calls=%fused_computation.6 | convolution fusion | flops 1614938112 | bytes 9961472 | tf_op jit(solution)/shard_map/dot_general | solution.py:123
  (16 shorter events, 0.2 us)
Async XLA Ops:
  0.6 2.0 %copy-start = (s32[32,4]{0,1:T(4,128)S(1)}, s32[32,4]{0,1:T(4,128)}, u32[]{:S(2)}) copy-start(s32[32,4]{0,1:T(4,128)} %param.10) | copy-start | bytes 1540
  2.7 4.9 %copy-start.4 = (s32[32,8]{0,1:T(8,128)S(1)}, s32[32,8]{0,1:T(8,128)}, u32[]{:S(2)}) copy-start(s32[32,8]{0,1:T(8,128)} %param.12) | copy-start | bytes 3076
  5.1 7.4 %copy-start.3 = (bf16[32,4096]{1,0:T(8,128)(2,1)S(1)}, bf16[32,4096]{1,0:T(8,128)(2,1)}, u32[]{:S(2)}) copy-start(bf16[32,4096]{1,0:T(8,128)(2,1)} %param.8) | copy-start | bytes 786436
  100.4 4.8 %copy-start.1 = (f32[256,768]{1,0:T(8,128)S(1)}, f32[256,768]{1,0:T(8,128)}, u32[]{:S(2)}) copy-start(f32[256,768]{1,0:T(8,128)} %get-tuple-element.7) | copy-start | bytes 2359300
  100.4 4.8 %copy-start.2 = (f32[256,768]{1,0:T(8,128)S(1)}, f32[256,768]{1,0:T(8,128)}, u32[]{:S(2)}) copy-start(f32[256,768]{1,0:T(8,128)} %get-tuple-element.6) | copy-start | bytes 2359300
  100.4 9.7 %slice-start = ((s8[6291456]{0:T(1024)(128)(4,1)}), s8[4194304]{0:T(1024)(128)(4,1)S(1)}, s32[]{:S(2)}) async-start(s8[6291456]{0:T(1024)(128)(4,1)} %bitcast.34), calls=%async_computation | async-start | bytes 8388608
  105.2 4.9 %slice-start.1 = ((s8[6291456]{0:T(1024)(128)(4,1)}), s8[2097152]{0:T(1024)(128)(4,1)S(1)}, s32[]{:S(2)}) async-start(s8[6291456]{0:T(1024)(128)(4,1)} %bitcast.34), calls=%async_computation.1 | async-start | bytes 4194304

commit v8 on v5

--- a/solution.py
+++ b/solution.py
@@ -7,12 +7,16 @@
 from jax.experimental.pallas import tpu as pltpu
 
 
-def _exchange_kernel(n_local, *refs):
-    count = (len(refs) - 2) // 2
+def _exchange_kernel(n_local, count, n_work_in, n_work_out, work, *refs):
     srcs = refs[:count]
-    dsts = refs[count:2 * count]
-    send_sems = refs[2 * count]
-    recv_sems = refs[2 * count + 1]
+    work_in = refs[count:count + n_work_in]
+    base = count + n_work_in
+    dsts = refs[base:base + count]
+    work_out = refs[base + count:base + count + n_work_out]
+    base = base + count + n_work_out
+    send_sems = refs[base]
+    recv_sems = refs[base + 1]
+    work_scratch = refs[base + 2:]
     node = lax.axis_index("node")
     local = lax.axis_index("local")
     me = node * n_local + local
@@ -56,6 +60,8 @@
         return carry
 
     lax.fori_loop(1, devices, start_body, 0)
+    if work is not None:
+        work(*work_in, *work_out, *work_scratch)
     nxt = lax.rem(me + 1, devices)
     for i in range(count):
         pltpu.make_async_copy(dsts[i], dsts[i], recv_sems.at[i]).wait()
@@ -69,20 +75,34 @@
         ).wait_send()
 
 
-def exchange(*arrays):
+def exchange(arrays, work=None, work_in=(), work_in_specs=(), work_out=(), work_out_specs=(),
+             work_scratch=()):
     n_local = lax.axis_size("local")
     count = len(arrays)
     return pl.pallas_call(
-        functools.partial(_exchange_kernel, n_local),
-        out_shape=[jax.ShapeDtypeStruct(a.shape, a.dtype) for a in arrays],
-        in_specs=[pl.BlockSpec(memory_space=pl.ANY)] * count,
-        out_specs=[pl.BlockSpec(memory_space=pl.ANY)] * count,
+        functools.partial(_exchange_kernel, n_local, count, len(work_in), len(work_out), work),
+        out_shape=[jax.ShapeDtypeStruct(a.shape, a.dtype) for a in arrays] + list(work_out),
+        in_specs=[pl.BlockSpec(memory_space=pl.ANY)] * count + list(work_in_specs),
+        out_specs=[pl.BlockSpec(memory_space=pl.ANY)] * count + list(work_out_specs),
         scratch_shapes=[
             pltpu.SemaphoreType.DMA((count,)),
             pltpu.SemaphoreType.DMA((count,)),
-        ],
+        ] + list(work_scratch),
         compiler_params=pltpu.CompilerParams(has_side_effects=True),
-    )(*arrays)
+    )(*arrays, *work_in)
+
+
+def _down_grad_work(hidden_t_ref, dy_ref, down_out):
+    n_step = 512
+
+    def step(c, carry):
+        cc = pl.multiple_of(c * n_step, n_step)
+        down_out[:, pl.ds(cc, n_step)] = jnp.dot(
+            hidden_t_ref[...], dy_ref[:, pl.ds(cc, n_step)], preferred_element_type=jnp.float32
+        ).astype(down_out.dtype)
+        return carry
+
+    lax.fori_loop(0, dy_ref.shape[1] // n_step, step, 0)
 
 
 def expert_math(x_rows, dy_rows, w_gate_e, w_up_e, w_down_e):
@@ -92,9 +112,6 @@
     hidden = (gate_act * sig * up_act).astype(jnp.bfloat16)
     contract_rows = (((0,), (0,)), ((), ()))
     contract_last = (((1,), (1,)), ((), ()))
-    down_local = lax.dot_general(
-        hidden, dy_rows, contract_rows, preferred_element_type=jnp.float32
-    ).astype(jnp.bfloat16)
     hidden_grad = lax.dot_general(
         dy_rows, w_down_e, contract_last, preferred_element_type=jnp.float32
     )
@@ -104,7 +121,7 @@
         lax.dot_general(gate_grad, w_gate_e, contract_last, preferred_element_type=jnp.float32)
         + lax.dot_general(up_grad, w_up_e, contract_last, preferred_element_type=jnp.float32)
     ).astype(jnp.bfloat16)
-    return (down_local, row_grad)
+    return (hidden, row_grad)
 
 
 def body(
@@ -153,11 +170,18 @@
     gate_rows = jnp.repeat(gate_val, blocks)
     og_sel = jnp.dot(select, og_pieces, preferred_element_type=jnp.float32)
     send_dy = (gate_rows[:, None] * og_sel).astype(jnp.bfloat16)
-    x_flat, dy_flat = exchange(send_x, send_dy)
+    x_flat, dy_flat = exchange([send_x, send_dy])
     x_rows = x_flat.reshape(experts * capacity, width)
     dy_rows = dy_flat.reshape(experts * capacity, width)
-    down_local, row_grad = expert_math(x_rows, dy_rows, w_gate_e, w_up_e, w_down_e)
-    (returned,) = exchange(row_grad.reshape(experts * tile_rows, piece))
+    hidden, row_grad = expert_math(x_rows, dy_rows, w_gate_e, w_up_e, w_down_e)
+    returned, down_local = exchange(
+        [row_grad.reshape(experts * tile_rows, piece)],
+        work=_down_grad_work,
+        work_in=(hidden.T, dy_rows),
+        work_in_specs=(pl.BlockSpec(memory_space=pltpu.VMEM),) * 2,
+        work_out=(jax.ShapeDtypeStruct((hidden.shape[1], width), jnp.bfloat16),),
+        work_out_specs=(pl.BlockSpec(memory_space=pltpu.VMEM),),
+    )
     total = jnp.dot(select.T, returned, preferred_element_type=jnp.float32)
     token_grad = total.reshape(tok_dev, width).astype(jnp.bfloat16)
     return (token_grad, down_local[None])

time: 155 us -> 165 us (1.065)
  local copies, waits for them, and re-layouts: 22.2 us -> 28 us
  Pallas kernels: 98.5 us -> 103 us
  matrix products: 32.2 us -> 29.6 us
  other arithmetic: 0.55 us -> 3.05 us
    dot_general x1 -> x0, matrix products: 5.72 us -> none  [expert_math(): lax.dot_general(hidden, dy_rows, contract_rows, preferred_element_type=jn...]
    unnamed x21 -> x22, local copies, waits for them, and re-layouts: 2.47 us -> 7.18 us
    pallas_call x2, Pallas kernels: 98.5 us -> 103 us  [exchange(): pl.pallas_call(functools.partial(_exchange_kernel, n_local, count, len(wo...]
    dot_general x1, matrix products: 1.95 us -> 4.85 us  [expert_math(): lax.dot_general(gate_grad, w_gate_e, contract_last, preferred_element_typ...]
    convert_element_type x0 -> x1, other arithmetic: none -> 2.52 us  [expert_math(): hidden = (gate_act * sig * up_act).astype(jnp.bfloat16)]
    dot_general x0 -> x2, local copies, waits for them, and re-layouts: none -> 2.31 us  [the longest x1 1.16 us: expert_math(): gate_act = jnp.dot(x_rows, w_gate_e, preferred_element_type=jnp.float32)]
    reshape x1, local copies, waits for them, and re-layouts: 4.33 us -> 2.56 us  [body(): row_grad.reshape(experts * tile_rows, piece)]
where the time goes in v8:
time: 165 us
  Pallas kernels  103 us (62%)
  matrix products  29.6 us (18%)
  local copies, waits for them, and re-layouts  28 us (17%)
  other arithmetic  3.05 us (2%)
    pallas_call x2, Pallas kernels, exchange(): pl.pallas_call(functools.partial(_exchange_kernel, n_local, count, len(wo...  103 us
    unnamed x22, local copies, waits for them, and re-layouts  7.18 us
    dot_general x1, matrix products, expert_math(): lax.dot_general(dy_rows, w_down_e, contract_last, preferred_element_type=...  5.38 us
    dot_general x1, matrix products, expert_math(): gate_act = jnp.dot(x_rows, w_gate_e, preferred_element_type=jnp.float32)  5.34 us
    dot_general x1, matrix products, expert_math(): lax.dot_general(gate_grad, w_gate_e, contract_last, preferred_element_typ...  4.85 us
    reshape x1, local copies, waits for them, and re-layouts, body(): x_rows = x_flat.reshape(experts * capacity, width)  4.62 us
    dot_general x1, matrix products, expert_math(): up_act = jnp.dot(x_rows, w_up_e, preferred_element_type=jnp.float32)  4.59 us

profile of v8, /device:TPU:1, one launch (start us, length us, event | category | flops | bytes accessed | tf_op | source)
XLA Modules:
  0.0 164.5 jit_solution(17043048798913653655)
XLA Ops:
  0.6 0.0 copy-start
  0.7 0.8 copy.12
  1.4 0.1 reshape.134
  1.5 0.0 copy-done
  1.5 0.0 copy-start.6
  1.6 0.0 copy-start.4
  1.6 0.0 copy-start.5
  1.6 2.4 %gather_fusion.1 = s32[256]{0:T(256)S(1)} fusion(s32[32,4]{0,1:T(4,128)S(1)} %copy-done, s32[256]{0:T(256)S(1)} %reshape.134), kind=kCustom, calls=%fused_computation.1 | custom fusion | bytes 4096 | tf_op jit(solution)/shard_map/jit(take_along_axis)/gather | solution.py:136
  4.0 0.1 reshape.137
  4.1 0.1 mul.81
  4.2 0.1 eq.46
  4.3 0.1 eq.42
  4.4 0.0 copy-done.6
  4.4 0.1 copy.18
  4.5 0.1 reshape.121
  4.6 0.1 copy.16
  4.7 0.2 fusion.25
  5.0 0.2 fusion.26
  5.2 1.4 scatter_custom_fusion
  6.6 1.9 %gather_fusion = s32[256]{0:T(256)S(1)} fusion(s32[256]{0:T(256)S(1)} %reshape.121, s32[1024]{0:T(1024)S(1)} %pad_clamp_fusion), kind=kCustom, calls=%fused_computation | custom fusion | bytes 3072 | tf_op jit(solution)/shard_map/gather | solution.py:169
  8.6 0.1 broadcast_in_dim.42
  8.7 0.1 reshape.119
  8.8 0.1 broadcast_in_dim.43
  8.9 0.1 mul.84
  9.1 0.1 broadcast_in_dim.47
  9.2 0.1 mul.88
  9.3 0.0 copy-done.4
  9.3 0.2 reshape.120
  9.5 0.0 copy-done.5
  9.5 0.2 reshape.122
  9.7 2.1 %multiply_convert_fusion.refs_1_ = bf16[1024,1024]{1,0:T(8,128)(2,1)} fusion(bf16[128,1024]{1,0:T(8,128)(2,1)S(1)} %reshape.122, f32[1024]{0:T(1024)S(1)} %mul.88, s32[1024]{0:T(1024)S(1)} %fusion.33), kind=kOutput, calls=%fused_computation.15 | convolution fusion | flops 270663680 | bytes 2367488 | tf_op jit(solution)/shard_map/dot_general | solution.py:171
  11.7 2.1 %convolution_convert_fusion.refs_0_ = bf16[1024,1024]{1,0:T(8,128)(2,1)} fusion(bf16[128,1024]{1,0:T(8,128)(2,1)S(1)} %reshape.120, s32[1024]{0:T(1024)S(1)} %fusion.33), kind=kOutput, calls=%fused_computation.16 | convolution fusion | flops 269615104 | bytes 2363392 | tf_op jit(solution)/shard_map/dot_general | solution.py:168
  13.8 63.6 %shard_map.95 = (bf16[1024,1024]{1,0:T(8,128)(2,1)}, bf16[1024,1024]{1,0:T(8,128)(2,1)}) custom-call(bf16[1024,1024]{1,0:T(8,128)(2,1)} %convolution_convert_fusion.refs_0_, bf16[1024,1024]{1,0:T(8,128)(2,1)} %multiply_convert_fusion.refs_1_), custom_call_target="tpu_custom_call" | custom-call | tf_op jit(solution)/shard_map/pallas_call | solution.py:82
  77.4 3.1 %reshape.123.refs_2_ = bf16[256,4096]{1,0:T(8,128)(2,1)S(1)} reshape(bf16[1024,1024]{1,0:T(8,128)(2,1)} %get-tuple-element.6) | data formatting | bytes 4194304 | tf_op jit(solution)/shard_map/reshape | solution.py:175
  80.5 0.0 copy-start.1
  80.5 5.4 %fusion.8 = f32[256,768]{1,0:T(8,128)S(1)} fusion(bf16[256,4096]{1,0:T(8,128)(2,1)S(1)} %reshape.123.refs_2_, bf16[1,768,4096]{2,1,0:T(8,128)(2,1)} %param.15), kind=kOutput, calls=%fused_computation.11 | convolution fusion | flops 1610612736 | bytes 9175040 | tf_op jit(solution)/shard_map/dot_general | solution.py:115
  85.9 0.0 copy-done.1
  85.9 0.0 copy-start.2
  85.9 4.6 %reshape.124 = bf16[256,4096]{1,0:T(8,128)(2,1)} reshape(bf16[1024,1024]{1,0:T(8,128)(2,1)} %get-tuple-element.7) | data formatting | bytes 4194304 | tf_op jit(solution)/shard_map/reshape | solution.py:174
  90.6 0.0 copy-start.3
  90.6 5.3 %fusion.2 = f32[256,768]{1,0:T(8,128)S(1)} fusion(bf16[256,4096]{1,0:T(8,128)(2,1)} %reshape.124, bf16[1,4096,768]{2,1,0:T(8,128)(2,1)} %param.13), kind=kOutput, calls=%fused_computation.5 | convolution fusion | flops 1610612736 | bytes 9175040 | tf_op jit(solution)/shard_map/dot_general | solution.py:109
  95.9 0.0 copy-done.3
  95.9 4.6 %fusion.6 = f32[256,768]{1,0:T(8,128)S(1)} fusion(bf16[256,4096]{1,0:T(8,128)(2,1)S(1)} %copy-done.3, bf16[1,4096,768]{2,1,0:T(8,128)(2,1)} %param.14), kind=kOutput, calls=%fused_computation.9 | convolution fusion | flops 1610612736 | bytes 9175040 | tf_op jit(solution)/shard_map/dot_general | solution.py:110
  100.5 1.1 copy.20
  101.7 1.2 copy.19
  102.8 0.0 slice-start
  102.8 2.5 %fusion.16.refs_1_ = bf16[768,256]{1,0:T(8,128)(2,1)} fusion(f32[256,768]{0,1:T(8,128)} %copy.20, f32[256,768]{0,1:T(8,128)} %copy.19), kind=kLoop, calls=%fused_computation.19 | loop fusion | flops 1179648 | bytes 1966080 | tf_op jit(solution)/shard_map/convert_element_type | solution.py:112
  105.3 0.0 copy-done.2
  105.3 0.0 slice-start.1
  105.4 4.8 %fusion = f32[256,4096]{1,0:T(8,128)S(1)} fusion(bf16[1,4096,768]{2,1,0:T(8,128)(2,1)} %param.13, f32[256,768]{1,0:T(8,128)S(1)} %fusion.2, f32[256,768]{1,0:T(8,128)S(1)} %fusion.8, f32[256,768]{1,0:T(8,128)S(1)} %fusion.6), kind=kOutput, calls=%fused_computation.3 | convolution fusion | flops 1612578816 | bytes 12845056 | tf_op jit(solution)/shard_map/dot_general | solution.py:121
  110.2 0.0 slice-done
  110.2 0.0 slice-done.1
  110.2 3.0 %fusion.13 = bf16[256,4096]{1,0:T(8,128)(2,1)S(1)} fusion(f32[256,4096]{1,0:T(8,128)S(1)} %fusion, bf16[1,4096,768]{2,1,0:T(8,128)(2,1)S(1)} %bitcast.60, f32[256,768]{1,0:T(8,128)} %copy-done.2, f32[256,768]{1,0:T(8,128)S(1)} %fusion.2), kind=kOutput, calls=%fused_computation.14 | convolution fusion | flops 1613889536 | bytes 14155776 | tf_op jit(solution)/shard_map/dot_general | solution.py:122
  113.3 2.6 %reshape.125.refs_0_ = bf16[1024,1024]{1,0:T(8,128)(2,1)} reshape(bf16[256,4096]{1,0:T(8,128)(2,1)S(1)} %fusion.13) | data formatting | bytes 4194304 | tf_op jit(solution)/shard_map/reshape | solution.py:178
  115.8 39.3 %shard_map.96 = (bf16[1024,1024]{1,0:T(8,128)(2,1)}, bf16[768,4096]{1,0:T(8,128)(2,1)}) custom-call(bf16[1024,1024]{1,0:T(8,128)(2,1)} %reshape.125.refs_0_, bf16[768,256]{1,0:T(8,128)(2,1)} %fusion.16.refs_1_, bf16[256,4096]{1,0:T(8,128)(2,1)} %copy-done.1), custom_call_target="tpu_custom_call" | custom-call | tf_op jit(solution)/shard_map/pallas_call | solution.py:82
  155.1 2.3 %convolution_convert_fusion.1 = bf16[128,1024]{1,0:T(8,128)(2,1)S(1)} fusion(bf16[1024,1024]{1,0:T(8,128)(2,1)} %get-tuple-element.8, s32[1024]{0:T(1024)S(1)} %fusion.33), kind=kOutput, calls=%fused_computation.17 | convolution fusion | flops 268697600 | bytes 2363392 | tf_op jit(solution)/shard_map/dot_general | solution.py:185
  157.3 0.9 convert_element_type.43
  158.2 6.3 %copy.22 = bf16[1,768,4096]{2,1,0:T(8,128)(2,1)} copy(bf16[1,768,4096]{2,1,0:T(8,128)(2,1)} %bitcast.61) | data formatting | bytes 12582912
  (17 shorter events, 0.2 us)
Async XLA Ops:
  0.6 0.9 copy-start
  1.5 2.9 %copy-start.6 = (s32[32,8]{0,1:T(8,128)S(1)}, s32[32,8]{0,1:T(8,128)}, u32[]{:S(2)}) copy-start(s32[32,8]{0,1:T(8,128)} %param.12) | copy-start | bytes 3076
  1.6 7.7 %copy-start.4 = (bf16[32,4096]{1,0:T(8,128)(2,1)S(1)}, bf16[32,4096]{1,0:T(8,128)(2,1)}, u32[]{:S(2)}) copy-start(bf16[32,4096]{1,0:T(8,128)(2,1)} %param.8) | copy-start | bytes 786436
  1.6 7.9 %copy-start.5 = (bf16[32,4096]{1,0:T(8,128)(2,1)S(1)}, bf16[32,4096]{1,0:T(8,128)(2,1)}, u32[]{:S(2)}) copy-start(bf16[32,4096]{1,0:T(8,128)(2,1)} %param.9) | copy-start | bytes 786436
  80.5 5.4 %copy-start.1 = (bf16[256,4096]{1,0:T(8,128)(2,1)}, bf16[256,4096]{1,0:T(8,128)(2,1)S(1)}, u32[]{:S(2)}) copy-start(bf16[256,4096]{1,0:T(8,128)(2,1)S(1)} %reshape.123.refs_2_) | copy-start | bytes 6291460
  85.9 19.4 %copy-start.2 = (f32[256,768]{1,0:T(8,128)}, f32[256,768]{1,0:T(8,128)S(1)}, u32[]{:S(2)}) copy-start(f32[256,768]{1,0:T(8,128)S(1)} %fusion.8) | copy-start | bytes 2359300
  90.6 5.4 %copy-start.3 = (bf16[256,4096]{1,0:T(8,128)(2,1)S(1)}, bf16[256,4096]{1,0:T(8,128)(2,1)}, u32[]{:S(2)}) copy-start(bf16[256,4096]{1,0:T(8,128)(2,1)} %reshape.124) | copy-start | bytes 6291460
  102.8 7.4 %slice-start = ((s8[6291456]{0:T(1024)(128)(4,1)}), s8[4194304]{0:T(1024)(128)(4,1)S(1)}, s32[]{:S(2)}) async-start(s8[6291456]{0:T(1024)(128)(4,1)} %bitcast.59), calls=%async_computation | async-start | bytes 8388608
  105.3 4.9 %slice-start.1 = ((s8[6291456]{0:T(1024)(128)(4,1)}), s8[2097152]{0:T(1024)(128)(4,1)S(1)}, s32[]{:S(2)}) async-start(s8[6291456]{0:T(1024)(128)(4,1)} %bitcast.59), calls=%async_computation.1 | async-start | bytes 4194304

commit v9 on v5

--- a/solution.py
+++ b/solution.py
@@ -85,25 +85,109 @@
     )(*arrays)
 
 
+def _expert_kernel(x_ref, dy_ref, wg_hbm, wu_hbm, wd_hbm, row_out, down_hbm,
+                   wg, wu, wd, gate_act, up_act, hidden_grad, down_buf, wsem, osem):
+    k_total = x_ref.shape[1]
+    step = 512
+    n_steps = k_total // step
+    nt = (((1,), (1,)), ((), ()))
+    loads = [
+        pltpu.make_async_copy(src, dst, wsem.at[i])
+        for i, (src, dst) in enumerate(((wg_hbm, wg), (wu_hbm, wu), (wd_hbm, wd)))
+    ]
+    for c in loads:
+        c.start()
+
+    def project(w, out):
+        out[...] = jnp.zeros(out.shape, out.dtype)
+
+        def body(k, carry):
+            kk = pl.multiple_of(k * step, step)
+            out[...] += jnp.dot(
+                x_ref[:, pl.ds(kk, step)], w[pl.ds(kk, step), :], preferred_element_type=jnp.float32
+            )
+            return carry
+
+        lax.fori_loop(0, n_steps, body, 0)
+
+    loads[0].wait()
+    project(wg, gate_act)
+    loads[1].wait()
+    project(wu, up_act)
+    loads[2].wait()
+    hidden_grad[...] = jnp.zeros(hidden_grad.shape, hidden_grad.dtype)
+
+    def hg_body(k, carry):
+        kk = pl.multiple_of(k * step, step)
+        hidden_grad[...] += lax.dot_general(
+            dy_ref[:, pl.ds(kk, step)], wd[:, pl.ds(kk, step)], nt,
+            preferred_element_type=jnp.float32,
+        )
+        return carry
+
+    lax.fori_loop(0, n_steps, hg_body, 0)
+    g = gate_act[...]
+    u = up_act[...]
+    hg = hidden_grad[...]
+    sig = 1.0 / (1.0 + jnp.exp(-g))
+    hidden = (g * sig * u).astype(jnp.bfloat16)
+    gate_grad = (hg * u * sig * (1.0 + g * (1.0 - sig))).astype(jnp.bfloat16)
+    up_grad = (hg * g * sig).astype(jnp.bfloat16)
+    hidden_t = jnp.transpose(hidden.astype(jnp.float32)).astype(jnp.bfloat16)
+
+    def out_body(c, carry):
+        cc = pl.multiple_of(c * step, step)
+        row_out[:, pl.ds(cc, step)] = (
+            lax.dot_general(gate_grad, wg[pl.ds(cc, step), :], nt, preferred_element_type=jnp.float32)
+            + lax.dot_general(up_grad, wu[pl.ds(cc, step), :], nt, preferred_element_type=jnp.float32)
+        ).astype(row_out.dtype)
+        slot = c % 2
+
+        @pl.when(c >= 2)
+        def _():
+            pltpu.make_async_copy(
+                down_buf.at[slot], down_hbm.at[:, pl.ds(cc - 2 * step, step)], osem.at[slot]
+            ).wait()
+
+        down_buf[slot] = jnp.dot(
+            hidden_t, dy_ref[:, pl.ds(cc, step)], preferred_element_type=jnp.float32
+        ).astype(down_buf.dtype)
+        pltpu.make_async_copy(down_buf.at[slot], down_hbm.at[:, pl.ds(cc, step)], osem.at[slot]).start()
+        return carry
+
+    lax.fori_loop(0, n_steps, out_body, 0)
+    for c in (n_steps - 2, n_steps - 1):
+        pltpu.make_async_copy(
+            down_buf.at[c % 2], down_hbm.at[:, pl.ds(c * step, step)], osem.at[c % 2]
+        ).wait()
+
+
 def expert_math(x_rows, dy_rows, w_gate_e, w_up_e, w_down_e):
-    gate_act = jnp.dot(x_rows, w_gate_e, preferred_element_type=jnp.float32)
-    up_act = jnp.dot(x_rows, w_up_e, preferred_element_type=jnp.float32)
-    sig = jax.nn.sigmoid(gate_act)
-    hidden = (gate_act * sig * up_act).astype(jnp.bfloat16)
-    contract_rows = (((0,), (0,)), ((), ()))
-    contract_last = (((1,), (1,)), ((), ()))
-    down_local = lax.dot_general(
-        hidden, dy_rows, contract_rows, preferred_element_type=jnp.float32
-    ).astype(jnp.bfloat16)
-    hidden_grad = lax.dot_general(
-        dy_rows, w_down_e, contract_last, preferred_element_type=jnp.float32
-    )
-    gate_grad = (hidden_grad * up_act * sig * (1.0 + gate_act * (1.0 - sig))).astype(jnp.bfloat16)
-    up_grad = (hidden_grad * gate_act * sig).astype(jnp.bfloat16)
-    row_grad = (
-        lax.dot_general(gate_grad, w_gate_e, contract_last, preferred_element_type=jnp.float32)
-        + lax.dot_general(up_grad, w_up_e, contract_last, preferred_element_type=jnp.float32)
-    ).astype(jnp.bfloat16)
+    n_rows, width = x_rows.shape
+    hid = w_gate_e.shape[1]
+    vmem = pl.BlockSpec(memory_space=pltpu.VMEM)
+    hbm = pl.BlockSpec(memory_space=pl.ANY)
+    row_grad, down_local = pl.pallas_call(
+        _expert_kernel,
+        out_shape=[
+            jax.ShapeDtypeStruct((n_rows, width), jnp.bfloat16),
+            jax.ShapeDtypeStruct((hid, width), jnp.bfloat16),
+        ],
+        in_specs=[vmem, vmem, hbm, hbm, hbm],
+        out_specs=[vmem, hbm],
+        scratch_shapes=[
+            pltpu.VMEM(w_gate_e.shape, w_gate_e.dtype),
+            pltpu.VMEM(w_up_e.shape, w_up_e.dtype),
+            pltpu.VMEM(w_down_e.shape, w_down_e.dtype),
+            pltpu.VMEM((n_rows, hid), jnp.float32),
+            pltpu.VMEM((n_rows, hid), jnp.float32),
+            pltpu.VMEM((n_rows, hid), jnp.float32),
+            pltpu.VMEM((2, hid, 512), jnp.bfloat16),
+            pltpu.SemaphoreType.DMA((3,)),
+            pltpu.SemaphoreType.DMA((2,)),
+        ],
+        compiler_params=pltpu.CompilerParams(vmem_limit_bytes=60 * 1024 * 1024),
+    )(x_rows, dy_rows, w_gate_e, w_up_e, w_down_e)
     return (down_local, row_grad)
 
 

time: 155 us -> 152 us (0.981)
  matrix products: 32.2 us -> 6.45 us
  Pallas kernels: 98.5 us -> 123 us
  local copies, waits for them, and re-layouts: 22.2 us -> 20.6 us
    dot_general x6 -> x0, matrix products: 25.7 us -> none  [the longest x1 5.72 us: expert_math(): lax.dot_general(hidden, dy_rows, contract_rows, preferred_element_type=jn...]
    pallas_call x0 -> x1, Pallas kernels: none -> 25 us  [expert_math(): pl.pallas_call(_expert_kernel, out_shape=[jax.ShapeDtypeStruct((n_rows, w...]
    unnamed x21 -> x13, local copies, waits for them, and re-layouts: 2.47 us -> 0.88 us
where the time goes in v9:
time: 152 us
  Pallas kernels  123 us (81%)
  local copies, waits for them, and re-layouts  20.6 us (14%)
  matrix products  6.45 us (4%)
    pallas_call x2, Pallas kernels, exchange(): pl.pallas_call(functools.partial(_exchange_kernel, n_local), out_shape=[j...  98.5 us
    pallas_call x1, Pallas kernels, expert_math(): pl.pallas_call(_expert_kernel, out_shape=[jax.ShapeDtypeStruct((n_rows, w...  25 us
    reshape x1, local copies, waits for them, and re-layouts, body(): x_rows = x_flat.reshape(experts * capacity, width)  4.5 us
    reshape x1, local copies, waits for them, and re-layouts, body(): returned, = exchange(row_grad.reshape(experts * tile_rows, piece))  4.36 us

profile of v9, /device:TPU:1, one launch (start us, length us, event | category | flops | bytes accessed | tf_op | source)
XLA Modules:
  0.0 151.9 jit_solution(11004700551129707249)
XLA Ops:
  0.6 0.0 copy-start
  0.7 0.8 copy.10
  1.4 0.1 reshape.134
  1.5 0.0 copy-done
  1.5 0.0 copy-start.4
  1.6 2.4 %gather_fusion.1 = s32[256]{0:T(256)S(1)} fusion(s32[32,4]{0,1:T(4,128)S(1)} %copy-done, s32[256]{0:T(256)S(1)} %reshape.134), kind=kCustom, calls=%fused_computation.1 | custom fusion | bytes 4096 | tf_op jit(solution)/shard_map/jit(take_along_axis)/gather | solution.py:203
  4.0 0.0 copy-start.2
  4.0 0.0 copy-start.3
  4.0 0.1 reshape.137
  4.1 0.1 mul.55
  4.2 0.1 eq.46
  4.3 0.1 eq.42
  4.4 0.0 copy-done.4
  4.4 0.1 copy.16
  4.5 0.1 reshape.121
  4.6 0.1 copy.14
  4.7 0.2 fusion.3
  5.0 0.2 fusion.4
  5.2 1.4 scatter_custom_fusion
  6.6 1.9 %gather_fusion = s32[256]{0:T(256)S(1)} fusion(s32[256]{0:T(256)S(1)} %reshape.121, s32[1024]{0:T(1024)S(1)} %pad_clamp_fusion), kind=kCustom, calls=%fused_computation | custom fusion | bytes 3072 | tf_op jit(solution)/shard_map/gather | solution.py:236
  8.6 0.1 broadcast_in_dim.42
  8.7 0.1 reshape.119
  8.8 0.1 broadcast_in_dim.43
  8.9 0.1 mul.58
  9.1 0.1 broadcast_in_dim.47
  9.2 0.1 mul.62
  9.3 0.0 copy-done.2
  9.3 0.2 reshape.120
  9.5 0.0 copy-done.3
  9.5 0.2 reshape.122
  9.7 2.1 %multiply_convert_fusion.refs_1_ = bf16[1024,1024]{1,0:T(8,128)(2,1)} fusion(bf16[128,1024]{1,0:T(8,128)(2,1)S(1)} %reshape.122, f32[1024]{0:T(1024)S(1)} %mul.62, s32[1024]{0:T(1024)S(1)} %fusion.11), kind=kOutput, calls=%fused_computation.3 | convolution fusion | flops 270663680 | bytes 2367488 | tf_op jit(solution)/shard_map/dot_general | solution.py:238
  11.8 2.1 %convolution_convert_fusion.refs_0_ = bf16[1024,1024]{1,0:T(8,128)(2,1)} fusion(bf16[128,1024]{1,0:T(8,128)(2,1)S(1)} %reshape.120, s32[1024]{0:T(1024)S(1)} %fusion.11), kind=kOutput, calls=%fused_computation.4 | convolution fusion | flops 269615104 | bytes 2363392 | tf_op jit(solution)/shard_map/dot_general | solution.py:235
  13.9 63.6 %shard_map.95 = (bf16[1024,1024]{1,0:T(8,128)(2,1)}, bf16[1024,1024]{1,0:T(8,128)(2,1)}) custom-call(bf16[1024,1024]{1,0:T(8,128)(2,1)} %convolution_convert_fusion.refs_0_, bf16[1024,1024]{1,0:T(8,128)(2,1)} %multiply_convert_fusion.refs_1_), custom_call_target="tpu_custom_call" | custom-call | tf_op jit(solution)/shard_map/pallas_call | solution.py:75
  77.4 0.0 copy-start.1
  77.5 4.5 %reshape.123.x_ref = bf16[256,4096]{1,0:T(8,128)(2,1)} reshape(bf16[1024,1024]{1,0:T(8,128)(2,1)} %get-tuple-element.6) | data formatting | bytes 4194304 | tf_op jit(solution)/shard_map/reshape | solution.py:241
  82.0 0.0 copy-done.1
  82.0 2.6 %reshape.124.dy_ref = bf16[256,4096]{1,0:T(8,128)(2,1)} reshape(bf16[1024,1024]{1,0:T(8,128)(2,1)S(1)} %copy-done.1) | data formatting | bytes 4194304 | tf_op jit(solution)/shard_map/reshape | solution.py:242
  84.5 25.0 %shard_map.96 = (bf16[256,4096]{1,0:T(8,128)(2,1)}, bf16[768,4096]{1,0:T(8,128)(2,1)}) custom-call(bf16[256,4096]{1,0:T(8,128)(2,1)} %reshape.123.x_ref, bf16[256,4096]{1,0:T(8,128)(2,1)} %reshape.124.dy_ref, bf16[4096,768]{1,0:T(8,128)(2,1)} %bitcast.25, bf16[4096,768]{1,0:T(8,128)(2,1)} %bitcast.26, bf16[768,4096]{1,0:T(8,128)(2,1)} %bitcast.27), custom_call_target="tpu_custom_call" | custom-call | tf_op jit(solution)/shard_map/pallas_call | solution.py:170
  109.5 4.4 %reshape.125.refs_0_ = bf16[1024,1024]{1,0:T(8,128)(2,1)} reshape(bf16[256,4096]{1,0:T(8,128)(2,1)} %get-tuple-element.8) | data formatting | bytes 4194304 | tf_op jit(solution)/shard_map/reshape | solution.py:244
  113.9 34.9 %shard_map.97 = bf16[1024,1024]{1,0:T(8,128)(2,1)} custom-call(bf16[1024,1024]{1,0:T(8,128)(2,1)} %reshape.125.refs_0_), custom_call_target="tpu_custom_call" | custom-call | tf_op jit(solution)/shard_map/pallas_call | solution.py:75
  148.8 2.3 %convolution_convert_fusion.1 = bf16[128,1024]{1,0:T(8,128)(2,1)S(1)} fusion(bf16[1024,1024]{1,0:T(8,128)(2,1)} %shard_map.97, s32[1024]{0:T(1024)S(1)} %fusion.11), kind=kOutput, calls=%fused_computation.5 | convolution fusion | flops 268697600 | bytes 2363392 | tf_op jit(solution)/shard_map/dot_general | solution.py:245
  151.0 0.9 convert_element_type.26
  (16 shorter events, 0.2 us)
Async XLA Ops:
  0.6 0.9 copy-start
  1.5 2.9 %copy-start.4 = (s32[32,8]{0,1:T(8,128)S(1)}, s32[32,8]{0,1:T(8,128)}, u32[]{:S(2)}) copy-start(s32[32,8]{0,1:T(8,128)} %param.12) | copy-start | bytes 3076
  4.0 5.3 %copy-start.2 = (bf16[32,4096]{1,0:T(8,128)(2,1)S(1)}, bf16[32,4096]{1,0:T(8,128)(2,1)}, u32[]{:S(2)}) copy-start(bf16[32,4096]{1,0:T(8,128)(2,1)} %param.8) | copy-start | bytes 786436
  4.0 5.5 %copy-start.3 = (bf16[32,4096]{1,0:T(8,128)(2,1)S(1)}, bf16[32,4096]{1,0:T(8,128)(2,1)}, u32[]{:S(2)}) copy-start(bf16[32,4096]{1,0:T(8,128)(2,1)} %param.9) | copy-start | bytes 786436
  77.4 4.5 %copy-start.1 = (bf16[1024,1024]{1,0:T(8,128)(2,1)S(1)}, bf16[1024,1024]{1,0:T(8,128)(2,1)}, u32[]{:S(2)}) copy-start(bf16[1024,1024]{1,0:T(8,128)(2,1)} %get-tuple-element.7) | copy-start | bytes 6291460

commit v10 on v9

--- a/solution.py
+++ b/solution.py
@@ -91,34 +91,47 @@
     step = 512
     n_steps = k_total // step
     nt = (((1,), (1,)), ((), ()))
-    loads = [
-        pltpu.make_async_copy(src, dst, wsem.at[i])
-        for i, (src, dst) in enumerate(((wg_hbm, wg), (wu_hbm, wu), (wd_hbm, wd)))
-    ]
-    for c in loads:
-        c.start()
-
-    def project(w, out):
-        out[...] = jnp.zeros(out.shape, out.dtype)
-
-        def body(k, carry):
-            kk = pl.multiple_of(k * step, step)
-            out[...] += jnp.dot(
-                x_ref[:, pl.ds(kk, step)], w[pl.ds(kk, step), :], preferred_element_type=jnp.float32
-            )
-            return carry
-
-        lax.fori_loop(0, n_steps, body, 0)
-
-    loads[0].wait()
-    project(wg, gate_act)
-    loads[1].wait()
-    project(wu, up_act)
-    loads[2].wait()
+    sources = ((wg_hbm, wg), (wu_hbm, wu))
+
+    def row_chunk(i, k):
+        src, dst = sources[i]
+        kk = pl.multiple_of(k * step, step)
+        return pltpu.make_async_copy(src.at[pl.ds(kk, step)], dst.at[pl.ds(kk, step)], wsem.at[i, k])
+
+    def col_chunk(k):
+        kk = pl.multiple_of(k * step, step)
+        return pltpu.make_async_copy(wd_hbm.at[:, pl.ds(kk, step)], wd.at[:, pl.ds(kk, step)], wsem.at[2, k])
+
+    def start_body(k, carry):
+        row_chunk(0, k).start()
+        row_chunk(1, k).start()
+        return carry
+
+    lax.fori_loop(0, n_steps, start_body, 0)
+
+    def start_wd(k, carry):
+        col_chunk(k).start()
+        return carry
+
+    lax.fori_loop(0, n_steps, start_wd, 0)
+    gate_act[...] = jnp.zeros(gate_act.shape, gate_act.dtype)
+    up_act[...] = jnp.zeros(up_act.shape, up_act.dtype)
+
+    def proj_body(k, carry):
+        kk = pl.multiple_of(k * step, step)
+        x_blk = x_ref[:, pl.ds(kk, step)]
+        row_chunk(0, k).wait()
+        gate_act[...] += jnp.dot(x_blk, wg[pl.ds(kk, step), :], preferred_element_type=jnp.float32)
+        row_chunk(1, k).wait()
+        up_act[...] += jnp.dot(x_blk, wu[pl.ds(kk, step), :], preferred_element_type=jnp.float32)
+        return carry
+
+    lax.fori_loop(0, n_steps, proj_body, 0)
     hidden_grad[...] = jnp.zeros(hidden_grad.shape, hidden_grad.dtype)
 
     def hg_body(k, carry):
         kk = pl.multiple_of(k * step, step)
+        col_chunk(k).wait()
         hidden_grad[...] += lax.dot_general(
             dy_ref[:, pl.ds(kk, step)], wd[:, pl.ds(kk, step)], nt,
             preferred_element_type=jnp.float32,
@@ -183,7 +196,7 @@
             pltpu.VMEM((n_rows, hid), jnp.float32),
             pltpu.VMEM((n_rows, hid), jnp.float32),
             pltpu.VMEM((2, hid, 512), jnp.bfloat16),
-            pltpu.SemaphoreType.DMA((3,)),
+            pltpu.SemaphoreType.DMA((3, width // 512)),
             pltpu.SemaphoreType.DMA((2,)),
         ],
         compiler_params=pltpu.CompilerParams(vmem_limit_bytes=60 * 1024 * 1024),

time: 152 us -> 152 us (level)
  no operation moved by 1% of the time
where the time goes in v10:
time: 152 us; the launch traced here: 151 us
  Pallas kernels  123 us (81%)
  local copies, waits for them, and re-layouts  20.6 us (14%)
  matrix products  6.45 us (4%)
    pallas_call x2, Pallas kernels, exchange(): pl.pallas_call(functools.partial(_exchange_kernel, n_local), out_shape=[j...  98.5 us
    pallas_call x1, Pallas kernels, expert_math(): pl.pallas_call(_expert_kernel, out_shape=[jax.ShapeDtypeStruct((n_rows, w...  24.5 us
    reshape x1, local copies, waits for them, and re-layouts, body(): x_rows = x_flat.reshape(experts * capacity, width)  4.5 us
    reshape x1, local copies, waits for them, and re-layouts, body(): returned, = exchange(row_grad.reshape(experts * tile_rows, piece))  4.36 us

profile of v10, /device:TPU:1, one launch (start us, length us, event | category | flops | bytes accessed | tf_op | source)
XLA Modules:
  0.0 151.5 jit_solution(2465229915186893075)
XLA Ops:
  0.6 0.0 copy-start
  0.7 0.8 copy.10
  1.4 0.1 reshape.134
  1.5 0.0 copy-done
  1.5 0.0 copy-start.4
  1.6 2.4 %gather_fusion.1 = s32[256]{0:T(256)S(1)} fusion(s32[32,4]{0,1:T(4,128)S(1)} %copy-done, s32[256]{0:T(256)S(1)} %reshape.134), kind=kCustom, calls=%fused_computation.1 | custom fusion | bytes 4096 | tf_op jit(solution)/shard_map/jit(take_along_axis)/gather | solution.py:216
  4.0 0.0 copy-start.2
  4.0 0.0 copy-start.3
  4.0 0.1 reshape.137
  4.1 0.1 mul.55
  4.2 0.1 eq.46
  4.3 0.1 eq.42
  4.4 0.0 copy-done.4
  4.4 0.1 copy.16
  4.5 0.1 reshape.121
  4.6 0.1 copy.14
  4.7 0.2 fusion.3
  5.0 0.2 fusion.4
  5.2 1.4 scatter_custom_fusion
  6.6 1.9 %gather_fusion = s32[256]{0:T(256)S(1)} fusion(s32[256]{0:T(256)S(1)} %reshape.121, s32[1024]{0:T(1024)S(1)} %pad_clamp_fusion), kind=kCustom, calls=%fused_computation | custom fusion | bytes 3072 | tf_op jit(solution)/shard_map/gather | solution.py:249
  8.6 0.1 broadcast_in_dim.42
  8.7 0.1 reshape.119
  8.8 0.1 broadcast_in_dim.43
  8.9 0.1 mul.58
  9.1 0.1 broadcast_in_dim.47
  9.2 0.1 mul.62
  9.3 0.0 copy-done.2
  9.3 0.2 reshape.120
  9.5 0.0 copy-done.3
  9.5 0.2 reshape.122
  9.7 2.1 %multiply_convert_fusion.refs_1_ = bf16[1024,1024]{1,0:T(8,128)(2,1)} fusion(bf16[128,1024]{1,0:T(8,128)(2,1)S(1)} %reshape.122, f32[1024]{0:T(1024)S(1)} %mul.62, s32[1024]{0:T(1024)S(1)} %fusion.11), kind=kOutput, calls=%fused_computation.3 | convolution fusion | flops 270663680 | bytes 2367488 | tf_op jit(solution)/shard_map/dot_general | solution.py:251
  11.8 2.1 %convolution_convert_fusion.refs_0_ = bf16[1024,1024]{1,0:T(8,128)(2,1)} fusion(bf16[128,1024]{1,0:T(8,128)(2,1)S(1)} %reshape.120, s32[1024]{0:T(1024)S(1)} %fusion.11), kind=kOutput, calls=%fused_computation.4 | convolution fusion | flops 269615104 | bytes 2363392 | tf_op jit(solution)/shard_map/dot_general | solution.py:248
  13.9 63.6 %shard_map.95 = (bf16[1024,1024]{1,0:T(8,128)(2,1)}, bf16[1024,1024]{1,0:T(8,128)(2,1)}) custom-call(bf16[1024,1024]{1,0:T(8,128)(2,1)} %convolution_convert_fusion.refs_0_, bf16[1024,1024]{1,0:T(8,128)(2,1)} %multiply_convert_fusion.refs_1_), custom_call_target="tpu_custom_call" | custom-call | tf_op jit(solution)/shard_map/pallas_call | solution.py:75
  77.4 0.0 copy-start.1
  77.5 4.5 %reshape.123.x_ref = bf16[256,4096]{1,0:T(8,128)(2,1)} reshape(bf16[1024,1024]{1,0:T(8,128)(2,1)} %get-tuple-element.6) | data formatting | bytes 4194304 | tf_op jit(solution)/shard_map/reshape | solution.py:254
  82.0 0.0 copy-done.1
  82.0 2.6 %reshape.124.dy_ref = bf16[256,4096]{1,0:T(8,128)(2,1)} reshape(bf16[1024,1024]{1,0:T(8,128)(2,1)S(1)} %copy-done.1) | data formatting | bytes 4194304 | tf_op jit(solution)/shard_map/reshape | solution.py:255
  84.5 24.5 %shard_map.96 = (bf16[256,4096]{1,0:T(8,128)(2,1)}, bf16[768,4096]{1,0:T(8,128)(2,1)}) custom-call(bf16[256,4096]{1,0:T(8,128)(2,1)} %reshape.123.x_ref, bf16[256,4096]{1,0:T(8,128)(2,1)} %reshape.124.dy_ref, bf16[4096,768]{1,0:T(8,128)(2,1)} %bitcast.25, bf16[4096,768]{1,0:T(8,128)(2,1)} %bitcast.26, bf16[768,4096]{1,0:T(8,128)(2,1)} %bitcast.27), custom_call_target="tpu_custom_call" | custom-call | tf_op jit(solution)/shard_map/pallas_call | solution.py:183
  109.1 4.4 %reshape.125.refs_0_ = bf16[1024,1024]{1,0:T(8,128)(2,1)} reshape(bf16[256,4096]{1,0:T(8,128)(2,1)} %get-tuple-element.8) | data formatting | bytes 4194304 | tf_op jit(solution)/shard_map/reshape | solution.py:257
  113.4 34.9 %shard_map.97 = bf16[1024,1024]{1,0:T(8,128)(2,1)} custom-call(bf16[1024,1024]{1,0:T(8,128)(2,1)} %reshape.125.refs_0_), custom_call_target="tpu_custom_call" | custom-call | tf_op jit(solution)/shard_map/pallas_call | solution.py:75
  148.3 2.3 %convolution_convert_fusion.1 = bf16[128,1024]{1,0:T(8,128)(2,1)S(1)} fusion(bf16[1024,1024]{1,0:T(8,128)(2,1)} %shard_map.97, s32[1024]{0:T(1024)S(1)} %fusion.11), kind=kOutput, calls=%fused_computation.5 | convolution fusion | flops 268697600 | bytes 2363392 | tf_op jit(solution)/shard_map/dot_general | solution.py:258
  150.6 0.9 convert_element_type.26
  (16 shorter events, 0.2 us)
Async XLA Ops:
  0.6 0.9 copy-start
  1.5 2.9 %copy-start.4 = (s32[32,8]{0,1:T(8,128)S(1)}, s32[32,8]{0,1:T(8,128)}, u32[]{:S(2)}) copy-start(s32[32,8]{0,1:T(8,128)} %param.12) | copy-start | bytes 3076
  4.0 5.3 %copy-start.2 = (bf16[32,4096]{1,0:T(8,128)(2,1)S(1)}, bf16[32,4096]{1,0:T(8,128)(2,1)}, u32[]{:S(2)}) copy-start(bf16[32,4096]{1,0:T(8,128)(2,1)} %param.8) | copy-start | bytes 786436
  4.0 5.5 %copy-start.3 = (bf16[32,4096]{1,0:T(8,128)(2,1)S(1)}, bf16[32,4096]{1,0:T(8,128)(2,1)}, u32[]{:S(2)}) copy-start(bf16[32,4096]{1,0:T(8,128)(2,1)} %param.9) | copy-start | bytes 786436
  77.4 4.5 %copy-start.1 = (bf16[1024,1024]{1,0:T(8,128)(2,1)S(1)}, bf16[1024,1024]{1,0:T(8,128)(2,1)}, u32[]{:S(2)}) copy-start(bf16[1024,1024]{1,0:T(8,128)(2,1)} %get-tuple-element.7) | copy-start | bytes 6291460

commit v11 on v10

--- a/solution.py
+++ b/solution.py
@@ -85,9 +85,21 @@
     )(*arrays)
 
 
-def _expert_kernel(x_ref, dy_ref, wg_hbm, wu_hbm, wd_hbm, row_out, down_hbm,
-                   wg, wu, wd, gate_act, up_act, hidden_grad, down_buf, wsem, osem):
+def _expert_kernel(xf_ref, dyf_ref, wg_hbm, wu_hbm, wd_hbm, row_out, down_hbm,
+                   wg, wu, wd, gate_act, up_act, hidden_grad, down_buf, x_ref, dy_ref, wide,
+                   wsem, osem):
     k_total = x_ref.shape[1]
+    lane = wide.shape[2]
+    n_rows = x_ref.shape[0]
+    blocks = wide.shape[1] // n_rows
+    piece = wide.shape[0] * lane
+    for src, dst in ((xf_ref, x_ref), (dyf_ref, dy_ref)):
+        for cb in range(wide.shape[0]):
+            wide[cb] = src[:, cb * lane:(cb + 1) * lane].astype(jnp.float32)
+        for j in range(blocks):
+            for cb in range(wide.shape[0]):
+                col = j * piece + cb * lane
+                dst[:, col:col + lane] = wide[cb, pl.ds(j, n_rows, stride=blocks), :].astype(dst.dtype)
     step = 512
     n_steps = k_total // step
     nt = (((1,), (1,)), ((), ()))
@@ -148,42 +160,42 @@
     up_grad = (hg * g * sig).astype(jnp.bfloat16)
     hidden_t = jnp.transpose(hidden.astype(jnp.float32)).astype(jnp.bfloat16)
 
-    def out_body(c, carry):
-        cc = pl.multiple_of(c * step, step)
-        row_out[:, pl.ds(cc, step)] = (
-            lax.dot_general(gate_grad, wg[pl.ds(cc, step), :], nt, preferred_element_type=jnp.float32)
-            + lax.dot_general(up_grad, wu[pl.ds(cc, step), :], nt, preferred_element_type=jnp.float32)
-        ).astype(row_out.dtype)
+    for c in range(n_steps):
+        cc = c * step
+        rg = (
+            lax.dot_general(gate_grad, wg[cc:cc + step, :], nt, preferred_element_type=jnp.float32)
+            + lax.dot_general(up_grad, wu[cc:cc + step, :], nt, preferred_element_type=jnp.float32)
+        ).astype(jnp.bfloat16)
+        j, h = divmod(cc, piece)
+        for q in range(step // lane):
+            wide[h // lane + q, pl.ds(j, n_rows, stride=blocks), :] = (
+                rg[:, q * lane:(q + 1) * lane].astype(jnp.float32)
+            )
         slot = c % 2
-
-        @pl.when(c >= 2)
-        def _():
+        if c >= 2:
             pltpu.make_async_copy(
-                down_buf.at[slot], down_hbm.at[:, pl.ds(cc - 2 * step, step)], osem.at[slot]
+                down_buf.at[slot], down_hbm.at[:, cc - 2 * step:cc - step], osem.at[slot]
             ).wait()
-
         down_buf[slot] = jnp.dot(
-            hidden_t, dy_ref[:, pl.ds(cc, step)], preferred_element_type=jnp.float32
+            hidden_t, dy_ref[:, cc:cc + step], preferred_element_type=jnp.float32
         ).astype(down_buf.dtype)
-        pltpu.make_async_copy(down_buf.at[slot], down_hbm.at[:, pl.ds(cc, step)], osem.at[slot]).start()
-        return carry
-
-    lax.fori_loop(0, n_steps, out_body, 0)
+        pltpu.make_async_copy(down_buf.at[slot], down_hbm.at[:, cc:cc + step], osem.at[slot]).start()
+    for cb in range(wide.shape[0]):
+        row_out[:, cb * lane:(cb + 1) * lane] = wide[cb].astype(row_out.dtype)
     for c in (n_steps - 2, n_steps - 1):
         pltpu.make_async_copy(
-            down_buf.at[c % 2], down_hbm.at[:, pl.ds(c * step, step)], osem.at[c % 2]
+            down_buf.at[c % 2], down_hbm.at[:, c * step:(c + 1) * step], osem.at[c % 2]
         ).wait()
 
 
-def expert_math(x_rows, dy_rows, w_gate_e, w_up_e, w_down_e):
-    n_rows, width = x_rows.shape
+def expert_math(x_flat, dy_flat, w_gate_e, w_up_e, w_down_e, n_rows, width):
     hid = w_gate_e.shape[1]
     vmem = pl.BlockSpec(memory_space=pltpu.VMEM)
     hbm = pl.BlockSpec(memory_space=pl.ANY)
-    row_grad, down_local = pl.pallas_call(
+    row_flat, down_local = pl.pallas_call(
         _expert_kernel,
         out_shape=[
-            jax.ShapeDtypeStruct((n_rows, width), jnp.bfloat16),
+            jax.ShapeDtypeStruct(x_flat.shape, jnp.bfloat16),
             jax.ShapeDtypeStruct((hid, width), jnp.bfloat16),
         ],
         in_specs=[vmem, vmem, hbm, hbm, hbm],
@@ -196,12 +208,15 @@
             pltpu.VMEM((n_rows, hid), jnp.float32),
             pltpu.VMEM((n_rows, hid), jnp.float32),
             pltpu.VMEM((2, hid, 512), jnp.bfloat16),
+            pltpu.VMEM((n_rows, width), jnp.bfloat16),
+            pltpu.VMEM((n_rows, width), jnp.bfloat16),
+            pltpu.VMEM((x_flat.shape[1] // 128, x_flat.shape[0], 128), jnp.float32),
             pltpu.SemaphoreType.DMA((3, width // 512)),
             pltpu.SemaphoreType.DMA((2,)),
         ],
-        compiler_params=pltpu.CompilerParams(vmem_limit_bytes=60 * 1024 * 1024),
-    )(x_rows, dy_rows, w_gate_e, w_up_e, w_down_e)
-    return (down_local, row_grad)
+        compiler_params=pltpu.CompilerParams(vmem_limit_bytes=62 * 1024 * 1024),
+    )(x_flat, dy_flat, w_gate_e, w_up_e, w_down_e)
+    return (down_local, row_flat)
 
 
 def body(
@@ -251,10 +266,10 @@
     og_sel = jnp.dot(select, og_pieces, preferred_element_type=jnp.float32)
     send_dy = (gate_rows[:, None] * og_sel).astype(jnp.bfloat16)
     x_flat, dy_flat = exchange(send_x, send_dy)
-    x_rows = x_flat.reshape(experts * capacity, width)
-    dy_rows = dy_flat.reshape(experts * capacity, width)
-    down_local, row_grad = expert_math(x_rows, dy_rows, w_gate_e, w_up_e, w_down_e)
-    (returned,) = exchange(row_grad.reshape(experts * tile_rows, piece))
+    down_local, row_flat = expert_math(
+        x_flat, dy_flat, w_gate_e, w_up_e, w_down_e, experts * capacity, width
+    )
+    (returned,) = exchange(row_flat)
     total = jnp.dot(select.T, returned, preferred_element_type=jnp.float32)
     token_grad = total.reshape(tok_dev, width).astype(jnp.bfloat16)
     return (token_grad, down_local[None])

time: 152 us -> 141 us (0.928)
  local copies, waits for them, and re-layouts: 20.6 us -> 9.13 us
    reshape x3 -> x0, local copies, waits for them, and re-layouts: 11.4 us -> none  [the longest x1 4.5 us: body(): x_rows = x_flat.reshape(experts * capacity, width)]
where the time goes in v11:
time: 141 us
  Pallas kernels  124 us (88%)
  local copies, waits for them, and re-layouts  9.13 us (6%)
  matrix products  6.43 us (5%)
    pallas_call x2, Pallas kernels, exchange(): pl.pallas_call(functools.partial(_exchange_kernel, n_local), out_shape=[j...  98.5 us
    pallas_call x1, Pallas kernels, expert_math(): pl.pallas_call(_expert_kernel, out_shape=[jax.ShapeDtypeStruct(x_flat.sha...  25.3 us

profile of v11, /device:TPU:1, one launch (start us, length us, event | category | flops | bytes accessed | tf_op | source)
XLA Modules:
  0.0 140.8 jit_solution(4754756652721701008)
XLA Ops:
  0.6 0.0 copy-start
  0.7 0.8 copy.10
  1.4 0.1 reshape.122
  1.5 0.0 copy-done
  1.5 0.0 copy-start.3
  1.6 2.4 %gather_fusion.1 = s32[256]{0:T(256)S(1)} fusion(s32[32,4]{0,1:T(4,128)S(1)} %copy-done, s32[256]{0:T(256)S(1)} %reshape.122), kind=kCustom, calls=%fused_computation.1 | custom fusion | bytes 4096 | tf_op jit(solution)/shard_map/jit(take_along_axis)/gather | solution.py:231
  4.0 0.0 copy-start.1
  4.0 0.0 copy-start.2
  4.0 0.1 reshape.125
  4.1 0.1 mul.55
  4.2 0.1 eq.46
  4.3 0.1 eq.42
  4.4 0.0 copy-done.3
  4.4 0.1 copy.16
  4.5 0.1 reshape.112
  4.6 0.1 copy.14
  4.7 0.2 fusion.3
  5.0 0.2 fusion.4
  5.2 1.4 scatter_custom_fusion
  6.6 1.9 %gather_fusion = s32[256]{0:T(256)S(1)} fusion(s32[256]{0:T(256)S(1)} %reshape.112, s32[1024]{0:T(1024)S(1)} %pad_clamp_fusion), kind=kCustom, calls=%fused_computation | custom fusion | bytes 3072 | tf_op jit(solution)/shard_map/gather | solution.py:264
  8.6 0.1 broadcast_in_dim.42
  8.7 0.1 reshape.110
  8.8 0.1 broadcast_in_dim.43
  8.9 0.1 mul.58
  9.1 0.1 broadcast_in_dim.47
  9.2 0.1 mul.62
  9.3 0.0 copy-done.1
  9.3 0.2 reshape.111
  9.5 0.0 copy-done.2
  9.5 0.2 reshape.113
  9.7 2.1 %multiply_convert_fusion.refs_1_ = bf16[1024,1024]{1,0:T(8,128)(2,1)} fusion(bf16[128,1024]{1,0:T(8,128)(2,1)S(1)} %reshape.113, f32[1024]{0:T(1024)S(1)} %mul.62, s32[1024]{0:T(1024)S(1)} %fusion.11), kind=kOutput, calls=%fused_computation.3 | convolution fusion | flops 270663680 | bytes 2367488 | tf_op jit(solution)/shard_map/dot_general | solution.py:266
  11.8 2.1 %convolution_convert_fusion.refs_0_ = bf16[1024,1024]{1,0:T(8,128)(2,1)} fusion(bf16[128,1024]{1,0:T(8,128)(2,1)S(1)} %reshape.111, s32[1024]{0:T(1024)S(1)} %fusion.11), kind=kOutput, calls=%fused_computation.4 | convolution fusion | flops 269615104 | bytes 2363392 | tf_op jit(solution)/shard_map/dot_general | solution.py:263
  13.8 63.6 %shard_map.95 = (bf16[1024,1024]{1,0:T(8,128)(2,1)}, bf16[1024,1024]{1,0:T(8,128)(2,1)}) custom-call(bf16[1024,1024]{1,0:T(8,128)(2,1)} %convolution_convert_fusion.refs_0_, bf16[1024,1024]{1,0:T(8,128)(2,1)} %multiply_convert_fusion.refs_1_), custom_call_target="tpu_custom_call" | custom-call | tf_op jit(solution)/shard_map/pallas_call | solution.py:75
  77.4 25.3 %shard_map.96 = (bf16[1024,1024]{1,0:T(8,128)(2,1)}, bf16[768,4096]{1,0:T(8,128)(2,1)}) custom-call(bf16[1024,1024]{1,0:T(8,128)(2,1)} %get-tuple-element.6.xf_ref, bf16[1024,1024]{1,0:T(8,128)(2,1)} %get-tuple-element.7.dyf_ref, bf16[4096,768]{1,0:T(8,128)(2,1)} %bitcast.25, bf16[4096,768]{1,0:T(8,128)(2,1)} %bitcast.26, bf16[768,4096]{1,0:T(8,128)(2,1)} %bitcast.27), custom_call_target="tpu_custom_call" | custom-call | tf_op jit(solution)/shard_map/pallas_call | solution.py:195
  102.7 34.9 %shard_map.97 = bf16[1024,1024]{1,0:T(8,128)(2,1)} custom-call(bf16[1024,1024]{1,0:T(8,128)(2,1)} %get-tuple-element.8.refs_0_), custom_call_target="tpu_custom_call" | custom-call | tf_op jit(solution)/shard_map/pallas_call | solution.py:75
  137.7 2.3 %convolution_convert_fusion.1 = bf16[128,1024]{1,0:T(8,128)(2,1)S(1)} fusion(bf16[1024,1024]{1,0:T(8,128)(2,1)} %shard_map.97, s32[1024]{0:T(1024)S(1)} %fusion.11), kind=kOutput, calls=%fused_computation.5 | convolution fusion | flops 268697600 | bytes 2363392 | tf_op jit(solution)/shard_map/dot_general | solution.py:273
  139.9 0.9 convert_element_type.26
  (16 shorter events, 0.2 us)
Async XLA Ops:
  0.6 0.9 copy-start
  1.5 2.9 %copy-start.3 = (s32[32,8]{0,1:T(8,128)S(1)}, s32[32,8]{0,1:T(8,128)}, u32[]{:S(2)}) copy-start(s32[32,8]{0,1:T(8,128)} %param.12) | copy-start | bytes 3076
  4.0 5.3 %copy-start.1 = (bf16[32,4096]{1,0:T(8,128)(2,1)S(1)}, bf16[32,4096]{1,0:T(8,128)(2,1)}, u32[]{:S(2)}) copy-start(bf16[32,4096]{1,0:T(8,128)(2,1)} %param.8) | copy-start | bytes 786436
  4.0 5.5 %copy-start.2 = (bf16[32,4096]{1,0:T(8,128)(2,1)S(1)}, bf16[32,4096]{1,0:T(8,128)(2,1)}, u32[]{:S(2)}) copy-start(bf16[32,4096]{1,0:T(8,128)(2,1)} %param.9) | copy-start | bytes 786436

commit v12 on v11

--- a/solution.py
+++ b/solution.py
@@ -228,7 +228,10 @@
     tok_dev, top_count = expert_local.shape
     width = tokens.shape[1]
     capacity = tok_dev * top_count // experts
-    node_pick = jnp.take_along_axis(node_lists, expert_local // per_node, axis=1)
+    group_pos = expert_local // per_node
+    node_pick = jnp.zeros_like(expert_local)
+    for k in range(node_lists.shape[1]):
+        node_pick = node_pick + jnp.where(group_pos == k, node_lists[:, k:k + 1], 0)
     expert_ids = (node_pick * per_node + expert_local % per_node).reshape(-1)
     onehot = (expert_ids[:, None] == jnp.arange(experts, dtype=jnp.int32)[None, :]).astype(
         jnp.int32
@@ -241,11 +244,11 @@
     w_up_e = up_weight[0]
     w_down_e = down_weight[0]
     gate_flat = gate_fixed.reshape(-1)
-    table = jnp.full((experts * capacity,), -1, jnp.int32)
-    table = table.at[position].set(jnp.arange(tok_dev * top_count, dtype=jnp.int32), mode="drop")
-    valid = table >= 0
-    safe = jnp.maximum(table, 0)
-    rows = safe // top_count
+    fills = position[:, None] == jnp.arange(experts * capacity, dtype=jnp.int32)[None, :]
+    valid = jnp.any(fills, axis=0)
+    assign_ids = jnp.arange(tok_dev * top_count, dtype=jnp.int32)[:, None]
+    rows = jnp.sum(jnp.where(fills, assign_ids // top_count, 0), axis=0)
+    gate_slot = jnp.sum(jnp.where(fills, gate_flat[:, None], 0), axis=0)
     tile_rows = 8
     blocks = tile_rows // capacity
     piece = width // blocks
@@ -261,7 +264,7 @@
     tok_pieces = tokens.reshape(tok_dev * blocks, piece)
     og_pieces = out_grad.reshape(tok_dev * blocks, piece)
     send_x = jnp.dot(select, tok_pieces, preferred_element_type=jnp.float32).astype(jnp.bfloat16)
-    gate_val = jnp.where(valid, gate_flat[safe].astype(jnp.float32) * (1.0 / 65536.0), 0.0)
+    gate_val = jnp.where(valid, gate_slot.astype(jnp.float32) * (1.0 / 65536.0), 0.0)
     gate_rows = jnp.repeat(gate_val, blocks)
     og_sel = jnp.dot(select, og_pieces, preferred_element_type=jnp.float32)
     send_dy = (gate_rows[:, None] * og_sel).astype(jnp.bfloat16)

time: 141 us -> 138 us (0.979)
  local copies, waits for them, and re-layouts: 9.13 us -> 4.88 us
    gather x4 -> x0, local copies, waits for them, and re-layouts: 4.53 us -> none  [the longest x3 2.58 us: body(): jnp.take_along_axis(node_lists, expert_local // per_node, axis=1)]
where the time goes in v12:
time: 138 us; the launch traced here: 137 us
  Pallas kernels  124 us (90%)
  matrix products  6.43 us (5%)
  local copies, waits for them, and re-layouts  4.88 us (4%)
  other arithmetic  1.47 us (1%)
    pallas_call x2, Pallas kernels, exchange(): pl.pallas_call(functools.partial(_exchange_kernel, n_local), out_shape=[j...  98.5 us
    pallas_call x1, Pallas kernels, expert_math(): pl.pallas_call(_expert_kernel, out_shape=[jax.ShapeDtypeStruct(x_flat.sha...  25.3 us

profile of v12, /device:TPU:1, one launch (start us, length us, event | category | flops | bytes accessed | tf_op | source)
XLA Modules:
  0.0 137.3 jit_solution(16460976404836334623)
XLA Ops:
  0.6 0.0 copy-start
  0.6 0.8 slice_bitcast_fusion.4
  1.5 0.7 fusion.8
  2.2 0.1 copy.15
  2.3 0.1 eq.75
  2.3 0.1 eq.79
  2.4 0.8 copy.19
  3.2 0.1 broadcast_in_dim.101
  3.3 0.1 copy.17
  3.4 0.2 fusion.4
  3.7 0.2 fusion.5
  3.9 0.2 select_reduce_fusion
  4.1 0.1 fusion.3
  4.2 0.1 broadcast_in_dim.96
  4.3 0.1 reshape.107
  4.5 0.1 broadcast_in_dim.99
  4.6 0.1 mul.51
  4.7 0.1 broadcast_in_dim.104
  4.8 0.1 mul.55
  4.9 1.1 reshape.108
  6.1 0.0 copy-done
  6.1 0.2 reshape.109
  6.2 2.1 %multiply_convert_fusion.refs_1_ = bf16[1024,1024]{1,0:T(8,128)(2,1)} fusion(bf16[128,1024]{1,0:T(8,128)(2,1)S(1)} %reshape.109, f32[1024]{0:T(1024)S(1)} %mul.55, s32[1024]{0:T(1024)S(1)} %fusion.10), kind=kOutput, calls=%fused_computation | convolution fusion | flops 270663680 | bytes 2367488 | tf_op jit(solution)/shard_map/dot_general | solution.py:269
  8.3 2.1 %convolution_convert_fusion.refs_0_ = bf16[1024,1024]{1,0:T(8,128)(2,1)} fusion(bf16[128,1024]{1,0:T(8,128)(2,1)S(1)} %reshape.108, s32[1024]{0:T(1024)S(1)} %fusion.10), kind=kOutput, calls=%fused_computation.1 | convolution fusion | flops 269615104 | bytes 2363392 | tf_op jit(solution)/shard_map/dot_general | solution.py:266
  10.4 63.6 %shard_map.95 = (bf16[1024,1024]{1,0:T(8,128)(2,1)}, bf16[1024,1024]{1,0:T(8,128)(2,1)}) custom-call(bf16[1024,1024]{1,0:T(8,128)(2,1)} %convolution_convert_fusion.refs_0_, bf16[1024,1024]{1,0:T(8,128)(2,1)} %multiply_convert_fusion.refs_1_), custom_call_target="tpu_custom_call" | custom-call | tf_op jit(solution)/shard_map/pallas_call | solution.py:75
  74.0 25.3 %shard_map.96 = (bf16[1024,1024]{1,0:T(8,128)(2,1)}, bf16[768,4096]{1,0:T(8,128)(2,1)}) custom-call(bf16[1024,1024]{1,0:T(8,128)(2,1)} %get-tuple-element.6.xf_ref, bf16[1024,1024]{1,0:T(8,128)(2,1)} %get-tuple-element.7.dyf_ref, bf16[4096,768]{1,0:T(8,128)(2,1)} %bitcast.26, bf16[4096,768]{1,0:T(8,128)(2,1)} %bitcast.27, bf16[768,4096]{1,0:T(8,128)(2,1)} %bitcast.28), custom_call_target="tpu_custom_call" | custom-call | tf_op jit(solution)/shard_map/pallas_call | solution.py:195
  99.3 34.9 %shard_map.97 = bf16[1024,1024]{1,0:T(8,128)(2,1)} custom-call(bf16[1024,1024]{1,0:T(8,128)(2,1)} %get-tuple-element.8.refs_0_), custom_call_target="tpu_custom_call" | custom-call | tf_op jit(solution)/shard_map/pallas_call | solution.py:75
  134.2 2.3 %convolution_convert_fusion.1 = bf16[128,1024]{1,0:T(8,128)(2,1)S(1)} fusion(bf16[1024,1024]{1,0:T(8,128)(2,1)} %shard_map.97, s32[1024]{0:T(1024)S(1)} %fusion.10), kind=kOutput, calls=%fused_computation.2 | convolution fusion | flops 268697600 | bytes 2363392 | tf_op jit(solution)/shard_map/dot_general | solution.py:276
  136.5 0.9 convert_element_type.26
  (10 shorter events, 0.1 us)
Async XLA Ops:
  0.6 5.4 %copy-start = (bf16[32,4096]{1,0:T(8,128)(2,1)S(1)}, bf16[32,4096]{1,0:T(8,128)(2,1)}, u32[]{:S(2)}) copy-start(bf16[32,4096]{1,0:T(8,128)(2,1)} %param.9) | copy-start | bytes 786436

commit v13 on v12

--- a/solution.py
+++ b/solution.py
@@ -100,7 +100,7 @@
             for cb in range(wide.shape[0]):
                 col = j * piece + cb * lane
                 dst[:, col:col + lane] = wide[cb, pl.ds(j, n_rows, stride=blocks), :].astype(dst.dtype)
-    step = 512
+    step = 1024
     n_steps = k_total // step
     nt = (((1,), (1,)), ((), ()))
     sources = ((wg_hbm, wg), (wu_hbm, wu))
@@ -207,11 +207,11 @@
             pltpu.VMEM((n_rows, hid), jnp.float32),
             pltpu.VMEM((n_rows, hid), jnp.float32),
             pltpu.VMEM((n_rows, hid), jnp.float32),
-            pltpu.VMEM((2, hid, 512), jnp.bfloat16),
+            pltpu.VMEM((2, hid, 1024), jnp.bfloat16),
             pltpu.VMEM((n_rows, width), jnp.bfloat16),
             pltpu.VMEM((n_rows, width), jnp.bfloat16),
             pltpu.VMEM((x_flat.shape[1] // 128, x_flat.shape[0], 128), jnp.float32),
-            pltpu.SemaphoreType.DMA((3, width // 512)),
+            pltpu.SemaphoreType.DMA((3, width // 1024)),
             pltpu.SemaphoreType.DMA((2,)),
         ],
         compiler_params=pltpu.CompilerParams(vmem_limit_bytes=62 * 1024 * 1024),

time: 138 us -> 135 us (0.978)
  Pallas kernels: 124 us -> 121 us
    pallas_call x1, Pallas kernels: 25.3 us -> 22.8 us  [expert_math(): pl.pallas_call(_expert_kernel, out_shape=[jax.ShapeDtypeStruct(x_flat.sha...]
where the time goes in v13:
time: 135 us
  Pallas kernels  121 us (90%)
  matrix products  6.43 us (5%)
  local copies, waits for them, and re-layouts  4.88 us (4%)
  other arithmetic  1.47 us (1%)
    pallas_call x2, Pallas kernels, exchange(): pl.pallas_call(functools.partial(_exchange_kernel, n_local), out_shape=[j...  98.5 us
    pallas_call x1, Pallas kernels, expert_math(): pl.pallas_call(_expert_kernel, out_shape=[jax.ShapeDtypeStruct(x_flat.sha...  22.8 us

profile of v13, /device:TPU:1, one launch (start us, length us, event | category | flops | bytes accessed | tf_op | source)
XLA Modules:
  0.0 134.9 jit_solution(5522808653786252017)
XLA Ops:
  0.6 0.0 copy-start
  0.6 0.8 slice_bitcast_fusion.4
  1.5 0.7 fusion.8
  2.2 0.1 copy.15
  2.3 0.1 eq.75
  2.3 0.1 eq.79
  2.4 0.8 copy.19
  3.2 0.1 broadcast_in_dim.101
  3.3 0.1 copy.17
  3.4 0.2 fusion.4
  3.7 0.2 fusion.5
  3.9 0.2 select_reduce_fusion
  4.1 0.1 fusion.3
  4.2 0.1 broadcast_in_dim.96
  4.3 0.1 reshape.107
  4.5 0.1 broadcast_in_dim.99
  4.6 0.1 mul.51
  4.7 0.1 broadcast_in_dim.104
  4.8 0.1 mul.55
  4.9 1.1 reshape.108
  6.1 0.0 copy-done
  6.1 0.2 reshape.109
  6.2 2.1 %multiply_convert_fusion.refs_1_ = bf16[1024,1024]{1,0:T(8,128)(2,1)} fusion(bf16[128,1024]{1,0:T(8,128)(2,1)S(1)} %reshape.109, f32[1024]{0:T(1024)S(1)} %mul.55, s32[1024]{0:T(1024)S(1)} %fusion.10), kind=kOutput, calls=%fused_computation | convolution fusion | flops 270663680 | bytes 2367488 | tf_op jit(solution)/shard_map/dot_general | solution.py:269
  8.3 2.1 %convolution_convert_fusion.refs_0_ = bf16[1024,1024]{1,0:T(8,128)(2,1)} fusion(bf16[128,1024]{1,0:T(8,128)(2,1)S(1)} %reshape.108, s32[1024]{0:T(1024)S(1)} %fusion.10), kind=kOutput, calls=%fused_computation.1 | convolution fusion | flops 269615104 | bytes 2363392 | tf_op jit(solution)/shard_map/dot_general | solution.py:266
  10.4 63.6 %shard_map.95 = (bf16[1024,1024]{1,0:T(8,128)(2,1)}, bf16[1024,1024]{1,0:T(8,128)(2,1)}) custom-call(bf16[1024,1024]{1,0:T(8,128)(2,1)} %convolution_convert_fusion.refs_0_, bf16[1024,1024]{1,0:T(8,128)(2,1)} %multiply_convert_fusion.refs_1_), custom_call_target="tpu_custom_call" | custom-call | tf_op jit(solution)/shard_map/pallas_call | solution.py:75
  74.0 22.8 %shard_map.96 = (bf16[1024,1024]{1,0:T(8,128)(2,1)}, bf16[768,4096]{1,0:T(8,128)(2,1)}) custom-call(bf16[1024,1024]{1,0:T(8,128)(2,1)} %get-tuple-element.6.xf_ref, bf16[1024,1024]{1,0:T(8,128)(2,1)} %get-tuple-element.7.dyf_ref, bf16[4096,768]{1,0:T(8,128)(2,1)} %bitcast.26, bf16[4096,768]{1,0:T(8,128)(2,1)} %bitcast.27, bf16[768,4096]{1,0:T(8,128)(2,1)} %bitcast.28), custom_call_target="tpu_custom_call" | custom-call | tf_op jit(solution)/shard_map/pallas_call | solution.py:195
  96.8 35.0 %shard_map.97 = bf16[1024,1024]{1,0:T(8,128)(2,1)} custom-call(bf16[1024,1024]{1,0:T(8,128)(2,1)} %get-tuple-element.8.refs_0_), custom_call_target="tpu_custom_call" | custom-call | tf_op jit(solution)/shard_map/pallas_call | solution.py:75
  131.8 2.3 %convolution_convert_fusion.1 = bf16[128,1024]{1,0:T(8,128)(2,1)S(1)} fusion(bf16[1024,1024]{1,0:T(8,128)(2,1)} %shard_map.97, s32[1024]{0:T(1024)S(1)} %fusion.10), kind=kOutput, calls=%fused_computation.2 | convolution fusion | flops 268697600 | bytes 2363392 | tf_op jit(solution)/shard_map/dot_general | solution.py:276
  134.1 0.9 convert_element_type.26
  (10 shorter events, 0.1 us)
Async XLA Ops:
  0.6 5.4 %copy-start = (bf16[32,4096]{1,0:T(8,128)(2,1)S(1)}, bf16[32,4096]{1,0:T(8,128)(2,1)}, u32[]{:S(2)}) copy-start(bf16[32,4096]{1,0:T(8,128)(2,1)} %param.9) | copy-start | bytes 786436

commit v14 on v13

--- a/solution.py
+++ b/solution.py
@@ -100,7 +100,7 @@
             for cb in range(wide.shape[0]):
                 col = j * piece + cb * lane
                 dst[:, col:col + lane] = wide[cb, pl.ds(j, n_rows, stride=blocks), :].astype(dst.dtype)
-    step = 1024
+    step = 2048
     n_steps = k_total // step
     nt = (((1,), (1,)), ((), ()))
     sources = ((wg_hbm, wg), (wu_hbm, wu))
@@ -166,9 +166,9 @@
             lax.dot_general(gate_grad, wg[cc:cc + step, :], nt, preferred_element_type=jnp.float32)
             + lax.dot_general(up_grad, wu[cc:cc + step, :], nt, preferred_element_type=jnp.float32)
         ).astype(jnp.bfloat16)
-        j, h = divmod(cc, piece)
         for q in range(step // lane):
-            wide[h // lane + q, pl.ds(j, n_rows, stride=blocks), :] = (
+            j, h = divmod(cc + q * lane, piece)
+            wide[h // lane, pl.ds(j, n_rows, stride=blocks), :] = (
                 rg[:, q * lane:(q + 1) * lane].astype(jnp.float32)
             )
         slot = c % 2
@@ -207,11 +207,11 @@
             pltpu.VMEM((n_rows, hid), jnp.float32),
             pltpu.VMEM((n_rows, hid), jnp.float32),
             pltpu.VMEM((n_rows, hid), jnp.float32),
-            pltpu.VMEM((2, hid, 1024), jnp.bfloat16),
+            pltpu.VMEM((2, hid, 2048), jnp.bfloat16),
             pltpu.VMEM((n_rows, width), jnp.bfloat16),
             pltpu.VMEM((n_rows, width), jnp.bfloat16),
             pltpu.VMEM((x_flat.shape[1] // 128, x_flat.shape[0], 128), jnp.float32),
-            pltpu.SemaphoreType.DMA((3, width // 1024)),
+            pltpu.SemaphoreType.DMA((3, width // 2048)),
             pltpu.SemaphoreType.DMA((2,)),
         ],
         compiler_params=pltpu.CompilerParams(vmem_limit_bytes=62 * 1024 * 1024),

time: 135 us -> 134 us (level)
  no operation moved by 1% of the time
where the time goes in v14:
time: 134 us
  Pallas kernels  121 us (90%)
  matrix products  6.43 us (5%)
  local copies, waits for them, and re-layouts  4.88 us (4%)
  other arithmetic  1.47 us (1%)
    pallas_call x2, Pallas kernels, exchange(): pl.pallas_call(functools.partial(_exchange_kernel, n_local), out_shape=[j...  98.5 us
    pallas_call x1, Pallas kernels, expert_math(): pl.pallas_call(_expert_kernel, out_shape=[jax.ShapeDtypeStruct(x_flat.sha...  22.1 us

profile of v14, /device:TPU:1, one launch (start us, length us, event | category | flops | bytes accessed | tf_op | source)
XLA Modules:
  0.0 134.2 jit_solution(16393480350014912333)
XLA Ops:
  0.6 0.0 copy-start
  0.6 0.8 slice_bitcast_fusion.4
  1.5 0.7 fusion.8
  2.2 0.1 copy.15
  2.3 0.1 eq.75
  2.3 0.1 eq.79
  2.4 0.8 copy.19
  3.2 0.1 broadcast_in_dim.101
  3.3 0.1 copy.17
  3.4 0.2 fusion.4
  3.7 0.2 fusion.5
  3.9 0.2 select_reduce_fusion
  4.1 0.1 fusion.3
  4.2 0.1 broadcast_in_dim.96
  4.3 0.1 reshape.107
  4.5 0.1 broadcast_in_dim.99
  4.6 0.1 mul.51
  4.7 0.1 broadcast_in_dim.104
  4.8 0.1 mul.55
  4.9 1.1 reshape.108
  6.1 0.0 copy-done
  6.1 0.2 reshape.109
  6.2 2.1 %multiply_convert_fusion.refs_1_ = bf16[1024,1024]{1,0:T(8,128)(2,1)} fusion(bf16[128,1024]{1,0:T(8,128)(2,1)S(1)} %reshape.109, f32[1024]{0:T(1024)S(1)} %mul.55, s32[1024]{0:T(1024)S(1)} %fusion.10), kind=kOutput, calls=%fused_computation | convolution fusion | flops 270663680 | bytes 2367488 | tf_op jit(solution)/shard_map/dot_general | solution.py:269
  8.3 2.1 %convolution_convert_fusion.refs_0_ = bf16[1024,1024]{1,0:T(8,128)(2,1)} fusion(bf16[128,1024]{1,0:T(8,128)(2,1)S(1)} %reshape.108, s32[1024]{0:T(1024)S(1)} %fusion.10), kind=kOutput, calls=%fused_computation.1 | convolution fusion | flops 269615104 | bytes 2363392 | tf_op jit(solution)/shard_map/dot_general | solution.py:266
  10.4 63.6 %shard_map.95 = (bf16[1024,1024]{1,0:T(8,128)(2,1)}, bf16[1024,1024]{1,0:T(8,128)(2,1)}) custom-call(bf16[1024,1024]{1,0:T(8,128)(2,1)} %convolution_convert_fusion.refs_0_, bf16[1024,1024]{1,0:T(8,128)(2,1)} %multiply_convert_fusion.refs_1_), custom_call_target="tpu_custom_call" | custom-call | tf_op jit(solution)/shard_map/pallas_call | solution.py:75
  74.0 22.1 %shard_map.96 = (bf16[1024,1024]{1,0:T(8,128)(2,1)}, bf16[768,4096]{1,0:T(8,128)(2,1)}) custom-call(bf16[1024,1024]{1,0:T(8,128)(2,1)} %get-tuple-element.6.xf_ref, bf16[1024,1024]{1,0:T(8,128)(2,1)} %get-tuple-element.7.dyf_ref, bf16[4096,768]{1,0:T(8,128)(2,1)} %bitcast.26, bf16[4096,768]{1,0:T(8,128)(2,1)} %bitcast.27, bf16[768,4096]{1,0:T(8,128)(2,1)} %bitcast.28), custom_call_target="tpu_custom_call" | custom-call | tf_op jit(solution)/shard_map/pallas_call | solution.py:195
  96.1 35.0 %shard_map.97 = bf16[1024,1024]{1,0:T(8,128)(2,1)} custom-call(bf16[1024,1024]{1,0:T(8,128)(2,1)} %get-tuple-element.8.refs_0_), custom_call_target="tpu_custom_call" | custom-call | tf_op jit(solution)/shard_map/pallas_call | solution.py:75
  131.1 2.3 %convolution_convert_fusion.1 = bf16[128,1024]{1,0:T(8,128)(2,1)S(1)} fusion(bf16[1024,1024]{1,0:T(8,128)(2,1)} %shard_map.97, s32[1024]{0:T(1024)S(1)} %fusion.10), kind=kOutput, calls=%fused_computation.2 | convolution fusion | flops 268697600 | bytes 2363392 | tf_op jit(solution)/shard_map/dot_general | solution.py:276
  133.3 0.9 convert_element_type.26
  (10 shorter events, 0.1 us)
Async XLA Ops:
  0.6 5.4 %copy-start = (bf16[32,4096]{1,0:T(8,128)(2,1)S(1)}, bf16[32,4096]{1,0:T(8,128)(2,1)}, u32[]{:S(2)}) copy-start(bf16[32,4096]{1,0:T(8,128)(2,1)} %param.9) | copy-start | bytes 786436

commit v15 on v14

--- a/solution.py
+++ b/solution.py
@@ -263,11 +263,13 @@
     ).astype(jnp.bfloat16)
     tok_pieces = tokens.reshape(tok_dev * blocks, piece)
     og_pieces = out_grad.reshape(tok_dev * blocks, piece)
-    send_x = jnp.dot(select, tok_pieces, preferred_element_type=jnp.float32).astype(jnp.bfloat16)
     gate_val = jnp.where(valid, gate_slot.astype(jnp.float32) * (1.0 / 65536.0), 0.0)
     gate_rows = jnp.repeat(gate_val, blocks)
-    og_sel = jnp.dot(select, og_pieces, preferred_element_type=jnp.float32)
-    send_dy = (gate_rows[:, None] * og_sel).astype(jnp.bfloat16)
+    both = jnp.dot(
+        select, jnp.concatenate([tok_pieces, og_pieces], axis=1), preferred_element_type=jnp.float32
+    )
+    send_x = both[:, :piece].astype(jnp.bfloat16)
+    send_dy = (gate_rows[:, None] * both[:, piece:]).astype(jnp.bfloat16)
     x_flat, dy_flat = exchange(send_x, send_dy)
     down_local, row_flat = expert_math(
         x_flat, dy_flat, w_gate_e, w_up_e, w_down_e, experts * capacity, width

time: 134 us -> 136 us (1.015)
  matrix products: 6.43 us -> 3.55 us
  local copies, waits for them, and re-layouts: 4.88 us -> 7.48 us
  other arithmetic: 1.47 us -> 3.09 us
    dot_general x2 -> x1, matrix products: 4.16 us -> 1.29 us  [body(): jnp.dot(select, jnp.concatenate([tok_pieces, og_pieces], axis=1), preferr...]
    slice x0 -> x1, local copies, waits for them, and re-layouts: none -> 1.65 us  [body(): send_x = both[:, :piece].astype(jnp.bfloat16)]
    convert_element_type x0 -> x1, other arithmetic: none -> 1.62 us  [body(): send_dy = (gate_rows[:, None] * both[:, piece:]).astype(jnp.bfloat16)]
where the time goes in v15:
time: 136 us
  Pallas kernels  121 us (89%)
  local copies, waits for them, and re-layouts  7.48 us (6%)
  matrix products  3.55 us (3%)
  other arithmetic  3.09 us (2%)
    pallas_call x2, Pallas kernels, exchange(): pl.pallas_call(functools.partial(_exchange_kernel, n_local), out_shape=[j...  98.5 us
    pallas_call x1, Pallas kernels, expert_math(): pl.pallas_call(_expert_kernel, out_shape=[jax.ShapeDtypeStruct(x_flat.sha...  22.1 us

profile of v15, /device:TPU:1, one launch (start us, length us, event | category | flops | bytes accessed | tf_op | source)
XLA Modules:
  0.0 135.5 jit_solution(2579628835426377396)
XLA Ops:
  0.6 0.8 slice_bitcast_fusion.4
  1.5 0.7 fusion.12
  2.2 0.1 copy.15
  2.2 0.1 eq.75
  2.3 0.1 eq.79
  2.4 0.8 copy.19
  3.2 0.1 broadcast_in_dim.101
  3.3 0.1 copy.17
  3.4 0.2 fusion.8
  3.7 0.2 fusion.9
  3.9 0.2 select_reduce_fusion
  4.1 0.1 fusion.7
  4.2 0.1 broadcast_in_dim.96
  4.3 0.1 reshape.107
  4.5 0.1 broadcast_in_dim.99
  4.6 0.1 mul.51
  4.7 0.1 broadcast_in_dim.104
  4.8 0.1 mul.55
  4.9 1.1 reshape.108
  6.0 1.1 reshape.109
  7.2 1.3 fusion.1
  8.5 1.6 %fusion.refs_1_ = bf16[1024,1024]{1,0:T(8,128)(2,1)} fusion(f32[1024,2048]{1,0:T(8,128)S(1)} %fusion.1, f32[1024]{0:T(1024)S(1)} %mul.55), kind=kLoop, calls=%fused_computation.1 | loop fusion | flops 2097152 | bytes 6295552 | tf_op jit(solution)/shard_map/convert_element_type | solution.py:272
  10.1 1.6 %slice.45.refs_0_ = bf16[1024,1024]{1,0:T(8,128)(2,1)} slice(f32[1024,2048]{1,0:T(8,128)S(1)} %fusion.1), slice={[0:1024], [0:1024]} | slice | bytes 4194304 | tf_op jit(solution)/shard_map/slice | solution.py:271
  11.7 63.6 %shard_map.95 = (bf16[1024,1024]{1,0:T(8,128)(2,1)}, bf16[1024,1024]{1,0:T(8,128)(2,1)}) custom-call(bf16[1024,1024]{1,0:T(8,128)(2,1)} %slice.45.refs_0_, bf16[1024,1024]{1,0:T(8,128)(2,1)} %fusion.refs_1_), custom_call_target="tpu_custom_call" | custom-call | tf_op jit(solution)/shard_map/pallas_call | solution.py:75
  75.3 22.1 %shard_map.96 = (bf16[1024,1024]{1,0:T(8,128)(2,1)}, bf16[768,4096]{1,0:T(8,128)(2,1)}) custom-call(bf16[1024,1024]{1,0:T(8,128)(2,1)} %get-tuple-element.6.xf_ref, bf16[1024,1024]{1,0:T(8,128)(2,1)} %get-tuple-element.7.dyf_ref, bf16[4096,768]{1,0:T(8,128)(2,1)} %bitcast.24, bf16[4096,768]{1,0:T(8,128)(2,1)} %bitcast.25, bf16[768,4096]{1,0:T(8,128)(2,1)} %bitcast.26), custom_call_target="tpu_custom_call" | custom-call | tf_op jit(solution)/shard_map/pallas_call | solution.py:195
  97.4 34.9 %shard_map.97 = bf16[1024,1024]{1,0:T(8,128)(2,1)} custom-call(bf16[1024,1024]{1,0:T(8,128)(2,1)} %get-tuple-element.8.refs_0_), custom_call_target="tpu_custom_call" | custom-call | tf_op jit(solution)/shard_map/pallas_call | solution.py:75
  132.4 2.3 %convolution_convert_fusion = bf16[128,1024]{1,0:T(8,128)(2,1)S(1)} fusion(bf16[1024,1024]{1,0:T(8,128)(2,1)} %shard_map.97, s32[1024]{0:T(1024)S(1)} %fusion.14), kind=kOutput, calls=%fused_computation.3 | convolution fusion | flops 268697600 | bytes 2363392 | tf_op jit(solution)/shard_map/dot_general | solution.py:278
  134.6 0.9 convert_element_type.23
  (10 shorter events, 0.1 us)

commit v16 on v14

--- a/solution.py
+++ b/solution.py
@@ -100,7 +100,7 @@
             for cb in range(wide.shape[0]):
                 col = j * piece + cb * lane
                 dst[:, col:col + lane] = wide[cb, pl.ds(j, n_rows, stride=blocks), :].astype(dst.dtype)
-    step = 2048
+    step = 4096
     n_steps = k_total // step
     nt = (((1,), (1,)), ((), ()))
     sources = ((wg_hbm, wg), (wu_hbm, wu))
@@ -182,7 +182,7 @@
         pltpu.make_async_copy(down_buf.at[slot], down_hbm.at[:, cc:cc + step], osem.at[slot]).start()
     for cb in range(wide.shape[0]):
         row_out[:, cb * lane:(cb + 1) * lane] = wide[cb].astype(row_out.dtype)
-    for c in (n_steps - 2, n_steps - 1):
+    for c in range(max(0, n_steps - 2), n_steps):
         pltpu.make_async_copy(
             down_buf.at[c % 2], down_hbm.at[:, c * step:(c + 1) * step], osem.at[c % 2]
         ).wait()
@@ -207,11 +207,11 @@
             pltpu.VMEM((n_rows, hid), jnp.float32),
             pltpu.VMEM((n_rows, hid), jnp.float32),
             pltpu.VMEM((n_rows, hid), jnp.float32),
-            pltpu.VMEM((2, hid, 2048), jnp.bfloat16),
+            pltpu.VMEM((2, hid, 4096), jnp.bfloat16),
             pltpu.VMEM((n_rows, width), jnp.bfloat16),
             pltpu.VMEM((n_rows, width), jnp.bfloat16),
             pltpu.VMEM((x_flat.shape[1] // 128, x_flat.shape[0], 128), jnp.float32),
-            pltpu.SemaphoreType.DMA((3, width // 2048)),
+            pltpu.SemaphoreType.DMA((3, width // 4096)),
             pltpu.SemaphoreType.DMA((2,)),
         ],
         compiler_params=pltpu.CompilerParams(vmem_limit_bytes=62 * 1024 * 1024),

time: 134 us -> 134 us (level)
  no operation moved by 1% of the time
where the time goes in v16:
time: 134 us
  Pallas kernels  121 us (90%)
  matrix products  6.42 us (5%)
  local copies, waits for them, and re-layouts  4.88 us (4%)
  other arithmetic  1.47 us (1%)
    pallas_call x2, Pallas kernels, exchange(): pl.pallas_call(functools.partial(_exchange_kernel, n_local), out_shape=[j...  98.5 us
    pallas_call x1, Pallas kernels, expert_math(): pl.pallas_call(_expert_kernel, out_shape=[jax.ShapeDtypeStruct(x_flat.sha...  22 us

profile of v16, /device:TPU:1, one launch (start us, length us, event | category | flops | bytes accessed | tf_op | source)
XLA Modules:
  0.0 134.1 jit_solution(13114361036281966373)
XLA Ops:
  0.6 0.0 copy-start
  0.6 0.8 slice_bitcast_fusion.4
  1.5 0.7 fusion.8
  2.2 0.1 copy.15
  2.3 0.1 eq.75
  2.3 0.1 eq.79
  2.4 0.8 copy.19
  3.2 0.1 broadcast_in_dim.101
  3.3 0.1 copy.17
  3.4 0.2 fusion.4
  3.7 0.2 fusion.5
  3.9 0.2 select_reduce_fusion
  4.1 0.1 fusion.3
  4.2 0.1 broadcast_in_dim.96
  4.3 0.1 reshape.107
  4.5 0.1 broadcast_in_dim.99
  4.6 0.1 mul.51
  4.7 0.1 broadcast_in_dim.104
  4.8 0.1 mul.55
  4.9 1.1 reshape.108
  6.1 0.0 copy-done
  6.1 0.2 reshape.109
  6.2 2.1 %multiply_convert_fusion.refs_1_ = bf16[1024,1024]{1,0:T(8,128)(2,1)} fusion(bf16[128,1024]{1,0:T(8,128)(2,1)S(1)} %reshape.109, f32[1024]{0:T(1024)S(1)} %mul.55, s32[1024]{0:T(1024)S(1)} %fusion.10), kind=kOutput, calls=%fused_computation | convolution fusion | flops 270663680 | bytes 2367488 | tf_op jit(solution)/shard_map/dot_general | solution.py:269
  8.3 2.1 %convolution_convert_fusion.refs_0_ = bf16[1024,1024]{1,0:T(8,128)(2,1)} fusion(bf16[128,1024]{1,0:T(8,128)(2,1)S(1)} %reshape.108, s32[1024]{0:T(1024)S(1)} %fusion.10), kind=kOutput, calls=%fused_computation.1 | convolution fusion | flops 269615104 | bytes 2363392 | tf_op jit(solution)/shard_map/dot_general | solution.py:266
  10.4 63.6 %shard_map.95 = (bf16[1024,1024]{1,0:T(8,128)(2,1)}, bf16[1024,1024]{1,0:T(8,128)(2,1)}) custom-call(bf16[1024,1024]{1,0:T(8,128)(2,1)} %convolution_convert_fusion.refs_0_, bf16[1024,1024]{1,0:T(8,128)(2,1)} %multiply_convert_fusion.refs_1_), custom_call_target="tpu_custom_call" | custom-call | tf_op jit(solution)/shard_map/pallas_call | solution.py:75
  74.0 22.0 %shard_map.96 = (bf16[1024,1024]{1,0:T(8,128)(2,1)}, bf16[768,4096]{1,0:T(8,128)(2,1)}) custom-call(bf16[1024,1024]{1,0:T(8,128)(2,1)} %get-tuple-element.6.xf_ref, bf16[1024,1024]{1,0:T(8,128)(2,1)} %get-tuple-element.7.dyf_ref, bf16[4096,768]{1,0:T(8,128)(2,1)} %bitcast.26, bf16[4096,768]{1,0:T(8,128)(2,1)} %bitcast.27, bf16[768,4096]{1,0:T(8,128)(2,1)} %bitcast.28), custom_call_target="tpu_custom_call" | custom-call | tf_op jit(solution)/shard_map/pallas_call | solution.py:195
  96.0 35.0 %shard_map.97 = bf16[1024,1024]{1,0:T(8,128)(2,1)} custom-call(bf16[1024,1024]{1,0:T(8,128)(2,1)} %get-tuple-element.8.refs_0_), custom_call_target="tpu_custom_call" | custom-call | tf_op jit(solution)/shard_map/pallas_call | solution.py:75
  131.0 2.3 %convolution_convert_fusion.1 = bf16[128,1024]{1,0:T(8,128)(2,1)S(1)} fusion(bf16[1024,1024]{1,0:T(8,128)(2,1)} %shard_map.97, s32[1024]{0:T(1024)S(1)} %fusion.10), kind=kOutput, calls=%fused_computation.2 | convolution fusion | flops 268697600 | bytes 2363392 | tf_op jit(solution)/shard_map/dot_general | solution.py:276
  133.3 0.9 convert_element_type.26
  (10 shorter events, 0.1 us)
Async XLA Ops:
  0.6 5.4 %copy-start = (bf16[32,4096]{1,0:T(8,128)(2,1)S(1)}, bf16[32,4096]{1,0:T(8,128)(2,1)}, u32[]{:S(2)}) copy-start(bf16[32,4096]{1,0:T(8,128)(2,1)} %param.9) | copy-start | bytes 786436

commit v17 on v14

--- a/solution.py
+++ b/solution.py
@@ -273,8 +273,14 @@
         x_flat, dy_flat, w_gate_e, w_up_e, w_down_e, experts * capacity, width
     )
     (returned,) = exchange(row_flat)
-    total = jnp.dot(select.T, returned, preferred_element_type=jnp.float32)
-    token_grad = total.reshape(tok_dev, width).astype(jnp.bfloat16)
+    gather_t = select.T
+    token_grad = jnp.concatenate(
+        [
+            jnp.dot(gather_t[j::blocks], returned, preferred_element_type=jnp.float32)
+            for j in range(blocks)
+        ],
+        axis=1,
+    ).astype(jnp.bfloat16)
     return (token_grad, down_local[None])
 
 

time: 134 us -> 136 us (1.015)
    dot_general x1 -> x4, matrix products: 2.26 us -> 3.51 us  [body(): jnp.dot(gather_t[j::blocks], returned, preferred_element_type=jnp.float32)]
where the time goes in v17:
time: 136 us
  Pallas kernels  121 us (89%)
  matrix products  7.67 us (6%)
  local copies, waits for them, and re-layouts  4.51 us (3%)
  other arithmetic  2.27 us (2%)
    pallas_call x2, Pallas kernels, exchange(): pl.pallas_call(functools.partial(_exchange_kernel, n_local), out_shape=[j...  98.5 us
    pallas_call x1, Pallas kernels, expert_math(): pl.pallas_call(_expert_kernel, out_shape=[jax.ShapeDtypeStruct(x_flat.sha...  22.1 us
    dot_general x4, matrix products, body(): jnp.dot(gather_t[j::blocks], returned, preferred_element_type=jnp.float32)  3.51 us

profile of v17, /device:TPU:1, one launch (start us, length us, event | category | flops | bytes accessed | tf_op | source)
XLA Modules:
  0.0 135.9 jit_solution(8600889940473996460)
XLA Ops:
  0.6 0.8 slice_bitcast_fusion.4
  1.5 0.7 fusion.7
  2.2 0.1 copy.15
  2.2 0.1 eq.86
  2.3 0.1 copy.17
  2.5 0.2 fusion.3
  2.7 0.0 copy-start.1
  2.8 0.1 eq.82
  2.9 0.2 fusion.4
  3.0 0.8 copy.19
  3.8 0.1 broadcast_in_dim.101
  3.9 0.2 select_reduce_fusion
  4.1 0.1 fusion.2
  4.2 0.1 broadcast_in_dim.104
  4.3 0.1 mul.55
  4.5 0.1 broadcast_in_dim.99
  4.6 0.1 mul.51
  4.7 0.1 broadcast_in_dim.96
  4.8 0.1 reshape.105
  4.9 1.1 reshape.107
  6.0 2.1 %multiply_convert_fusion.refs_1_ = bf16[1024,1024]{1,0:T(8,128)(2,1)} fusion(bf16[128,1024]{1,0:T(8,128)(2,1)S(1)} %reshape.107, f32[1024]{0:T(1024)S(1)} %mul.55, s32[1024]{0:T(1024)S(1)} %fusion.9), kind=kOutput, calls=%fused_computation | convolution fusion | flops 270663680 | bytes 2367488 | tf_op jit(solution)/shard_map/dot_general | solution.py:269
  8.1 0.0 copy-done.1
  8.1 0.2 reshape.106
  8.3 2.1 %convolution_convert_fusion.refs_0_ = bf16[1024,1024]{1,0:T(8,128)(2,1)} fusion(bf16[128,1024]{1,0:T(8,128)(2,1)S(1)} %reshape.106, s32[1024]{0:T(1024)S(1)} %fusion.9), kind=kOutput, calls=%fused_computation.1 | convolution fusion | flops 269615104 | bytes 2363392 | tf_op jit(solution)/shard_map/dot_general | solution.py:266
  10.4 63.6 %shard_map.95 = (bf16[1024,1024]{1,0:T(8,128)(2,1)}, bf16[1024,1024]{1,0:T(8,128)(2,1)}) custom-call(bf16[1024,1024]{1,0:T(8,128)(2,1)} %convolution_convert_fusion.refs_0_, bf16[1024,1024]{1,0:T(8,128)(2,1)} %multiply_convert_fusion.refs_1_), custom_call_target="tpu_custom_call" | custom-call | tf_op jit(solution)/shard_map/pallas_call | solution.py:75
  74.0 22.1 %shard_map.96 = (bf16[1024,1024]{1,0:T(8,128)(2,1)}, bf16[768,4096]{1,0:T(8,128)(2,1)}) custom-call(bf16[1024,1024]{1,0:T(8,128)(2,1)} %get-tuple-element.6.xf_ref, bf16[1024,1024]{1,0:T(8,128)(2,1)} %get-tuple-element.7.dyf_ref, bf16[4096,768]{1,0:T(8,128)(2,1)} %bitcast.33, bf16[4096,768]{1,0:T(8,128)(2,1)} %bitcast.34, bf16[768,4096]{1,0:T(8,128)(2,1)} %bitcast.35), custom_call_target="tpu_custom_call" | custom-call | tf_op jit(solution)/shard_map/pallas_call | solution.py:195
  96.1 35.0 %shard_map.97 = bf16[1024,1024]{1,0:T(8,128)(2,1)} custom-call(bf16[1024,1024]{1,0:T(8,128)(2,1)} %get-tuple-element.8.refs_0_), custom_call_target="tpu_custom_call" | custom-call | tf_op jit(solution)/shard_map/pallas_call | solution.py:75
  131.0 0.0 copy-start
  131.0 0.1 iota_compare_fusion.3
  131.1 0.1 slice.36
  131.3 2.2 %convolution_convert_fusion.4 = bf16[32,1024]{1,0:T(8,128)(2,1)S(1)} fusion(pred[32,1024]{1,0:T(8,128)(4,1)S(1)} %slice.36, bf16[1024,1024]{1,0:T(8,128)(2,1)} %shard_map.97), kind=kOutput, calls=%fused_computation.5 | convolution fusion | flops 67141632 | bytes 2195456 | tf_op jit(solution)/shard_map/dot_general | solution.py:279
  133.4 0.1 slice.37
  133.5 0.0 copy-done
  133.5 0.5 convolution_convert_fusion.3
  134.0 0.1 slice.38
  134.1 0.5 convolution_convert_fusion.2
  134.6 0.1 slice.39
  134.7 0.5 convolution_convert_fusion.1
  135.2 0.7 pad_maximum_fusion
  (10 shorter events, 0.1 us)
Async XLA Ops:
  2.7 5.4 %copy-start.1 = (bf16[32,4096]{1,0:T(8,128)(2,1)S(1)}, bf16[32,4096]{1,0:T(8,128)(2,1)}, u32[]{:S(2)}) copy-start(bf16[32,4096]{1,0:T(8,128)(2,1)} %param.8) | copy-start | bytes 786436
  131.0 2.5 %copy-start = (bf16[1024,1024]{1,0:T(8,128)(2,1)S(1)}, bf16[1024,1024]{1,0:T(8,128)(2,1)}, u32[]{:S(2)}) copy-start(bf16[1024,1024]{1,0:T(8,128)(2,1)} %shard_map.97) | copy-start | bytes 6291460
